TPU v7x, 32 devices: a whole 2x2x4 slice. The times are simulated.
32 devices in a mesh: dp: 2 (over x), tok: 4 (over z), mp: 4 (over y, core).
Axes of the slice: x: 2, y: 2, z: 4, core: 2. Of those that a mesh axis runs over, the one named last changes fastest.
Arguments:
- tokens: bfloat16 [16384, 1024], P(('dp', 'tok'), 'mp'), may hold values from -6 to 6
- in_weight: bfloat16 [1024, 3, 1024], P(('dp', 'tok'), None, 'mp'), may hold values from -0.1875 to 0.1875
- conv_kernel: bfloat16 [3, 1024], P(None, 'mp'), may hold values from -2.5 to 2.5
- out_weight: bfloat16 [1024, 1024], P('mp', ('dp', 'tok')), may hold values from -0.1875 to 0.1875
- gate_weight: bfloat16 [1024, 4608], P(('dp', 'tok'), 'mp'), may hold values from -0.1875 to 0.1875
- up_weight: bfloat16 [1024, 4608], P(('dp', 'tok'), 'mp'), may hold values from -0.1875 to 0.1875
- down_weight: bfloat16 [4608, 1024], P('mp', ('dp', 'tok')), may hold values from -0.09375 to 0.09375
- mixer_norm_gain: float32 [1024], replicated, may hold values from 0.5 to 1.5
- gain_ffn: float32 [1024], replicated, may hold values from 0.5 to 1.5
- cotangent: bfloat16 [16384, 1024], P(('dp', 'tok'), 'mp'), may hold values from -6 to 6
Outputs:
- mixed: bfloat16 [16384, 1024], P(('dp', 'tok'), 'mp')
- input_token_gradient: float32 [16384, 1024], P(('dp', 'tok'), 'mp')
- grad_in_weight: float32 [1024, 3, 1024], P(('dp', 'tok'), None, 'mp')
- grad_conv_kernel: float32 [3, 1024], P(None, 'mp')
- grad_out_weight: float32 [1024, 1024], P('mp', ('dp', 'tok'))
- grad_gate_weight: float32 [1024, 4608], P(('dp', 'tok'), 'mp')
- grad_up_weight: float32 [1024, 4608], P(('dp', 'tok'), 'mp')
- grad_down_weight: float32 [4608, 1024], P('mp', ('dp', 'tok'))
- grad_gain_mix: float32 [1024], P('mp')
- grad_gain_ffn: float32 [1024], P('mp')
All inputs are finite; a program needn't handle non-finite values.
Results may differ from a plain program's by a relative error of at most 0.011.
Values may be sent and summed in bfloat16 or wider, within the bound.
No kernel may reach another device: no remote copies, remote signals or barrier semaphores. Data moves between devices by JAX's collectives and lax.ppermute only.
A program may use at most 192 MiB of HBM per device.

v0:
```python
import jax
import jax.numpy as jnp
from jax import lax
from jax.sharding import PartitionSpec as P

eps_norm = 1e-05


def passed_along(block, axis, distance):
    devices = range(lax.axis_size(axis))
    route = [(i - distance, i) for i in devices if i - distance in devices]
    return lax.ppermute(block, axis, route)


def collect_rows(values):
    return lax.all_gather(values, "mp", axis=1, tiled=True)


def sum_features(values):
    return lax.psum_scatter(values, "mp", scatter_dimension=1, tiled=True)


def total_row_count(values):
    return lax.psum(values, "mp")


def body(
    tokens,
    in_weight,
    conv_kernel,
    out_weight,
    gate_weight,
    up_weight,
    down_weight,
    mixer_norm_gain,
    gain_ffn,
    cotangent,
):
    f32 = jnp.float32
    brain_float_sixteen = jnp.bfloat16
    feature_width = tokens.shape[1]
    hidden_model_width = feature_width * lax.axis_size("mp")
    start_position = lax.axis_index("mp") * feature_width
    mix_slice = lax.dynamic_slice_in_dim(mixer_norm_gain, start_position, feature_width)
    feedforward_portion = lax.dynamic_slice_in_dim(gain_ffn, start_position, feature_width)
    w_in, w_out, w_gate, w_up, w_down = (
        lax.all_gather(in_weight, ("dp", "tok"), axis=0, tiled=True),
        lax.all_gather(out_weight, ("dp", "tok"), axis=1, tiled=True),
        lax.all_gather(gate_weight, ("dp", "tok"), axis=0, tiled=True),
        lax.all_gather(up_weight, ("dp", "tok"), axis=0, tiled=True),
        lax.all_gather(down_weight, ("dp", "tok"), axis=1, tiled=True),
    )
    taps = conv_kernel.astype(f32)
    complete_inputs = collect_rows(tokens).astype(f32)
    mixer_inverse_norm = lax.rsqrt(
        jnp.mean(complete_inputs * complete_inputs, -1, keepdims=True) + eps_norm
    )
    complete_normalized = complete_inputs * mixer_inverse_norm
    mixer_hidden = (complete_normalized * mixer_norm_gain).astype(brain_float_sixteen)
    proj = jnp.einsum("td,dkc->tkc", mixer_hidden, w_in, preferred_element_type=f32)
    gate_b = proj[:, 0]
    gate_c = proj[:, 1]
    gate_x = proj[:, 2]
    gated = (gate_b * gate_x).astype(brain_float_sixteen)
    edge = passed_along(gated[-2:], "tok", 1)
    extended = jnp.concatenate([edge, gated], 0).astype(f32)
    rows_count = gated.shape[0]
    conv = (
        taps[0] * extended[0:rows_count]
        + taps[1] * extended[1 : rows_count + 1]
        + taps[2] * extended[2:]
    )
    mixed_in = (gate_c * conv).astype(brain_float_sixteen)
    residual_stream = tokens.astype(f32) + sum_features(
        jnp.dot(mixed_in, w_out, preferred_element_type=f32)
    )
    square_sum = total_row_count(jnp.sum(residual_stream * residual_stream, -1))
    feedforward_inverse_norm = lax.rsqrt(square_sum[:, None] / hidden_model_width + eps_norm)
    feedforward_normalized = residual_stream * feedforward_inverse_norm
    feedforward_hidden = collect_rows(
        (feedforward_normalized * feedforward_portion).astype(brain_float_sixteen)
    )
    gate = jnp.dot(feedforward_hidden, w_gate, preferred_element_type=f32)
    upper = jnp.dot(feedforward_hidden, w_up, preferred_element_type=f32)
    sigma = jax.nn.sigmoid(gate)
    silu_gate = gate * sigma
    hidden = (silu_gate * upper).astype(brain_float_sixteen)
    result = residual_stream + sum_features(jnp.dot(hidden, w_down, preferred_element_type=f32))
    mixed = result.astype(brain_float_sixteen)
    cot_full = collect_rows(cotangent)
    dhidden = jnp.einsum("td,fd->tf", cot_full, w_down, preferred_element_type=f32)
    grad_down = jnp.einsum("tf,td->fd", hidden, cot_full, preferred_element_type=f32)
    dgate = (dhidden * upper * sigma * (1.0 + gate * (1.0 - sigma))).astype(brain_float_sixteen)
    dupper = (dhidden * silu_gate).astype(brain_float_sixteen)
    grad_gate = jnp.einsum("td,tf->df", feedforward_hidden, dgate, preferred_element_type=f32)
    grad_up = jnp.einsum("td,tf->df", feedforward_hidden, dupper, preferred_element_type=f32)
    back_ffn = jnp.einsum("tf,df->td", dgate, w_gate, preferred_element_type=f32) + jnp.einsum(
        "tf,df->td", dupper, w_up, preferred_element_type=f32
    )
    feedforward_hidden_gradient = sum_features(back_ffn)
    feedforward_gain_gradient = jnp.sum(feedforward_hidden_gradient * feedforward_normalized, 0)
    feedforward_scaled_input = feedforward_hidden_gradient * feedforward_portion
    feedforward_dot_product = total_row_count(
        jnp.sum(feedforward_scaled_input * feedforward_normalized, -1)
    )
    residual_gradient = cotangent.astype(f32) + feedforward_inverse_norm * (
        feedforward_scaled_input
        - feedforward_normalized * (feedforward_dot_product[:, None] / hidden_model_width)
    )
    dresid_full = collect_rows(residual_gradient.astype(brain_float_sixteen))
    grad_out = jnp.einsum("tc,td->cd", mixed_in, dresid_full, preferred_element_type=f32)
    dmixed = jnp.einsum("td,cd->tc", dresid_full, w_out, preferred_element_type=f32)
    dconv = (dmixed * gate_c).astype(brain_float_sixteen)
    dgate_c = dmixed * conv
    after = passed_along(dconv[:2], "tok", -1)
    dconv_ext = jnp.concatenate([dconv, after], 0).astype(f32)
    dconv_own = dconv_ext[0:rows_count]
    grad_taps = jnp.stack(
        [
            jnp.sum(dconv_own * extended[0:rows_count], 0),
            jnp.sum(dconv_own * extended[1 : rows_count + 1], 0),
            jnp.sum(dconv_own * extended[2:], 0),
        ],
        0,
    )
    dgated = taps[2] * dconv_own + taps[1] * dconv_ext[1 : rows_count + 1] + taps[0] * dconv_ext[2:]
    dproj = jnp.stack([dgated * gate_x, dgate_c, dgated * gate_b], 1).astype(brain_float_sixteen)
    grad_in = jnp.einsum("td,tkc->dkc", mixer_hidden, dproj, preferred_element_type=f32)
    mixer_hidden_gradient = sum_features(
        jnp.einsum("tkc,dkc->td", dproj, w_in, preferred_element_type=f32)
    )
    mixer_normalized = lax.dynamic_slice_in_dim(
        complete_normalized, start_position, feature_width, 1
    )
    mixer_gain_gradient = jnp.sum(mixer_hidden_gradient * mixer_normalized, 0)
    mixer_scaled_input = mixer_hidden_gradient * mix_slice
    mixer_dot_product = total_row_count(jnp.sum(mixer_scaled_input * mixer_normalized, -1))
    input_token_gradient = residual_gradient + mixer_inverse_norm * (
        mixer_scaled_input - mixer_normalized * (mixer_dot_product[:, None] / hidden_model_width)
    )
    grad_taps, mixer_gain_gradient, feedforward_gain_gradient = lax.psum(
        (grad_taps, mixer_gain_gradient, feedforward_gain_gradient), ("dp", "tok")
    )
    g_in, g_out, g_gate, g_up, g_down = (
        lax.psum_scatter(grad_in, ("dp", "tok"), scatter_dimension=0, tiled=True),
        lax.psum_scatter(grad_out, ("dp", "tok"), scatter_dimension=1, tiled=True),
        lax.psum_scatter(grad_gate, ("dp", "tok"), scatter_dimension=0, tiled=True),
        lax.psum_scatter(grad_up, ("dp", "tok"), scatter_dimension=0, tiled=True),
        lax.psum_scatter(grad_down, ("dp", "tok"), scatter_dimension=1, tiled=True),
    )
    return (
        mixed,
        input_token_gradient,
        g_in,
        grad_taps,
        g_out,
        g_gate,
        g_up,
        g_down,
        mixer_gain_gradient,
        feedforward_gain_gradient,
    )


def solution(mesh):
    return jax.shard_map(
        body,
        mesh=mesh,
        in_specs=(
            P(("dp", "tok"), "mp"),
            P(("dp", "tok"), None, "mp"),
            P(None, "mp"),
            P("mp", ("dp", "tok")),
            P(("dp", "tok"), "mp"),
            P(("dp", "tok"), "mp"),
            P("mp", ("dp", "tok")),
            P(),
            P(),
            P(("dp", "tok"), "mp"),
        ),
        out_specs=(
            P(("dp", "tok"), "mp"),
            P(("dp", "tok"), "mp"),
            P(("dp", "tok"), None, "mp"),
            P(None, "mp"),
            P("mp", ("dp", "tok")),
            P(("dp", "tok"), "mp"),
            P(("dp", "tok"), "mp"),
            P("mp", ("dp", "tok")),
            P("mp"),
            P("mp"),
        ),
        check_vma=False,
    )
```

profile of v0, /device:TPU:0, one launch (start us, length us, event | category | flops | bytes accessed | tf_op | source)
XLA Modules:
  0.0 1189.8 jit_solution(4125879485622382611)
XLA Ops:
  8.7 30.9 %all_gather.29 = bf16[256,1024]{1,0:T(8,128)(2,1)S(1)} all-gather(bf16[256,128]{1,0:T(8,128)(2,1)} %param.13), channel_id=1, replica_groups=mesh['dp'=2,'tok'=4,'mp'=4] {'dp','tok'}, dimensions={1}, use_global_device_ids=true | all-gather | bytes 589824 | tf_op jit(solution)/shard_map/all_gather | solution.py:48
  39.6 7.7 all-gather.9.cloned.1.call-done
  47.3 3.1 fusion.1
  50.4 43.3 %all-gather.11.cloned.1.call-done = bf16[1024,3,256]{2,0,1:T(8,128)(2,1)} async-done(((bf16[128,3,256]{2,0,1:T(8,128)(2,1)}), bf16[1024,3,256]{2,0,1:T(8,128)(2,1)}) %all-gather.11.cloned.1.call-update) | async-done | bytes 1572880 | tf_op jit(solution)/shard_map/all_gather | solution.py:47
  93.7 5.8 fusion.10
  99.7 3.8 collective-permute-start
  108.1 4.5 fusion.17
  114.0 69.7 %reduce-scatter.10.cloned.1.call-done = f32[2048,256]{1,0:T(8,128)} async-done(((f32[2048,1024]{1,0:T(8,128)}), f32[2048,256]{1,0:T(8,128)}) %reduce-scatter.10.cloned.1.call-update) | async-done | bytes 2097168 | tf_op jit(solution)/shard_map/reduce_scatter | solution.py:20
  183.7 3.2 multiply_reduce_fusion.7
  186.9 5.8 psum.42
  192.8 3.0 multiply_convert_fusion.8
  198.5 39.5 %all-gather.15.cloned.1.call-done = bf16[1024,1152]{1,0:T(8,128)(2,1)} async-done(((bf16[128,1152]{1,0:T(8,128)(2,1)}), bf16[1024,1152]{1,0:T(8,128)(2,1)}) %all-gather.15.cloned.1.call-update) | async-done | bytes 2359312 | tf_op jit(solution)/shard_map/all_gather | solution.py:49
  238.0 35.7 %all-gather.13.cloned.1.call-done = bf16[2048,1024]{1,0:T(8,128)(2,1)} async-done(((bf16[2048,256]{1,0:T(8,128)(2,1)}), bf16[2048,1024]{1,0:T(8,128)(2,1)}) %all-gather.13.cloned.1.call-update) | async-done | bytes 4194320 | tf_op jit(solution)/shard_map/all_gather | solution.py:16
  273.6 10.2 fusion.18
  283.9 44.0 %all-gather.17.cloned.1.call-done = bf16[1024,1152]{1,0:T(8,128)(2,1)} async-done(((bf16[128,1152]{1,0:T(8,128)(2,1)}), bf16[1024,1152]{1,0:T(8,128)(2,1)}) %all-gather.17.cloned.1.call-update) | async-done | bytes 2359312 | tf_op jit(solution)/shard_map/all_gather | solution.py:50
  327.9 10.2 fusion.19
  338.1 44.3 %all-gather.19.cloned.1.call-done = bf16[1152,1024]{1,0:T(8,128)(2,1)} async-done(((bf16[1152,128]{1,0:T(8,128)(2,1)}), bf16[1152,1024]{1,0:T(8,128)(2,1)}) %all-gather.19.cloned.1.call-update) | async-done | bytes 2359312 | tf_op jit(solution)/shard_map/all_gather | solution.py:51
  382.4 34.9 %all-gather.21.cloned.1.call-done = bf16[2048,1024]{1,0:T(8,128)(2,1)} async-done(((bf16[2048,256]{1,0:T(8,128)(2,1)}), bf16[2048,1024]{1,0:T(8,128)(2,1)}) %all-gather.21.cloned.1.call-update) | async-done | bytes 4194320 | tf_op jit(solution)/shard_map/all_gather | solution.py:16
  417.3 17.9 %multiply_convert_fusion = (bf16[2048,1152]{1,0:T(8,128)(2,1)}, bf16[2048,1152]{1,0:T(8,128)(2,1)}, bf16[2048,1152]{1,0:T(8,128)(2,1)}) fusion(f32[2048,1152]{1,0:T(8,128)} %fusion.18, f32[2048,1152]{1,0:T(8,128)} %fusion.19, bf16[2048,1024]{1,0:T(8,128)(2,1)} %all-gather.21.cloned.1.call-done, bf16[1152,1024]{1,0:T(8,128)(2,1)} %all-gather.19.cloned.1.call-done), kind=kOutput, calls=%fused_computation.2 | convolution fusion | flops 4867227648 | bytes 39583744 | tf_op jit(solution)/shard_map/td,fd->tf/dot_general | solution.py:91
  435.2 7.7 fusion.21
  442.9 8.5 convolution_add_fusion
  451.5 71.8 %reduce-scatter.14.cloned.1.call-done = f32[2048,256]{1,0:T(8,128)} async-done(((f32[2048,1024]{1,0:T(8,128)}), f32[2048,256]{1,0:T(8,128)}) %reduce-scatter.14.cloned.1.call-update) | async-done | bytes 2097168 | tf_op jit(solution)/shard_map/reduce_scatter | solution.py:20
  523.3 3.0 multiply_reduce_fusion
  526.3 5.9 psum.43
  532.2 3.4 fusion.14
  535.6 36.2 %all-gather.23.cloned.1.call-done = bf16[2048,1024]{1,0:T(8,128)(2,1)} async-done(((bf16[2048,256]{1,0:T(8,128)(2,1)}), bf16[2048,1024]{1,0:T(8,128)(2,1)}) %all-gather.23.cloned.1.call-update) | async-done | bytes 4194320 | tf_op jit(solution)/shard_map/all_gather | solution.py:16
  571.8 3.8 fusion.22
  575.7 2.3 fusion.7
  579.5 4.2 collective-permute-done.1
  587.1 5.8 convolution_bitcast_fusion
  593.0 10.6 fusion.20
  603.7 11.6 fusion.24
  615.4 10.6 fusion.25
  626.0 9.8 fusion.26
  637.1 4.5 fusion.23
  641.9 8.3 fusion.5
  650.3 6.0 convert_multiply_fusion
  656.4 7.5 reduce-scatter.16.cloned.1.call-done
  663.9 2.7 multiply_reduce_fusion.1
  666.6 22.3 %all-reduce = (f32[3,256]{1,0:T(4,128)}, f32[256]{0:T(256)}, f32[256]{0:T(256)}) all-reduce(f32[3,256]{1,0:T(4,128)S(1)} %pad_maximum_fusion.3, f32[256]{0:T(256)S(1)} %get-tuple-element.10, f32[256]{0:T(256)S(1)} %get-tuple-element.15), channel_id=1, replica_groups=mesh['dp'=2,'tok'=4,'mp'=4] {'dp','tok'}, use_global_device_ids=true, to_apply=%region_15.0 | all-reduce | flops 1280 | bytes 10240 | tf_op jit(solution)/shard_map/psum | solution.py:141
  688.9 6.4 psum.44
  695.4 43.2 %reduce-scatter.12.cloned.1.call-done = f32[2048,256]{1,0:T(8,128)} async-done(((f32[2048,1024]{1,0:T(8,128)}), f32[2048,256]{1,0:T(8,128)}) %reduce-scatter.12.cloned.1.call-update) | async-done | bytes 2097168 | tf_op jit(solution)/shard_map/reduce_scatter | solution.py:20
  738.6 5.2 multiply_add_fusion
  743.7 94.2 %reduce-scatter.22.cloned.1.call-done = f32[128,1152]{1,0:T(8,128)} async-done(((f32[1024,1152]{1,0:T(8,128)}), f32[128,1152]{1,0:T(8,128)}) %reduce-scatter.22.cloned.1.call-update) | async-done | bytes 589840 | tf_op jit(solution)/shard_map/reduce_scatter | solution.py:147
  837.9 99.3 %reduce-scatter.24.cloned.1.call-done = f32[128,1152]{1,0:T(8,128)} async-done(((f32[1024,1152]{1,0:T(8,128)}), f32[128,1152]{1,0:T(8,128)}) %reduce-scatter.24.cloned.1.call-update) | async-done | bytes 589840 | tf_op jit(solution)/shard_map/reduce_scatter | solution.py:148
  937.2 99.5 %reduce-scatter.26.cloned.1.call-done = f32[1152,128]{1,0:T(8,128)} async-done(((f32[1152,1024]{1,0:T(8,128)}), f32[1152,128]{1,0:T(8,128)}) %reduce-scatter.26.cloned.1.call-update) | async-done | bytes 589840 | tf_op jit(solution)/shard_map/reduce_scatter | solution.py:149
  1036.8 67.7 %reduce-scatter.20.cloned.1.call-done = f32[256,128]{1,0:T(8,128)} async-done(((f32[256,1024]{1,0:T(8,128)}), f32[256,128]{1,0:T(8,128)}) %reduce-scatter.20.cloned.1.call-update) | async-done | bytes 131088 | tf_op jit(solution)/shard_map/reduce_scatter | solution.py:146
  1104.4 78.5 %reduce-scatter.18.cloned.1.call-done = f32[128,3,256]{2,0,1:T(8,128)} async-done(((f32[1024,3,256]{2,0,1:T(8,128)}), f32[128,3,256]{2,0,1:T(8,128)}) %reduce-scatter.18.cloned.1.call-update) | async-done | bytes 393232 | tf_op jit(solution)/shard_map/reduce_scatter | solution.py:145
  (89 shorter events, 17.2 us)
Async XLA Ops:
  7.2 40.1 %all-gather.9.cloned.1.call-start = ((), (), s32[]{:S(2)}) async-start(), calls=%async_computation.9 | async-start | bytes 5242880 | tf_op jit(solution)/shard_map/all_gather | solution.py:16
  7.9 85.8 %all-gather.11.cloned.1.call-start = ((), (), s32[]{:S(2)}) async-start(), calls=%async_computation.10 | async-start | bytes 1769472 | tf_op jit(solution)/shard_map/all_gather | solution.py:47
  8.7 85.0 %copy-start.11 = (f32[1024]{0:T(1024)S(1)}, f32[1024]{0:T(1024)}, u32[]{:S(2)}) copy-start(f32[1024]{0:T(1024)} %param.17) | copy-start | bytes 12292
  8.7 175.0 %reduce-scatter.10.cloned.1.call-start = ((), (), s32[]{:S(2)}) async-start(), calls=%async_computation.11 | async-start | bytes 10485760 | tf_op jit(solution)/shard_map/reduce_scatter | solution.py:20
  39.6 67.5 %copy-start.7 = (bf16[256,1024]{1,0:T(8,128)(2,1)}, bf16[256,1024]{1,0:T(8,128)(2,1)S(1)}, u32[]{:S(2)}) copy-start(bf16[256,1024]{1,0:T(8,128)(2,1)S(1)} %all_gather.29) | copy-start | bytes 1572868
  99.5 5.6 copy-start.1
  99.5 4.1 copy-start.10
  99.7 5.1 collective-permute-start
  107.1 1.0 copy-start.4
  112.6 71.1 %copy-start.6 = (bf16[2048,256]{1,0:T(8,128)(2,1)S(1)}, bf16[2048,256]{1,0:T(8,128)(2,1)}, u32[]{:S(2)}) copy-start(bf16[2048,256]{1,0:T(8,128)(2,1)} %param.10) | copy-start | bytes 3145732
  112.6 125.4 %all-gather.15.cloned.1.call-start = ((), (), s32[]{:S(2)}) async-start(), calls=%async_computation.13 | async-start | bytes 2654208 | tf_op jit(solution)/shard_map/all_gather | solution.py:49
  113.2 160.4 %all-gather.13.cloned.1.call-start = ((), (), s32[]{:S(2)}) async-start(), calls=%async_computation.12 | async-start | bytes 5242880 | tf_op jit(solution)/shard_map/all_gather | solution.py:16
  195.8 132.1 %all-gather.17.cloned.1.call-start = ((), (), s32[]{:S(2)}) async-start(), calls=%async_computation.14 | async-start | bytes 2654208 | tf_op jit(solution)/shard_map/all_gather | solution.py:50
  196.4 186.0 %all-gather.19.cloned.1.call-start = ((), (), s32[]{:S(2)}) async-start(), calls=%async_computation.15 | async-start | bytes 2654208 | tf_op jit(solution)/shard_map/all_gather | solution.py:51
  197.1 220.2 %all-gather.21.cloned.1.call-start = ((), (), s32[]{:S(2)}) async-start(), calls=%async_computation.17 | async-start | bytes 5242880 | tf_op jit(solution)/shard_map/all_gather | solution.py:16
  197.9 325.4 %reduce-scatter.14.cloned.1.call-start = ((), (), s32[]{:S(2)}) async-start(), calls=%async_computation.18 | async-start | bytes 10485760 | tf_op jit(solution)/shard_map/reduce_scatter | solution.py:20
  417.3 17.9 %copy-start.12 = (bf16[1024,1152]{1,0:T(8,128)(2,1)S(1)}, bf16[1024,1152]{1,0:T(8,128)(2,1)}, u32[]{:S(2)}) copy-start(bf16[1024,1152]{1,0:T(8,128)(2,1)} %all-gather.15.cloned.1.call-done) | copy-start | bytes 7077892
  435.2 7.7 copy-start.13
  435.2 7.7 copy-start.15
  451.4 80.7 %copy-start.2 = (bf16[2048,256]{1,0:T(8,128)(2,1)S(1)}, bf16[2048,256]{1,0:T(8,128)(2,1)}, u32[]{:S(2)}) copy-start(bf16[2048,256]{1,0:T(8,128)(2,1)} %param.19) | copy-start | bytes 3145732
  451.4 120.4 %all-gather.23.cloned.1.call-start = ((), (), s32[]{:S(2)}) async-start(), calls=%async_computation.19 | async-start | bytes 5242880 | tf_op jit(solution)/shard_map/all_gather | solution.py:16
  535.6 128.4 %reduce-scatter.16.cloned.1.call-start = ((), (), s32[]{:S(2)}) async-start(), calls=%async_computation.20 | async-start | bytes 10485760 | tf_op jit(solution)/shard_map/reduce_scatter | solution.py:20
  571.8 3.8 copy-start.3
  575.7 8.2 slice-start
  575.7 8.2 slice-start.1
  578.0 7.8 copy-start.8
  578.1 5.6 collective-permute-start.1
  585.3 1.0 copy-start.9
  585.4 1.8 copy-start.14
  593.0 145.6 %reduce-scatter.12.cloned.1.call-start = ((), (), s32[]{:S(2)}) async-start(), calls=%async_computation.16 | async-start | bytes 10485760 | tf_op jit(solution)/shard_map/reduce_scatter | solution.py:20
  603.7 234.3 %reduce-scatter.22.cloned.1.call-start = ((), (), s32[]{:S(2)}) async-start(), calls=%async_computation.23 | async-start | bytes 5308416 | tf_op jit(solution)/shard_map/reduce_scatter | solution.py:147
  615.3 321.9 %reduce-scatter.24.cloned.1.call-start = ((), (), s32[]{:S(2)}) async-start(), calls=%async_computation.24 | async-start | bytes 5308416 | tf_op jit(solution)/shard_map/reduce_scatter | solution.py:148
  626.0 410.8 %reduce-scatter.26.cloned.1.call-start = ((), (), s32[]{:S(2)}) async-start(), calls=%async_computation.25 | async-start | bytes 5308416 | tf_op jit(solution)/shard_map/reduce_scatter | solution.py:149
  635.8 1.3 copy-start.5
  635.9 468.6 %reduce-scatter.20.cloned.1.call-start = ((), (), s32[]{:S(2)}) async-start(), calls=%async_computation.22 | async-start | bytes 1179648 | tf_op jit(solution)/shard_map/reduce_scatter | solution.py:146
  641.6 541.4 %reduce-scatter.18.cloned.1.call-start = ((), (), s32[]{:S(2)}) async-start(), calls=%async_computation.21 | async-start | bytes 3538944 | tf_op jit(solution)/shard_map/reduce_scatter | solution.py:145
  656.4 82.2 %copy-start = (f32[2048,256]{1,0:T(8,128)S(1)}, f32[2048,256]{1,0:T(8,128)}, u32[]{:S(2)}) copy-start(f32[2048,256]{1,0:T(8,128)} %get-tuple-element.23) | copy-start | bytes 6291460
Sparse Core Ops, SparseCore 0:
  9.6 37.7 all-gather.8
  49.5 44.1 all-gather.10
  112.7 70.9 reduce-scatter.9
  185.9 52.0 all-gather.14
  240.0 33.5 all-gather.12
  275.8 52.0 all-gather.16
  330.1 52.2 all-gather.18
  384.0 33.2 all-gather.20
  451.6 71.6 reduce-scatter.13
  535.7 36.1 all-gather.22
  593.1 70.7 reduce-scatter.15
  666.5 71.9 reduce-scatter.11
  742.8 95.1 reduce-scatter.21
  842.0 95.1 reduce-scatter.23
  941.3 95.4 reduce-scatter.25
  1040.6 63.7 reduce-scatter.19
  1108.9 74.0 reduce-scatter.17
where the time goes:
time: 1200 us; the launch traced here: 1190 us
  waiting for transfers between devices  927 us (77%)
  matrix products  130 us (11%)
  blocking collectives  71.4 us (6%)
  other arithmetic  36.5 us (3%)
  between operations  14.6 us (1%)
    reduce_scatter x4, waiting for transfers between devices, sum_features(): return lax.psum_scatter(values, 'mp', scatter_dimension=1, tiled=True)  192 us
    all_gather x4, waiting for transfers between devices, collect_rows(): return lax.all_gather(values, 'mp', axis=1, tiled=True)  114 us
    reduce_scatter x1, waiting for transfers between devices, body(): lax.psum_scatter(grad_down, ('dp', 'tok'), scatter_dimension=1, tiled=True)  99.5 us
    reduce_scatter x1, waiting for transfers between devices, body(): lax.psum_scatter(grad_up, ('dp', 'tok'), scatter_dimension=0, tiled=True)  99.3 us
    reduce_scatter x1, waiting for transfers between devices, body(): lax.psum_scatter(grad_gate, ('dp', 'tok'), scatter_dimension=0, tiled=True)  94.2 us
    reduce_scatter x1, waiting for transfers between devices, body(): lax.psum_scatter(grad_in, ('dp', 'tok'), scatter_dimension=0, tiled=True)  78.5 us
    reduce_scatter x1, waiting for transfers between devices, body(): lax.psum_scatter(grad_out, ('dp', 'tok'), scatter_dimension=1, tiled=True)  67.7 us
    all_gather x1, waiting for transfers between devices, body(): lax.all_gather(down_weight, ('dp', 'tok'), axis=1, tiled=True)  44.3 us
  transfers between devices with their start and end apart: 19, of which 19 were waited for; matrix products, arithmetic and copies ran while one was open for 8% of the time, Pallas kernels for 0%

commit v1 on v0

v1 whole, which is shorter than its diff:
```python
import jax
import jax.numpy as jnp
from jax import lax
from jax.sharding import Mesh
from jax.sharding import PartitionSpec as P

EPS = 1e-05
F32 = jnp.float32
BF16 = jnp.bfloat16


def swap(value, axis):
    return lax.ppermute(value, axis, [(0, 1), (1, 0)])


def fetch(value, axis, distance):
    size = lax.axis_size(axis)
    return lax.ppermute(value, axis, [(s, (s - distance) % size) for s in range(size)])


def deliver(value, axis, distance):
    size = lax.axis_size(axis)
    return lax.ppermute(value, axis, [(s, (s + distance) % size) for s in range(size)])


def dot(left, right, contract):
    return lax.dot_general(left, right, (contract, ((), ())), preferred_element_type=F32)


def nn(left, right):
    return dot(left, right, ((1,), (0,)))


def nt(left, right):
    return dot(left, right, ((1,), (1,)))


def tn(left, right):
    return dot(left, right, ((0,), (0,)))


def total(values):
    result = values[0].astype(F32)
    for value in values[1:]:
        result = result + value.astype(F32)
    return result


def gather_rows(shard):
    blocks = [shard] + [fetch(shard, "tok", j) for j in range(1, lax.axis_size("tok"))]
    parts = list(blocks)
    for i in range(1, lax.axis_size("dp")):
        parts += [fetch(block, "dp", i) for block in blocks]
    own = jnp.concatenate(parts, 0)
    return blocks[-1], own, swap(own, "c")


def scatter_rows(own, other):
    pair = total([own, swap(other, "c")]).astype(BF16)
    steps = lax.axis_size("dp")
    size = pair.shape[0] // steps
    mine = total(
        [pair[:size]]
        + [deliver(pair[i * size : (i + 1) * size], "dp", i) for i in range(1, steps)]
    ).astype(BF16)
    steps = lax.axis_size("tok")
    size = mine.shape[0] // steps
    return total(
        [mine[:size]]
        + [deliver(mine[i * size : (i + 1) * size], "tok", i) for i in range(1, steps)]
    )


def body(
    tokens,
    in_weight,
    conv_kernel,
    out_weight,
    gate_weight,
    up_weight,
    down_weight,
    mixer_norm_gain,
    gain_ffn,
    cotangent,
):
    x, z, y, c = (lax.axis_index(name) for name in ("dp", "tok", "y", "c"))
    nx, nz = lax.axis_size("dp"), lax.axis_size("tok")
    width = tokens.shape[1]
    features = 4 * width
    rows = tokens.shape[0] // 2
    half = rows // 2
    chunk = in_weight.shape[0]

    position = lax.broadcasted_iota(jnp.int32, (features, features), 1)
    block = position // chunk
    spread = (((x + block // nz) % nx) * nz + (z + block % nz) % nz) * chunk + position % chunk
    place = lax.broadcasted_iota(jnp.int32, (features, features), 0)
    piece = place // width
    natural = (2 * (y ^ (piece // 2)) + (c ^ (piece % 2))) * width + place % width
    order = (natural == spread).astype(BF16)

    def spread_gain(gain):
        return jnp.sum(jnp.where(place == spread, gain[:, None], 0.0), 0)

    def pick_rows(value, index, size):
        return lax.dynamic_slice_in_dim(value, index * size, size, 0)

    def feature_rows(value):
        mine, theirs = pick_rows(value, c, rows), pick_rows(value, 1 - c, rows)
        return jnp.concatenate([mine, swap(theirs, "c")], 1)

    def by_rank(index, first, second):
        return jnp.where(
            index == 0,
            jnp.concatenate([first, second], 0),
            jnp.concatenate([second, first], 0),
        )

    near = feature_rows(tokens)
    full = nn(jnp.concatenate([near, swap(near, "y")], 1), order).astype(BF16)

    flat_in = in_weight.reshape(chunk, 3 * width)
    first = jnp.concatenate([flat_in, out_weight.T], 1)
    last, first_own, first_other = gather_rows(first)
    gate_weight, up_weight, down_rows, last = lax.optimization_barrier(
        (gate_weight, up_weight, down_weight.T, last)
    )
    last, gate_own, gate_other = gather_rows(gate_weight)
    up_weight, down_rows, last = lax.optimization_barrier((up_weight, down_rows, last))
    last, up_own, up_other = gather_rows(up_weight)
    down_rows, last = lax.optimization_barrier((down_rows, last))
    last, down_own, down_other = gather_rows(down_rows)
    w_in = (first_own[:, : 3 * width], first_other[:, : 3 * width])
    w_out = (first_own[:, 3 * width :], first_other[:, 3 * width :])
    w_gate, w_up, w_down = (gate_own, gate_other), (up_own, up_other), (down_own, down_other)

    near_cot = feature_rows(cotangent)
    pieces_cot = jnp.concatenate([near_cot, swap(near_cot, "y")], 1)
    pieces_cot = jnp.concatenate(
        [pick_rows(pieces_cot, y, half), pick_rows(pieces_cot, 1 - y, half)], 0
    )
    cot = nn(pieces_cot, order).astype(BF16)

    full32 = full.astype(F32)
    inverse_mix = lax.rsqrt(jnp.mean(full32 * full32, -1, keepdims=True) + EPS)
    gain_mix_spread = spread_gain(mixer_norm_gain)
    gain_ffn_spread = spread_gain(gain_ffn)
    h_mix = (full32 * inverse_mix * gain_mix_spread).astype(BF16)

    def taps_of(which):
        other = swap(conv_kernel, "c")
        return (conv_kernel if which == 0 else other).astype(F32)

    gates = []
    for w in w_in:
        proj = nn(h_mix, w)
        gates.append((proj[:, :width], proj[:, width : 2 * width], proj[:, 2 * width :]))
    gated = [(b * xin).astype(BF16) for b, _, xin in gates]
    ranks = nz * 2
    edge = lax.ppermute(
        jnp.concatenate([gated[1][-2:], gated[0][-2:]], 1),
        ("tok", "c"),
        [(i, i + 1) for i in range(ranks - 1)],
    )
    taps = [taps_of(0), taps_of(1)]
    extended, convs, mixed_in = [], [], []
    for i in range(2):
        ext = jnp.concatenate([edge[:, i * width : (i + 1) * width], gated[i]], 0).astype(F32)
        conv = taps[i][0] * ext[:rows] + taps[i][1] * ext[1 : rows + 1] + taps[i][2] * ext[2:]
        extended.append(ext)
        convs.append(conv)
        mixed_in.append((gates[i][1] * conv).astype(BF16))

    def project_out(index):
        return nt(pick_rows(mixed_in[0], index, half), w_out[0]) + nt(
            pick_rows(mixed_in[1], index, half), w_out[1]
        )

    arrived = swap(project_out(1 - y).astype(BF16), "y")
    residual = pick_rows(full, y, half).astype(F32) + project_out(y) + arrived.astype(F32)

    inverse_ffn = lax.rsqrt(jnp.mean(residual * residual, -1, keepdims=True) + EPS)
    normalized = residual * inverse_ffn
    h_own = (normalized * gain_ffn_spread).astype(BF16)
    h = jnp.concatenate([h_own, swap(h_own, "y")], 0)
    hidden, d_gate, d_up = [], [], []
    for i in range(2):
        gate, up = nn(h, w_gate[i]), nn(h, w_up[i])
        sigma = jax.nn.sigmoid(gate)
        silu = gate * sigma
        hidden.append((silu * up).astype(BF16))
        dhid = nn(cot, w_down[i])
        d_gate.append((dhid * up * sigma * (1.0 + gate * (1.0 - sigma))).astype(BF16))
        d_up.append((dhid * silu).astype(BF16))

    def back(part):
        return sum(
            nt(d_gate[i][part], w_gate[i]) + nt(d_up[i][part], w_up[i]) for i in range(2)
        )

    arrived = swap(back(slice(half, None)).astype(BF16), "y")
    d_h = back(slice(0, half)) + arrived.astype(F32)
    grad_gain_ffn = jnp.sum(d_h * normalized, 0)
    scaled = d_h * gain_ffn_spread
    d_res = cot[:half].astype(F32) + inverse_ffn * (
        scaled - normalized * jnp.mean(scaled * normalized, -1, keepdims=True)
    )
    d_res_own = d_res.astype(BF16)
    d_res_full = by_rank(y, d_res_own, swap(d_res_own, "y"))

    grad_down = scatter_rows(*(tn(cot, hidden[i]).astype(BF16) for i in range(2)))
    grad_gate = scatter_rows(*(tn(h, d_gate[i]).astype(BF16) for i in range(2)))
    grad_up = scatter_rows(*(tn(h, d_up[i]).astype(BF16) for i in range(2)))

    made = nt(hidden[0], w_down[0]) + nt(hidden[1], w_down[1])
    made = jnp.concatenate([made[:half] + residual, made[half:]], 0).astype(BF16)
    made = nt(made, order).astype(BF16)
    arrived = swap(made[:, 2 * width :], "y").astype(F32)
    kept = made[:, : 2 * width].astype(F32)
    out_near = by_rank(
        y,
        (kept[:half] + arrived[half:]).astype(BF16),
        (kept[half:] + arrived[:half]).astype(BF16),
    )
    mixed = by_rank(c, out_near[:, :width], swap(out_near[:, width:], "c"))

    d_conv, d_c = [], []
    for i in range(2):
        d_y = nn(d_res_full, w_out[i])
        d_conv.append((d_y * gates[i][1]).astype(BF16))
        d_c.append(d_y * convs[i])
    after = lax.ppermute(
        jnp.concatenate([d_conv[1][:2], d_conv[0][:2]], 1),
        ("tok", "c"),
        [(i + 1, i) for i in range(ranks - 1)],
    )
    d_proj, grad_taps, row_dot = [], [], 0.0
    for i in range(2):
        ext = jnp.concatenate([d_conv[i], after[:, i * width : (i + 1) * width]], 0).astype(F32)
        mine = ext[:rows]
        grad_taps.append(
            jnp.stack([jnp.sum(mine * extended[i][k : rows + k], 0) for k in range(3)], 0)
        )
        d_gated = taps[i][2] * mine + taps[i][1] * ext[1 : rows + 1] + taps[i][0] * ext[2:]
        b, gate_c, xin = gates[i]
        parts = [(d_gated * xin).astype(BF16), d_c[i].astype(BF16), (d_gated * b).astype(BF16)]
        row_dot = row_dot + jnp.sum(
            parts[0].astype(F32) * b + parts[1].astype(F32) * gate_c + parts[2].astype(F32) * xin,
            -1,
        )
        d_proj.append(jnp.concatenate(parts, 1))
    lanes = 128
    row_dot = row_dot.reshape(rows // lanes, lanes)
    row_mean = ((row_dot + swap(row_dot, "y")) / features).reshape(rows, 1)
    w_in_pieces = [nn(order, w).astype(BF16) for w in w_in]

    def back_in(part):
        return nt(d_proj[0], w_in_pieces[0][part]) + nt(d_proj[1], w_in_pieces[1][part])

    arrived = swap(back_in(slice(2 * width, None)).astype(BF16), "y")
    d_h_mix = back_in(slice(0, 2 * width)) + arrived.astype(F32)
    grad_first = scatter_rows(
        *(
            jnp.concatenate(
                [tn(h_mix, d_proj[i]).astype(BF16), tn(d_res_full, mixed_in[i]).astype(BF16)], 1
            )
            for i in range(2)
        )
    )

    near_normal = near.astype(F32) * inverse_mix
    d_res_near = nt(d_res_full, order[: 2 * width])

    def own_gain(gain):
        return jnp.concatenate(
            [
                lax.dynamic_slice_in_dim(gain, (2 * y + c) * width, width),
                lax.dynamic_slice_in_dim(gain, (2 * y + 1 - c) * width, width),
            ]
        )

    grad_near = d_res_near + inverse_mix * (
        d_h_mix * own_gain(mixer_norm_gain) - near_normal * row_mean
    )
    input_gradient = by_rank(c, grad_near[:, :width], swap(grad_near[:, width:], "c"))

    def place_near(value):
        empty = jnp.zeros((value.shape[0], features), F32)
        empty = lax.dynamic_update_slice(empty, value[:, :width], (0, (2 * y + c) * width))
        return lax.dynamic_update_slice(empty, value[:, width:], (0, (2 * y + 1 - c) * width))

    near_sums = jnp.concatenate(
        [
            jnp.concatenate(grad_taps, 1),
            jnp.sum(d_h_mix * near_normal, 0)[None],
        ],
        0,
    )
    ffn_sum = jnp.sum(jnp.where(place == spread, grad_gain_ffn[None], 0.0), 1)
    sums = lax.psum(
        jnp.concatenate([place_near(near_sums), ffn_sum[None]], 0), ("dp", "tok", "y", "c")
    )
    sums = lax.dynamic_slice_in_dim(sums, (2 * y + c) * width, width, 1)

    return (
        mixed,
        input_gradient,
        grad_first[:, : 3 * width].reshape(chunk, 3, width),
        sums[:3],
        grad_first[:, 3 * width :].T,
        grad_gate,
        grad_up,
        grad_down.T,
        sums[3],
        sums[4],
    )


def solution(mesh):
    split = Mesh(
        mesh.devices.reshape(mesh.shape["dp"], mesh.shape["tok"], mesh.shape["mp"] // 2, 2),
        ("dp", "tok", "y", "c"),
    )
    tok, mp = ("dp", "tok"), ("y", "c")
    return jax.shard_map(
        body,
        mesh=split,
        in_specs=(
            P(tok, mp),
            P(tok, None, mp),
            P(None, mp),
            P(mp, tok),
            P(tok, mp),
            P(tok, mp),
            P(mp, tok),
            P(),
            P(),
            P(tok, mp),
        ),
        out_specs=(
            P(tok, mp),
            P(tok, mp),
            P(tok, None, mp),
            P(None, mp),
            P(mp, tok),
            P(tok, mp),
            P(tok, mp),
            P(mp, tok),
            P(mp),
            P(mp),
        ),
        check_vma=False,
    )
```

time: 1200 us -> 634 us (0.53)
  waiting for transfers between devices: 927 us -> 222 us
  starting transfers between devices: 6.68 us -> 111 us
  local copies, waits for them, and re-layouts: 4.42 us -> 35.4 us
  blocking collectives: 71.4 us -> 84 us
  between operations: 14.6 us -> 2.34 us
    reduce_scatter x9 -> x0, waiting for transfers between devices: 631 us -> none  [the longest x4 192 us: sum_features(): return lax.psum_scatter(values, 'mp', scatter_dimension=1, tiled=True)]
    all_gather x8 -> x0, waiting for transfers between devices: 286 us -> none  [the longest x4 114 us: collect_rows(): return lax.all_gather(values, 'mp', axis=1, tiled=True)]
    ppermute x2 -> x68, waiting for transfers between devices: 5.42 us -> 222 us  [the longest x22 82.7 us: swap(): return lax.ppermute(value, axis, [(0, 1), (1, 0)])]
    ppermute x2 -> x68, starting transfers between devices: 5.22 us -> 111 us  [the longest x28 58 us: fetch(): lax.ppermute(value, axis, [(s, (s - distance) % size) for s in range(size)])]
    psum x4 -> x1, blocking collectives: 40.4 us -> 84 us  [body(): lax.psum(jnp.concatenate([place_near(near_sums), ffn_sum[None]], 0), ('dp...]
    all_gather x1 -> x0, blocking collectives: 30.9 us -> none  [body(): lax.all_gather(out_weight, ('dp', 'tok'), axis=1, tiled=True)]
    unnamed x36 -> x172, local copies, waits for them, and re-layouts: 3.56 us -> 20.1 us
    slice x3 -> x22, local copies, waits for them, and re-layouts: 0.02 us -> 12.1 us  [the longest x4 3.67 us: scatter_rows(): pair[i * size:(i + 1) * size]]
  transfers between devices with their start and end apart: 19 -> 68, of which waited for: 19 -> 32; matrix products, arithmetic and copies ran while one was open for 8% -> 23% of each run, Pallas kernels for 0% -> 0%
where the time goes in v1:
time: 634 us; the launch traced here: 628 us
  waiting for transfers between devices  222 us (35%)
  matrix products  132 us (21%)
  starting transfers between devices  111 us (18%)
  blocking collectives  84 us (13%)
  other arithmetic  41.2 us (6%)
  local copies, waits for them, and re-layouts  35.4 us (6%)
    dot_general x44, matrix products, dot(): lax.dot_general(left, right, (contract, ((), ())), preferred_element_type...  132 us
    psum x1, blocking collectives, body(): lax.psum(jnp.concatenate([place_near(near_sums), ffn_sum[None]], 0), ('dp...  84 us
    ppermute x22, waiting for transfers between devices, swap(): return lax.ppermute(value, axis, [(0, 1), (1, 0)])  82.7 us
    ppermute x28, waiting for transfers between devices, fetch(): lax.ppermute(value, axis, [(s, (s - distance) % size) for s in range(size)])  76 us
    ppermute x16, waiting for transfers between devices, deliver(): lax.ppermute(value, axis, [(s, (s + distance) % size) for s in range(size)])  63 us
    ppermute x28, starting transfers between devices, fetch(): lax.ppermute(value, axis, [(s, (s - distance) % size) for s in range(size)])  58 us
    ppermute x16, starting transfers between devices, deliver(): lax.ppermute(value, axis, [(s, (s + distance) % size) for s in range(size)])  36.1 us
    unnamed x172, local copies, waits for them, and re-layouts  20.1 us
  transfers between devices with their start and end apart: 68, of which 32 were waited for; matrix products, arithmetic and copies ran while one was open for 23% of the time, Pallas kernels for 0%

profile of v1, /device:TPU:0, one launch (start us, length us, event | category | flops | bytes accessed | tf_op | source)
XLA Modules:
  0.0 628.1 jit_solution(10843190765338946267)
XLA Ops:
  23.5 8.6 %collective-permute-done.3 = bf16[128,1024]{0,1:T(8,128)(2,1)} collective-permute-done((bf16[128,1024]{0,1:T(8,128)(2,1)}, bf16[128,1024]{0,1:T(8,128)(2,1)}, u32[]{:S(2)}, u32[]{:S(2)}) %collective-permute-start.3) | collective-permute-done | bytes 262176 | tf_op jit(solution)/shard_map/ppermute | solution.py:18
  47.3 4.5 convolution_convert_fusion.9
  53.6 5.7 collective-permute-done.16
  64.4 3.9 collective-permute-start.23
  68.5 7.3 %collective-permute-done.23 = bf16[128,1152]{1,0:T(8,128)(2,1)S(1)} collective-permute-done((bf16[128,1152]{1,0:T(8,128)(2,1)S(1)}, bf16[128,1152]{1,0:T(8,128)(2,1)S(1)}, u32[]{:S(2)}, u32[]{:S(2)}) %collective-permute-start.23) | collective-permute-done | bytes 294944 | tf_op jit(solution)/shard_map/ppermute | solution.py:18
  75.8 13.2 %collective-permute-start.22 = (bf16[128,1152]{1,0:T(8,128)(2,1)S(1)}, bf16[128,1152]{1,0:T(8,128)(2,1)S(1)}, u32[]{:S(2)}, u32[]{:S(2)}) collective-permute-start(bf16[128,1152]{1,0:T(8,128)(2,1)S(1)} %copy-done.31), channel_id=1, source_target_pairs={{0,8},{4,12},{8,0},{12,4},{1,9},{5,13},{9,1},{13,5},{2,10},{6,14},... | collective-permute-start | bytes 884744 | tf_op jit(solution)/shard_map/ppermute | solution.py:18
  90.6 6.2 collective-permute-done.22
  100.5 6.2 collective-permute-done.19
  108.2 4.8 collective-permute-done.20
  114.6 4.8 collective-permute-done.24
  126.4 4.6 collective-permute-start.28
  131.2 4.4 collective-permute-done.28
  135.5 4.2 collective-permute-start.30
  139.8 8.7 %collective-permute-done.29 = bf16[128,1152]{0,1:T(8,128)(2,1)S(1)} collective-permute-done((bf16[128,1152]{0,1:T(8,128)(2,1)S(1)}, bf16[128,1152]{0,1:T(8,128)(2,1)S(1)}, u32[]{:S(2)}, u32[]{:S(2)}) %collective-permute-start.29) | collective-permute-done | bytes 294944 | tf_op jit(solution)/shard_map/ppermute | solution.py:18
  150.2 4.9 collective-permute-done.31
  179.0 18.9 %collective-permute-done.12 = bf16[512,1024]{1,0:T(8,128)(2,1)S(1)} collective-permute-done((bf16[512,1024]{1,0:T(8,128)(2,1)S(1)}, bf16[512,1024]{1,0:T(8,128)(2,1)S(1)}, u32[]{:S(2)}, u32[]{:S(2)}) %collective-permute-start.12) | collective-permute-done | bytes 1048608 | tf_op jit(solution)/shard_map/ppermute | solution.py:13
  206.3 16.9 %collective-permute-done.13 = bf16[512,1024]{1,0:T(8,128)(2,1)S(1)} collective-permute-done((bf16[512,1024]{1,0:T(8,128)(2,1)S(1)}, bf16[512,1024]{1,0:T(8,128)(2,1)S(1)}, u32[]{:S(2)}, u32[]{:S(2)}) %collective-permute-start.13) | collective-permute-done | bytes 1048608 | tf_op jit(solution)/shard_map/ppermute | solution.py:13
  223.1 4.9 fusion.127
  228.1 7.5 %fusion.126 = f32[1024,1152]{1,0:T(8,128)} fusion(bf16[1024,1152]{1,0:T(8,128)(2,1)} %collective-permute-done.36, bf16[512,1024]{1,0:T(8,128)(2,1)S(1)} %collective-permute-done.13, bf16[512,1024]{1,0:T(8,128)(2,1)S(1)} %multiply_convert_fusion.6), kind=kOutput, calls=%fused_computation.295 | convolution fusion | flops 2420113408 | bytes 9175040 | tf_op jit(solution)/shard_map/dot_general | solution.py:27
  235.5 8.6 %multiply_convert_fusion = (bf16[1024,1152]{1,0:T(8,128)(2,1)}, bf16[1024,1152]{1,0:T(8,128)(2,1)}, bf16[1024,1152]{1,0:T(8,128)(2,1)S(1)}) fusion(f32[1024,1152]{1,0:T(8,128)S(1)} %fusion.127, f32[1024,1152]{1,0:T(8,128)} %fusion.126, bf16[1024,1024]{1,0:T(8,128)(2,1)S(1)} %fusion.45, bf16[1024,1152]{0,1:T(8,128)(2,1)} %collective-permute-done.37), kind=kOutput, calls=%fused_computation.27 | convolution fusion | flops 2433613824 | bytes 20971520 | tf_op jit(solution)/shard_map/dot_general | solution.py:27
  245.5 4.3 convolution_convert_fusion
  249.8 5.3 fusion.129
  255.1 5.4 fusion.128
  260.5 9.1 %multiply_convert_fusion.3 = (bf16[1024,1152]{1,0:T(8,128)(2,1)}, bf16[1024,1152]{1,0:T(8,128)(2,1)}, bf16[1024,1152]{1,0:T(8,128)(2,1)}) fusion(f32[1024,1152]{1,0:T(8,128)} %fusion.129, f32[1024,1152]{1,0:T(8,128)} %fusion.128, bf16[1024,1024]{1,0:T(8,128)(2,1)S(1)} %fusion.45, bf16[1024,1152]{0,1:T(8,128)(2,1)S(1)} %copy-done.34), kind=kOutput, calls=%fused_computation.30 | convolution fusion | flops 2433613824 | bytes 20971520 | tf_op jit(solution)/shard_map/dot_general | solution.py:27
  269.6 4.7 fusion.142
  281.7 3.4 fusion.64
  285.1 3.2 fusion.62
  291.5 5.9 convolution_convert_fusion.4
  297.5 4.6 convolution_convert_fusion.2
  304.3 3.4 fusion.71
  307.7 4.5 fusion.69
  323.5 3.2 convolution_convert_fusion.5
  328.3 3.2 convolution_convert_fusion.3
  332.1 15.5 %collective-permute-done.38 = bf16[1024,512]{1,0:T(8,128)(2,1)S(1)} collective-permute-done((bf16[1024,512]{1,0:T(8,128)(2,1)S(1)}, bf16[1024,512]{1,0:T(8,128)(2,1)S(1)}, u32[]{:S(2)}, u32[]{:S(2)}) %collective-permute-start.38) | collective-permute-done | bytes 1048608 | tf_op jit(solution)/shard_map/ppermute | solution.py:13
  349.1 19.2 %collective-permute-done.43 = bf16[512,1024]{1,0:T(8,128)(2,1)S(1)} collective-permute-done((bf16[512,1024]{1,0:T(8,128)(2,1)S(1)}, bf16[512,1024]{1,0:T(8,128)(2,1)S(1)}, u32[]{:S(2)}, u32[]{:S(2)}) %collective-permute-start.43) | collective-permute-done | bytes 1048608 | tf_op jit(solution)/shard_map/ppermute | solution.py:13
  383.3 3.2 convolution_convert_fusion.7
  400.6 4.6 add_convert_fusion
  408.2 10.4 %collective-permute-done.45 = bf16[1024,512]{1,0:T(8,128)(2,1)S(1)} collective-permute-done((bf16[1024,512]{1,0:T(8,128)(2,1)S(1)}, bf16[1024,512]{1,0:T(8,128)(2,1)S(1)}, u32[]{:S(2)}, u32[]{:S(2)}) %collective-permute-start.45) | collective-permute-done | bytes 1048608 | tf_op jit(solution)/shard_map/ppermute | solution.py:13
  423.8 84.0 %psum.7 = f32[5,1024]{1,0:T(8,128)} all-reduce(f32[5,1024]{1,0:T(8,128)} %pad_maximum_fusion.8), channel_id=1, replica_groups=mesh['dp'=2,'tok'=4,'y'=2,'c'=2] {'dp','tok','y','c'}, use_global_device_ids=true, to_apply=%region_16.17 | all-reduce | flops 5120 | bytes 40960 | tf_op jit(solution)/shard_map/psum | solution.py:300
  522.4 4.3 collective-permute-start.57
  526.8 21.1 %collective-permute-done.66 = bf16[128,1152]{1,0:T(8,128)(2,1)S(1)} collective-permute-done((bf16[128,1152]{1,0:T(8,128)(2,1)S(1)}, bf16[128,1152]{1,0:T(8,128)(2,1)S(1)}, u32[]{:S(2)}, u32[]{:S(2)}) %collective-permute-start.66) | collective-permute-done | bytes 294944 | tf_op jit(solution)/shard_map/ppermute | solution.py:23
  555.7 4.5 collective-permute-start.61
  560.3 16.3 %collective-permute-done.56 = bf16[128,1152]{1,0:T(8,128)(2,1)} collective-permute-done((bf16[128,1152]{1,0:T(8,128)(2,1)}, bf16[128,1152]{1,0:T(8,128)(2,1)}, u32[]{:S(2)}, u32[]{:S(2)}) %collective-permute-start.56) | collective-permute-done | bytes 294944 | tf_op jit(solution)/shard_map/ppermute | solution.py:23
  581.0 9.2 %collective-permute-done.61 = bf16[128,1152]{1,0:T(8,128)(2,1)S(1)} collective-permute-done((bf16[128,1152]{1,0:T(8,128)(2,1)S(1)}, bf16[128,1152]{1,0:T(8,128)(2,1)S(1)}, u32[]{:S(2)}, u32[]{:S(2)}) %collective-permute-start.61) | collective-permute-done | bytes 294944 | tf_op jit(solution)/shard_map/ppermute | solution.py:23
  592.1 3.8 collective-permute-start.52
  595.9 9.3 %collective-permute-start.51 = (bf16[128,1024]{0,1:T(8,128)(2,1)S(1)}, bf16[128,1024]{0,1:T(8,128)(2,1)S(1)}, u32[]{:S(2)}, u32[]{:S(2)}) collective-permute-start(bf16[128,1024]{0,1:T(8,128)(2,1)S(1)} %get-tuple-element.107), channel_id=1, source_target_pairs={{0,8},{4,12},{8,0},{12,4},{1,9},{5,13},{9,1},{13,5},{2,10},{6,14},... | collective-permute-start | bytes 786440 | tf_op jit(solution)/shard_map/ppermute | solution.py:23
  607.2 3.2 maximum_select_fusion.1
  610.4 15.7 %collective-permute-done.51 = bf16[128,1024]{0,1:T(8,128)(2,1)S(1)} collective-permute-done((bf16[128,1024]{0,1:T(8,128)(2,1)S(1)}, bf16[128,1024]{0,1:T(8,128)(2,1)S(1)}, u32[]{:S(2)}, u32[]{:S(2)}) %collective-permute-start.51) | collective-permute-done | bytes 262176 | tf_op jit(solution)/shard_map/ppermute | solution.py:23
  (396 shorter events, 192.6 us)
Async XLA Ops:
  3.5 16.1 %collective-permute-start.4 = (bf16[128,1024]{0,1:T(8,128)(2,1)}, bf16[128,1024]{0,1:T(8,128)(2,1)}, u32[]{:S(2)}, u32[]{:S(2)}) collective-permute-start(bf16[128,1024]{0,1:T(8,128)(2,1)} %get-tuple-element.115), channel_id=1, source_target_pairs={{0,4},{4,8},{8,12},{12,0},{1,5},{5,9},{9,13},{13,1},{2,6},{6,10},{... | collective-permute-start | bytes 786440 | tf_op jit(solution)/shard_map/ppermute | solution.py:18
  6.6 13.7 %collective-permute-start.2 = (bf16[128,1024]{0,1:T(8,128)(2,1)}, bf16[128,1024]{0,1:T(8,128)(2,1)}, u32[]{:S(2)}, u32[]{:S(2)}) collective-permute-start(bf16[128,1024]{0,1:T(8,128)(2,1)} %get-tuple-element.115), channel_id=1, source_target_pairs={{0,12},{4,0},{8,4},{12,8},{1,13},{5,1},{9,5},{13,9},{2,14},{6,2},{... | collective-permute-start | bytes 786440 | tf_op jit(solution)/shard_map/ppermute | solution.py:18
  8.6 23.5 %collective-permute-start.3 = (bf16[128,1024]{0,1:T(8,128)(2,1)}, bf16[128,1024]{0,1:T(8,128)(2,1)}, u32[]{:S(2)}, u32[]{:S(2)}) collective-permute-start(bf16[128,1024]{0,1:T(8,128)(2,1)} %get-tuple-element.115), channel_id=1, source_target_pairs={{0,8},{4,12},{8,0},{12,4},{1,9},{5,13},{9,1},{13,5},{2,10},{6,14},... | collective-permute-start | bytes 786440 | tf_op jit(solution)/shard_map/ppermute | solution.py:18
  9.6 27.3 %collective-permute-start.5 = (bf16[128,1024]{0,1:T(8,128)(2,1)}, bf16[128,1024]{0,1:T(8,128)(2,1)}, u32[]{:S(2)}, u32[]{:S(2)}) collective-permute-start(bf16[128,1024]{0,1:T(8,128)(2,1)} %get-tuple-element.115), channel_id=1, source_target_pairs={{0,16},{16,0},{1,17},{17,1},{2,18},{18,2},{3,19},{19,3},{4,20},{20... | collective-permute-start | bytes 786440 | tf_op jit(solution)/shard_map/ppermute | solution.py:18
  19.1 32.7 %collective-permute-start = (bf16[1024,256]{1,0:T(8,128)(2,1)S(1)}, bf16[1024,256]{1,0:T(8,128)(2,1)S(1)}, u32[]{:S(2)}, u32[]{:S(2)}) collective-permute-start(bf16[1024,256]{1,0:T(8,128)(2,1)S(1)} %get-tuple-element.113), channel_id=1, source_target_pairs={{0,1},{1,0},{2,3},{3,2},{4,5},{5,4},{6,7},{7,6},{8,9},{9,8},{10,11... | collective-permute-start | bytes 1572872 | tf_op jit(solution)/shard_map/ppermute | solution.py:13
  19.7 33.8 %collective-permute-start.40 = (bf16[1024,256]{1,0:T(8,128)(2,1)S(1)}, bf16[1024,256]{1,0:T(8,128)(2,1)S(1)}, u32[]{:S(2)}, u32[]{:S(2)}) collective-permute-start(bf16[1024,256]{1,0:T(8,128)(2,1)S(1)} %get-tuple-element.109), channel_id=1, source_target_pairs={{0,1},{1,0},{2,3},{3,2},{4,5},{5,4},{6,7},{7,6},{8,9},{9,8},{10,11... | collective-permute-start | bytes 1572872 | tf_op jit(solution)/shard_map/ppermute | solution.py:13
  20.3 18.9 %collective-permute-start.6 = (bf16[128,1024]{0,1:T(8,128)(2,1)}, bf16[128,1024]{0,1:T(8,128)(2,1)S(1)}, u32[]{:S(2)}, u32[]{:S(2)}) collective-permute-start(bf16[128,1024]{0,1:T(8,128)(2,1)} %collective-permute-done.2), channel_id=1, source_target_pairs={{0,16},{16,0},{1,17},{17,1},{2,18},{18,2},{3,19},{19,3},{4,20},{20... | collective-permute-start | bytes 786440 | tf_op jit(solution)/shard_map/ppermute | solution.py:18
  39.1 21.8 %collective-permute-start.14 = (bf16[128,1152]{1,0:T(8,128)(2,1)S(1)}, bf16[128,1152]{1,0:T(8,128)(2,1)S(1)}, u32[]{:S(2)}, u32[]{:S(2)}) collective-permute-start(bf16[128,1152]{1,0:T(8,128)(2,1)S(1)} %copy-done.30), channel_id=1, source_target_pairs={{0,12},{4,0},{8,4},{12,8},{1,13},{5,1},{9,5},{13,9},{2,14},{6,2},{... | collective-permute-start | bytes 884744 | tf_op jit(solution)/shard_map/ppermute | solution.py:18
  41.5 22.9 %collective-permute-start.15 = (bf16[128,1152]{1,0:T(8,128)(2,1)S(1)}, bf16[128,1152]{1,0:T(8,128)(2,1)S(1)}, u32[]{:S(2)}, u32[]{:S(2)}) collective-permute-start(bf16[128,1152]{1,0:T(8,128)(2,1)S(1)} %copy-done.30), channel_id=1, source_target_pairs={{0,8},{4,12},{8,0},{12,4},{1,9},{5,13},{9,1},{13,5},{2,10},{6,14},... | collective-permute-start | bytes 884744 | tf_op jit(solution)/shard_map/ppermute | solution.py:18
  51.8 16.5 %collective-permute-start.17 = (bf16[128,1152]{1,0:T(8,128)(2,1)S(1)}, bf16[128,1152]{1,0:T(8,128)(2,1)S(1)}, u32[]{:S(2)}, u32[]{:S(2)}) collective-permute-start(bf16[128,1152]{1,0:T(8,128)(2,1)S(1)} %copy-done.30), channel_id=1, source_target_pairs={{0,16},{16,0},{1,17},{17,1},{2,18},{18,2},{3,19},{19,3},{4,20},{20... | collective-permute-start | bytes 884744 | tf_op jit(solution)/shard_map/ppermute | solution.py:18
  53.5 107.9 %collective-permute-start.9 = (bf16[1024,1024]{0,1:T(8,128)(2,1)S(1)}, bf16[1024,1024]{0,1:T(8,128)(2,1)S(1)}, u32[]{:S(2)}, u32[]{:S(2)}) collective-permute-start(bf16[1024,1024]{0,1:T(8,128)(2,1)S(1)} %copy-done.20), channel_id=1, source_target_pairs={{0,1},{1,0},{2,3},{3,2},{4,5},{5,4},{6,7},{7,6},{8,9},{9,8},{10,11... | collective-permute-start | bytes 6291464 | tf_op jit(solution)/shard_map/ppermute | solution.py:13
  59.4 95.9 %collective-permute-start.1 = (bf16[1024,512]{1,0:T(8,128)(2,1)S(1)}, bf16[1024,512]{1,0:T(8,128)(2,1)S(1)}, u32[]{:S(2)}, u32[]{:S(2)}) collective-permute-start(bf16[1024,512]{1,0:T(8,128)(2,1)S(1)} %pad_maximum_fusion.5), channel_id=1, source_target_pairs={{0,2},{2,0},{1,3},{3,1},{4,6},{6,4},{5,7},{7,5},{8,10},{10,8},{9,1... | collective-permute-start | bytes 3145736 | tf_op jit(solution)/shard_map/ppermute | solution.py:13
  60.9 139.5 %collective-permute-start.41 = (bf16[1024,512]{1,0:T(8,128)(2,1)S(1)}, bf16[1024,512]{1,0:T(8,128)(2,1)S(1)}, u32[]{:S(2)}, u32[]{:S(2)}) collective-permute-start(bf16[1024,512]{1,0:T(8,128)(2,1)S(1)} %pad_maximum_fusion.6), channel_id=1, source_target_pairs={{0,2},{2,0},{1,3},{3,1},{4,6},{6,4},{5,7},{7,5},{8,10},{10,8},{9,1... | collective-permute-start | bytes 3145736 | tf_op jit(solution)/shard_map/ppermute | solution.py:13
  68.4 20.6 %collective-permute-start.21 = (bf16[128,1152]{1,0:T(8,128)(2,1)S(1)}, bf16[128,1152]{1,0:T(8,128)(2,1)S(1)}, u32[]{:S(2)}, u32[]{:S(2)}) collective-permute-start(bf16[128,1152]{1,0:T(8,128)(2,1)S(1)} %copy-done.31), channel_id=1, source_target_pairs={{0,12},{4,0},{8,4},{12,8},{1,13},{5,1},{9,5},{13,9},{2,14},{6,2},{... | collective-permute-start | bytes 884744 | tf_op jit(solution)/shard_map/ppermute | solution.py:18
  75.8 21.0 %collective-permute-start.22 = (bf16[128,1152]{1,0:T(8,128)(2,1)S(1)}, bf16[128,1152]{1,0:T(8,128)(2,1)S(1)}, u32[]{:S(2)}, u32[]{:S(2)}) collective-permute-start(bf16[128,1152]{1,0:T(8,128)(2,1)S(1)} %copy-done.31), channel_id=1, source_target_pairs={{0,8},{4,12},{8,0},{12,4},{1,9},{5,13},{9,1},{13,5},{2,10},{6,14},... | collective-permute-start | bytes 884744 | tf_op jit(solution)/shard_map/ppermute | solution.py:18
  99.0 14.0 %collective-permute-start.20 = (bf16[128,1152]{1,0:T(8,128)(2,1)S(1)}, bf16[128,1152]{1,0:T(8,128)(2,1)S(1)}, u32[]{:S(2)}, u32[]{:S(2)}) collective-permute-start(bf16[128,1152]{1,0:T(8,128)(2,1)S(1)} %collective-permute-done.16), channel_id=1, source_target_pairs={{0,16},{16,0},{1,17},{17,1},{2,18},{18,2},{3,19},{19,3},{4,20},{20... | collective-permute-start | bytes 884744 | tf_op jit(solution)/shard_map/ppermute | solution.py:18
  131.0 17.4 %collective-permute-start.29 = (bf16[128,1152]{0,1:T(8,128)(2,1)S(1)}, bf16[128,1152]{0,1:T(8,128)(2,1)S(1)}, u32[]{:S(2)}, u32[]{:S(2)}) collective-permute-start(bf16[128,1152]{0,1:T(8,128)(2,1)S(1)} %bitcast.69), channel_id=1, source_target_pairs={{0,8},{4,12},{8,0},{12,4},{1,9},{5,13},{9,1},{13,5},{2,10},{6,14},... | collective-permute-start | bytes 884744 | tf_op jit(solution)/shard_map/ppermute | solution.py:18
  135.5 14.5 %collective-permute-start.30 = (bf16[128,1152]{0,1:T(8,128)(2,1)S(1)}, bf16[128,1152]{0,1:T(8,128)(2,1)S(1)}, u32[]{:S(2)}, u32[]{:S(2)}) collective-permute-start(bf16[128,1152]{0,1:T(8,128)(2,1)S(1)} %bitcast.70), channel_id=1, source_target_pairs={{0,4},{4,8},{8,12},{12,0},{1,5},{5,9},{9,13},{13,1},{2,6},{6,10},{... | collective-permute-start | bytes 884744 | tf_op jit(solution)/shard_map/ppermute | solution.py:18
  150.0 56.2 %collective-permute-start.35 = (bf16[1024,1152]{1,0:T(8,128)(2,1)S(1)}, bf16[1024,1152]{1,0:T(8,128)(2,1)}, u32[]{:S(2)}, u32[]{:S(2)}) collective-permute-start(bf16[1024,1152]{1,0:T(8,128)(2,1)S(1)} %constant_dynamic-update-slice_fusion.8), channel_id=1, source_target_pairs={{0,1},{1,0},{2,3},{3,2},{4,5},{5,4},{6,7},{7,6},{8,9},{9,8},{10,11... | collective-permute-start | bytes 7077896 | tf_op jit(solution)/shard_map/ppermute | solution.py:13
  155.2 72.9 %collective-permute-start.36 = (bf16[1024,1152]{1,0:T(8,128)(2,1)S(1)}, bf16[1024,1152]{1,0:T(8,128)(2,1)}, u32[]{:S(2)}, u32[]{:S(2)}) collective-permute-start(bf16[1024,1152]{1,0:T(8,128)(2,1)S(1)} %constant_dynamic-update-slice_fusion.16), channel_id=1, source_target_pairs={{0,1},{1,0},{2,3},{3,2},{4,5},{5,4},{6,7},{7,6},{8,9},{9,8},{10,11... | collective-permute-start | bytes 7077896 | tf_op jit(solution)/shard_map/ppermute | solution.py:13
  172.7 25.2 %collective-permute-start.12 = (bf16[512,1024]{1,0:T(8,128)(2,1)S(1)}, bf16[512,1024]{1,0:T(8,128)(2,1)S(1)}, u32[]{:S(2)}, u32[]{:S(2)}) collective-permute-start(bf16[512,1024]{1,0:T(8,128)(2,1)S(1)} %add_convert_fusion.11), channel_id=1, source_target_pairs={{0,2},{2,0},{1,3},{3,1},{4,6},{6,4},{5,7},{7,5},{8,10},{10,8},{9,1... | collective-permute-start | bytes 3145736 | tf_op jit(solution)/shard_map/ppermute | solution.py:13
  177.5 58.0 %collective-permute-start.37 = (bf16[1024,1152]{0,1:T(8,128)(2,1)S(1)}, bf16[1024,1152]{0,1:T(8,128)(2,1)}, u32[]{:S(2)}, u32[]{:S(2)}) collective-permute-start(bf16[1024,1152]{0,1:T(8,128)(2,1)S(1)} %constant_dynamic-update-slice_fusion.24), channel_id=1, source_target_pairs={{0,1},{1,0},{2,3},{3,2},{4,5},{5,4},{6,7},{7,6},{8,9},{9,8},{10,11... | collective-permute-start | bytes 7077896 | tf_op jit(solution)/shard_map/ppermute | solution.py:13
  198.8 24.3 %collective-permute-start.13 = (bf16[512,1024]{1,0:T(8,128)(2,1)S(1)}, bf16[512,1024]{1,0:T(8,128)(2,1)S(1)}, u32[]{:S(2)}, u32[]{:S(2)}) collective-permute-start(bf16[512,1024]{1,0:T(8,128)(2,1)S(1)} %multiply_convert_fusion.6), channel_id=1, source_target_pairs={{0,2},{2,0},{1,3},{3,1},{4,6},{6,4},{5,7},{7,5},{8,10},{10,8},{9,1... | collective-permute-start | bytes 3145736 | tf_op jit(solution)/shard_map/ppermute | solution.py:13
  289.9 23.5 %collective-permute-start.42 = (bf16[512,1024]{1,0:T(8,128)(2,1)S(1)}, bf16[512,1024]{1,0:T(8,128)(2,1)}, u32[]{:S(2)}, u32[]{:S(2)}) collective-permute-start(bf16[512,1024]{1,0:T(8,128)(2,1)S(1)} %add_convert_fusion.10), channel_id=1, source_target_pairs={{0,2},{2,0},{1,3},{3,1},{4,6},{6,4},{5,7},{7,5},{8,10},{10,8},{9,1... | collective-permute-start | bytes 3145736 | tf_op jit(solution)/shard_map/ppermute | solution.py:13
  297.5 96.8 %collective-permute-start.53 = (bf16[1024,1152]{1,0:T(8,128)(2,1)}, bf16[1024,1152]{1,0:T(8,128)(2,1)S(1)}, u32[]{:S(2)}, u32[]{:S(2)}) collective-permute-start(bf16[1024,1152]{1,0:T(8,128)(2,1)} %convolution_convert_fusion.4), channel_id=1, source_target_pairs={{0,1},{1,0},{2,3},{3,2},{4,5},{5,4},{6,7},{7,6},{8,9},{9,8},{10,11... | collective-permute-start | bytes 7077896 | tf_op jit(solution)/shard_map/ppermute | solution.py:13
  302.1 94.6 %collective-permute-start.58 = (bf16[1024,1152]{1,0:T(8,128)(2,1)}, bf16[1024,1152]{1,0:T(8,128)(2,1)S(1)}, u32[]{:S(2)}, u32[]{:S(2)}) collective-permute-start(bf16[1024,1152]{1,0:T(8,128)(2,1)} %convolution_convert_fusion.2), channel_id=1, source_target_pairs={{0,1},{1,0},{2,3},{3,2},{4,5},{5,4},{6,7},{7,6},{8,9},{9,8},{10,11... | collective-permute-start | bytes 7077896 | tf_op jit(solution)/shard_map/ppermute | solution.py:13
  302.7 96.4 %collective-permute-start.63 = (bf16[1024,1152]{1,0:T(8,128)(2,1)}, bf16[1024,1152]{1,0:T(8,128)(2,1)}, u32[]{:S(2)}, u32[]{:S(2)}) collective-permute-start(bf16[1024,1152]{1,0:T(8,128)(2,1)} %convolution_convert_fusion), channel_id=1, source_target_pairs={{0,1},{1,0},{2,3},{3,2},{4,5},{5,4},{6,7},{7,6},{8,9},{9,8},{10,11... | collective-permute-start | bytes 7077896 | tf_op jit(solution)/shard_map/ppermute | solution.py:13
  321.5 26.2 %collective-permute-start.38 = (bf16[1024,512]{1,0:T(8,128)(2,1)S(1)}, bf16[1024,512]{1,0:T(8,128)(2,1)S(1)}, u32[]{:S(2)}, u32[]{:S(2)}) collective-permute-start(bf16[1024,512]{1,0:T(8,128)(2,1)S(1)} %get-tuple-element.93), channel_id=1, source_target_pairs={{0,2},{2,0},{1,3},{3,1},{4,6},{6,4},{5,7},{7,5},{8,10},{10,8},{9,1... | collective-permute-start | bytes 3145736 | tf_op jit(solution)/shard_map/ppermute | solution.py:13
  326.7 41.6 %collective-permute-start.43 = (bf16[512,1024]{1,0:T(8,128)(2,1)S(1)}, bf16[512,1024]{1,0:T(8,128)(2,1)S(1)}, u32[]{:S(2)}, u32[]{:S(2)}) collective-permute-start(bf16[512,1024]{1,0:T(8,128)(2,1)S(1)} %get-tuple-element.88), channel_id=1, source_target_pairs={{0,2},{2,0},{1,3},{3,1},{4,6},{6,4},{5,7},{7,5},{8,10},{10,8},{9,1... | collective-permute-start | bytes 3145736 | tf_op jit(solution)/shard_map/ppermute | solution.py:13
  349.0 57.4 %collective-permute-start.39 = (bf16[1024,256]{1,0:T(8,128)(2,1)S(1)}, bf16[1024,256]{1,0:T(8,128)(2,1)S(1)}, u32[]{:S(2)}, u32[]{:S(2)}) collective-permute-start(bf16[1024,256]{1,0:T(8,128)(2,1)S(1)} %get-tuple-element.111), channel_id=1, source_target_pairs={{0,1},{1,0},{2,3},{3,2},{4,5},{5,4},{6,7},{7,6},{8,9},{9,8},{10,11... | collective-permute-start | bytes 1572872 | tf_op jit(solution)/shard_map/ppermute | solution.py:13
  393.3 25.4 %collective-permute-start.45 = (bf16[1024,512]{1,0:T(8,128)(2,1)S(1)}, bf16[1024,512]{1,0:T(8,128)(2,1)S(1)}, u32[]{:S(2)}, u32[]{:S(2)}) collective-permute-start(bf16[1024,512]{1,0:T(8,128)(2,1)S(1)} %add_convert_fusion.8), channel_id=1, source_target_pairs={{0,2},{2,0},{1,3},{3,1},{4,6},{6,4},{5,7},{7,5},{8,10},{10,8},{9,1... | collective-permute-start | bytes 3145736 | tf_op jit(solution)/shard_map/ppermute | solution.py:13
  394.3 157.4 %collective-permute-start.48 = (bf16[1024,1024]{0,1:T(8,128)(2,1)}, bf16[1024,1024]{0,1:T(8,128)(2,1)}, u32[]{:S(2)}, u32[]{:S(2)}) collective-permute-start(bf16[1024,1024]{0,1:T(8,128)(2,1)} %pad_maximum_fusion.2), channel_id=1, source_target_pairs={{0,1},{1,0},{2,3},{3,2},{4,5},{5,4},{6,7},{7,6},{8,9},{9,8},{10,11... | collective-permute-start | bytes 6291464 | tf_op jit(solution)/shard_map/ppermute | solution.py:13
  396.7 118.2 %collective-permute-start.54 = (bf16[512,1152]{1,0:T(8,128)(2,1)}, bf16[512,1152]{1,0:T(8,128)(2,1)}, u32[]{:S(2)}, u32[]{:S(2)}) collective-permute-start(bf16[512,1152]{1,0:T(8,128)(2,1)} %slice.458), channel_id=1, source_target_pairs={{0,16},{16,0},{1,17},{17,1},{2,18},{18,2},{3,19},{19,3},{4,20},{20... | collective-permute-start | bytes 3538952 | tf_op jit(solution)/shard_map/ppermute | solution.py:23
  399.1 118.5 %collective-permute-start.59 = (bf16[512,1152]{1,0:T(8,128)(2,1)}, bf16[512,1152]{1,0:T(8,128)(2,1)S(1)}, u32[]{:S(2)}, u32[]{:S(2)}) collective-permute-start(bf16[512,1152]{1,0:T(8,128)(2,1)} %slice.464), channel_id=1, source_target_pairs={{0,16},{16,0},{1,17},{17,1},{2,18},{18,2},{3,19},{19,3},{4,20},{20... | collective-permute-start | bytes 3538952 | tf_op jit(solution)/shard_map/ppermute | solution.py:23
  406.4 104.1 %collective-permute-start.64 = (bf16[512,1152]{1,0:T(8,128)(2,1)}, bf16[512,1152]{1,0:T(8,128)(2,1)}, u32[]{:S(2)}, u32[]{:S(2)}) collective-permute-start(bf16[512,1152]{1,0:T(8,128)(2,1)} %slice.470), channel_id=1, source_target_pairs={{0,16},{16,0},{1,17},{17,1},{2,18},{18,2},{3,19},{19,3},{4,20},{20... | collective-permute-start | bytes 3538952 | tf_op jit(solution)/shard_map/ppermute | solution.py:23
  423.1 184.1 %collective-permute-start.47 = (f32[1024,256]{1,0:T(8,128)}, f32[1024,256]{1,0:T(8,128)}, u32[]{:S(2)}, u32[]{:S(2)}) collective-permute-start(f32[1024,256]{1,0:T(8,128)} %get-tuple-element.87), channel_id=1, source_target_pairs={{0,1},{1,0},{2,3},{3,2},{4,5},{5,4},{6,7},{7,6},{8,9},{9,8},{10,11... | collective-permute-start | bytes 3145736 | tf_op jit(solution)/shard_map/ppermute | solution.py:13
  515.0 32.9 %collective-permute-start.66 = (bf16[128,1152]{1,0:T(8,128)(2,1)S(1)}, bf16[128,1152]{1,0:T(8,128)(2,1)S(1)}, u32[]{:S(2)}, u32[]{:S(2)}) collective-permute-start(bf16[128,1152]{1,0:T(8,128)(2,1)S(1)} %get-tuple-element.96), channel_id=1, source_target_pairs={{0,8},{4,12},{8,0},{12,4},{1,9},{5,13},{9,1},{13,5},{2,10},{6,14},... | collective-permute-start | bytes 884744 | tf_op jit(solution)/shard_map/ppermute | solution.py:23
  518.7 29.3 %collective-permute-start.65 = (bf16[128,1152]{1,0:T(8,128)(2,1)S(1)}, bf16[128,1152]{1,0:T(8,128)(2,1)S(1)}, u32[]{:S(2)}, u32[]{:S(2)}) collective-permute-start(bf16[128,1152]{1,0:T(8,128)(2,1)S(1)} %get-tuple-element.94), channel_id=1, source_target_pairs={{0,4},{4,8},{8,12},{12,0},{1,5},{5,9},{9,13},{13,1},{2,6},{6,10},{... | collective-permute-start | bytes 884744 | tf_op jit(solution)/shard_map/ppermute | solution.py:23
  522.4 33.3 %collective-permute-start.57 = (bf16[128,1152]{1,0:T(8,128)(2,1)}, bf16[128,1152]{1,0:T(8,128)(2,1)}, u32[]{:S(2)}, u32[]{:S(2)}) collective-permute-start(bf16[128,1152]{1,0:T(8,128)(2,1)} %get-tuple-element.101), channel_id=1, source_target_pairs={{0,12},{4,0},{8,4},{12,8},{1,13},{5,1},{9,5},{13,9},{2,14},{6,2},{... | collective-permute-start | bytes 884744 | tf_op jit(solution)/shard_map/ppermute | solution.py:23
  547.9 28.6 %collective-permute-start.56 = (bf16[128,1152]{1,0:T(8,128)(2,1)}, bf16[128,1152]{1,0:T(8,128)(2,1)}, u32[]{:S(2)}, u32[]{:S(2)}) collective-permute-start(bf16[128,1152]{1,0:T(8,128)(2,1)} %get-tuple-element.102), channel_id=1, source_target_pairs={{0,8},{4,12},{8,0},{12,4},{1,9},{5,13},{9,1},{13,5},{2,10},{6,14},... | collective-permute-start | bytes 884744 | tf_op jit(solution)/shard_map/ppermute | solution.py:23
  547.9 28.6 %collective-permute-start.55 = (bf16[128,1152]{1,0:T(8,128)(2,1)}, bf16[128,1152]{1,0:T(8,128)(2,1)}, u32[]{:S(2)}, u32[]{:S(2)}) collective-permute-start(bf16[128,1152]{1,0:T(8,128)(2,1)} %get-tuple-element.100), channel_id=1, source_target_pairs={{0,4},{4,8},{8,12},{12,0},{1,5},{5,9},{9,13},{13,1},{2,6},{6,10},{... | collective-permute-start | bytes 884744 | tf_op jit(solution)/shard_map/ppermute | solution.py:23
  551.7 29.3 %collective-permute-start.62 = (bf16[128,1152]{1,0:T(8,128)(2,1)}, bf16[128,1152]{1,0:T(8,128)(2,1)S(1)}, u32[]{:S(2)}, u32[]{:S(2)}) collective-permute-start(bf16[128,1152]{1,0:T(8,128)(2,1)} %get-tuple-element.98), channel_id=1, source_target_pairs={{0,12},{4,0},{8,4},{12,8},{1,13},{5,1},{9,5},{13,9},{2,14},{6,2},{... | collective-permute-start | bytes 884744 | tf_op jit(solution)/shard_map/ppermute | solution.py:23
  555.7 34.5 %collective-permute-start.61 = (bf16[128,1152]{1,0:T(8,128)(2,1)S(1)}, bf16[128,1152]{1,0:T(8,128)(2,1)S(1)}, u32[]{:S(2)}, u32[]{:S(2)}) collective-permute-start(bf16[128,1152]{1,0:T(8,128)(2,1)S(1)} %copy-done.29), channel_id=1, source_target_pairs={{0,8},{4,12},{8,0},{12,4},{1,9},{5,13},{9,1},{13,5},{2,10},{6,14},... | collective-permute-start | bytes 884744 | tf_op jit(solution)/shard_map/ppermute | solution.py:23
  576.5 13.7 %collective-permute-start.60 = (bf16[128,1152]{1,0:T(8,128)(2,1)S(1)}, bf16[128,1152]{1,0:T(8,128)(2,1)S(1)}, u32[]{:S(2)}, u32[]{:S(2)}) collective-permute-start(bf16[128,1152]{1,0:T(8,128)(2,1)S(1)} %copy-done.28), channel_id=1, source_target_pairs={{0,4},{4,8},{8,12},{12,0},{1,5},{5,9},{9,13},{13,1},{2,6},{6,10},{... | collective-permute-start | bytes 884744 | tf_op jit(solution)/shard_map/ppermute | solution.py:23
  576.5 15.1 %collective-permute-start.49 = (bf16[512,1024]{0,1:T(8,128)(2,1)S(1)}, bf16[512,1024]{0,1:T(8,128)(2,1)S(1)}, u32[]{:S(2)}, u32[]{:S(2)}) collective-permute-start(bf16[512,1024]{0,1:T(8,128)(2,1)S(1)} %slice.448), channel_id=1, source_target_pairs={{0,16},{16,0},{1,17},{17,1},{2,18},{18,2},{3,19},{19,3},{4,20},{20... | collective-permute-start | bytes 3145736 | tf_op jit(solution)/shard_map/ppermute | solution.py:23
  592.1 18.2 %collective-permute-start.52 = (bf16[128,1024]{0,1:T(8,128)(2,1)S(1)}, bf16[128,1024]{0,1:T(8,128)(2,1)S(1)}, u32[]{:S(2)}, u32[]{:S(2)}) collective-permute-start(bf16[128,1024]{0,1:T(8,128)(2,1)S(1)} %get-tuple-element.106), channel_id=1, source_target_pairs={{0,12},{4,0},{8,4},{12,8},{1,13},{5,1},{9,5},{13,9},{2,14},{6,2},{... | collective-permute-start | bytes 786440 | tf_op jit(solution)/shard_map/ppermute | solution.py:23
  595.9 30.2 %collective-permute-start.51 = (bf16[128,1024]{0,1:T(8,128)(2,1)S(1)}, bf16[128,1024]{0,1:T(8,128)(2,1)S(1)}, u32[]{:S(2)}, u32[]{:S(2)}) collective-permute-start(bf16[128,1024]{0,1:T(8,128)(2,1)S(1)} %get-tuple-element.107), channel_id=1, source_target_pairs={{0,8},{4,12},{8,0},{12,4},{1,9},{5,13},{9,1},{13,5},{2,10},{6,14},... | collective-permute-start | bytes 786440 | tf_op jit(solution)/shard_map/ppermute | solution.py:23
  605.3 20.9 %collective-permute-start.50 = (bf16[128,1024]{0,1:T(8,128)(2,1)S(1)}, bf16[128,1024]{0,1:T(8,128)(2,1)S(1)}, u32[]{:S(2)}, u32[]{:S(2)}) collective-permute-start(bf16[128,1024]{0,1:T(8,128)(2,1)S(1)} %get-tuple-element.105), channel_id=1, source_target_pairs={{0,4},{4,8},{8,12},{12,0},{1,5},{5,9},{9,13},{13,1},{2,6},{6,10},{... | collective-permute-start | bytes 786440 | tf_op jit(solution)/shard_map/ppermute | solution.py:23
  (91 other events, 1886.8 us)

commit v2 on v1

v2 whole, which is shorter than its diff:
```python
import functools

import jax
import jax.numpy as jnp
from jax import lax
from jax.experimental import pallas as pl
from jax.experimental.layout import Layout, with_layout_constraint
from jax.experimental.pallas import tpu as pltpu
from jax.sharding import Mesh
from jax.sharding import PartitionSpec as P

EPS = 1e-05
F32 = jnp.float32
BF16 = jnp.bfloat16
VMEM_LIMIT = 56 * 2**20


def swap(value, axis):
    return lax.ppermute(value, axis, [(0, 1), (1, 0)])


def deliver(value, axis, distance):
    size = lax.axis_size(axis)
    return lax.ppermute(value, axis, [(s, (s + distance) % size) for s in range(size)])


def dot(left, right, contract):
    return lax.dot_general(left, right, (contract, ((), ())), preferred_element_type=F32)


def nn(left, right):
    return dot(left, right, ((1,), (0,)))


def nt(left, right):
    return dot(left, right, ((1,), (1,)))


def tn(left, right):
    return dot(left, right, ((0,), (0,)))


def total(values):
    result = values[0].astype(F32)
    for value in values[1:]:
        result = result + value.astype(F32)
    return result


def tie(*values):
    return lax.optimization_barrier(values)


def pick_rows(value, index, size):
    return lax.dynamic_slice_in_dim(value, index * size, size, 0)


def by_rank(index, first, second, axis=0):
    return jnp.where(
        index == 0,
        jnp.concatenate([first, second], axis),
        jnp.concatenate([second, first], axis),
    )


def for_dp(own, other):
    steps = lax.axis_size("dp")
    size = own.shape[0] // steps
    indices = [(lax.axis_index("dp") + i) % steps for i in range(1, steps)]
    return [
        total([pick_rows(part, index, size) for part in (own, other)]).astype(BF16)
        for index in indices
    ]


def to_dp(pieces):
    return [deliver(piece, "dp", i + 1) for i, piece in enumerate(pieces)]


def to_tok(mine):
    return lax.all_to_all(mine, "tok", split_axis=0, concat_axis=0, tiled=True)


def add_tok(got):
    steps = lax.axis_size("tok")
    size = got.shape[0] // steps
    return total([got[i * size : (i + 1) * size] for i in range(steps)])


def add_dp(own, other, arrived):
    size = arrived[0].shape[0]
    mine = [pick_rows(part, lax.axis_index("dp"), size) for part in (own, other)]
    return total(mine + list(arrived)).astype(BF16)


def sum_over(value, axis):
    size = lax.axis_size(axis)
    if size & (size - 1):
        return lax.psum(value, axis)
    step = 1
    while step < size:
        value = value + lax.ppermute(value, axis, [(s, s ^ step) for s in range(size)])
        step *= 2
    return value


def hidden_kernel(h_own, h_other, cot, w_gate, w_up, w_down, h, hidden, d_gate, d_up):
    features = h.shape[1]
    half = h_own.shape[0]

    @pl.when(pl.program_id(0) == 0)
    def _():
        h[:half, :] = h_own[...]
        h[half:, :] = h_other[...]

    def both(w):
        return jnp.concatenate([w[:, i].reshape(features, w.shape[3]) for i in (0, 1)], 1)

    w_gate, w_up, w_down = both(w_gate), both(w_up), both(w_down)
    width = w_gate.shape[1] // 2
    step = 256
    for start in range(0, h.shape[0], step):
        part = pl.ds(start, step)
        gate, up = nn(h[part, :], w_gate), nn(h[part, :], w_up)
        d_hidden = nn(cot[part, :], w_down)
        sigma = jax.nn.sigmoid(gate)
        silu = gate * sigma
        results = (
            (hidden, silu * up),
            (d_gate, d_hidden * up * sigma * (1.0 + gate * (1.0 - sigma))),
            (d_up, d_hidden * silu),
        )
        for ref, value in results:
            value = value.astype(BF16)
            ref[0, part, :] = value[:, :width]
            ref[1, part, :] = value[:, width:]


def hidden_units(h_own, h_other, cot, weights):
    rows, features = cot.shape
    blocks, _, chunk, width = weights.shape
    width //= 3
    tile = 128
    tiles = width // tile

    def of(matrix):
        return pl.BlockSpec((blocks, 2, chunk, tile), lambda j: (0, 0, 0, matrix * tiles + j))

    whole = pl.BlockSpec((rows, features), lambda j: (0, 0))
    half = pl.BlockSpec((rows // 2, features), lambda j: (0, 0))
    return pl.pallas_call(
        hidden_kernel,
        out_shape=[jax.ShapeDtypeStruct((rows, features), BF16)]
        + [jax.ShapeDtypeStruct((2, rows, width), BF16)] * 3,
        grid=(tiles,),
        in_specs=[half, half, whole, of(0), of(1), of(2)],
        out_specs=[whole] + [pl.BlockSpec((2, rows, tile), lambda j: (0, 0, j))] * 3,
        compiler_params=pltpu.CompilerParams(vmem_limit_bytes=VMEM_LIMIT),
        cost_estimate=pl.CostEstimate(
            flops=12 * rows * features * width,
            bytes_accessed=4 * (rows * features + 3 * features * width + 3 * rows * width),
            transcendentals=2 * rows * width,
        ),
        name="hidden_units",
    )(h_own, h_other, cot, weights, weights, weights)


def run_jobs(name, scalars, jobs):
    starts, steps = [], 0
    for job in jobs:
        starts.append(steps)
        steps += job[0]
    in_specs, out_specs, shapes, args, counts = [], [], [], [], []

    def spec(block, index, start, size):
        return pl.BlockSpec(block, lambda t, s: index(jnp.clip(t - start, 0, size - 1), s))

    for start, (size, inputs, outputs, _) in zip(starts, jobs):
        for array, block, index in inputs:
            in_specs.append(spec(block, index, start, size))
            args.append(array)
        for shape, dtype, block, index in outputs:
            out_specs.append(spec(block, index, start, size))
            shapes.append(jax.ShapeDtypeStruct(shape, dtype))
        counts.append((len(inputs), len(outputs)))

    def kernel(scalars_ref, *refs):
        ins, outs = list(refs[: len(in_specs)]), list(refs[len(in_specs) :])
        step = pl.program_id(0)
        for start, (size, _, _, work), (n_in, n_out) in zip(starts, jobs, counts):
            mine, ins = ins[:n_in], ins[n_in:]
            made, outs = outs[:n_out], outs[n_out:]
            if len(jobs) == 1:
                work(step, scalars_ref, mine, made)
            else:
                pl.when((step >= start) & (step < start + size))(
                    functools.partial(work, step - start, scalars_ref, mine, made)
                )

    return pl.pallas_call(
        kernel,
        out_shape=shapes,
        grid_spec=pltpu.PrefetchScalarGridSpec(
            num_scalar_prefetch=1, grid=(steps,), in_specs=in_specs, out_specs=out_specs
        ),
        compiler_params=pltpu.CompilerParams(vmem_limit_bytes=VMEM_LIMIT),
        name=name,
    )(scalars, *args)


def sum_through(parts, weights, width):
    result = 0.0
    for part, weight in zip(parts, weights):
        for i in (0, 1):
            result = result + nt(part[i], weight[:, i].reshape(width, weight.shape[3]))
    return result


def back_job(parts, weights, matrices, rows_of, dtype, divide=1, block_of=None):
    blocks, _, chunk, _ = weights.shape
    _, rows, width = parts[0].shape
    features = blocks * chunk // divide
    tile = max(256, chunk)
    steps = features // tile
    if rows_of is not None:
        rows //= 2

    def at(j, s):
        return j if block_of is None else block_of(s) * steps + j

    inputs = [
        (part, (2, rows, width), lambda j, s: (0, 0 if rows_of is None else rows_of(s), 0))
        for part in parts
    ] + [
        (weights, (tile // chunk, 2, chunk, width), lambda j, s, m=m: (at(j, s), 0, 0, m))
        for m in matrices
    ]
    count = len(parts)

    def work(j, s, ins, outs):
        outs[0][...] = sum_through(ins[:count], ins[count:], tile).astype(dtype)

    return steps, inputs, [((rows, features), dtype, (rows, tile), lambda j, s: (0, j))], work


def back_tile(d_proj, weights, tokens, inverse, dots, gain, features):
    made = sum_through([d_proj], [weights], gain.shape[1]) * gain[...]
    scale = inverse[...] * (dots[0] + dots[1]) / features
    return made - tokens[...].astype(F32) * scale


def back_in_job(d_proj, weights, full, inverse, dots, gain, block_of, dtype):
    blocks, _, chunk, _ = weights.shape
    _, rows, width = d_proj.shape
    features = blocks * chunk
    tile = max(256, chunk)
    steps = features // tile // 2

    def at(j, s):
        return block_of(s) * steps + j

    inputs = [
        (d_proj, (2, rows, width), lambda j, s: (0, 0, 0)),
        (weights, (tile // chunk, 2, chunk, width), lambda j, s: (at(j, s), 0, 0, 0)),
        (full, (rows, tile), lambda j, s: (0, at(j, s))),
        (inverse, (rows, 1), lambda j, s: (0, 0)),
        (dots, (2, rows, 1), lambda j, s: (0, 0, 0)),
        (gain, (1, tile), lambda j, s: (0, at(j, s))),
    ]

    def work(j, s, ins, outs):
        outs[0][...] = back_tile(*ins, features).astype(dtype)

    outputs = [((rows, features // 2), dtype, (rows, tile), lambda j, s: (0, j))]
    return steps, inputs, outputs, work


def made_job(hidden, weights, matrix, residual):
    blocks, _, chunk, _ = weights.shape
    _, rows, width = hidden.shape
    features = blocks * chunk
    tile = max(256, chunk)
    steps = features // tile
    part = steps // 2
    height = residual.shape[0]

    def at(j, s):
        return jnp.where(j < part, (1 - s[1]) * part + j, s[1] * part + j - part)

    inputs = [
        (hidden, (2, rows, width), lambda j, s: (0, 0, 0)),
        (weights, (tile // chunk, 2, chunk, width), lambda j, s: (at(j, s), 0, 0, matrix)),
        (residual, (height, tile), lambda j, s: (0, at(j, s))),
    ]
    outputs = [
        ((rows, features // 2), BF16, (rows, tile), lambda j, s: (0, jnp.minimum(j, part - 1))),
        ((rows, features // 2), F32, (rows, tile), lambda j, s: (0, jnp.maximum(j - part, 0))),
    ]

    def work(j, s, ins, outs):
        result = sum_through(ins[:1], ins[1:2], tile)
        for out, mine in zip(outs, (j < part, j >= part)):

            @pl.when(mine)
            def _(out=out):
                out[:height, :] = (result[:height] + ins[2][...]).astype(out.dtype)
                out[height:, :] = result[height:].astype(out.dtype)

    return steps, inputs, outputs, work


def pair_job(left, right):
    rows, features = left.shape
    width = right.shape[2]
    tile = 256
    inputs = [
        (left, (rows, tile), lambda j, s: (0, j)),
        (right, (2, rows, width), lambda j, s: (0, 0, 0)),
    ]
    outputs = [((features, width), BF16, (tile, width), lambda j, s: (j, 0))] * 2

    def work(j, s, ins, outs):
        for i, index in enumerate((s[0], 1 - s[0])):
            outs[i][...] = tn(ins[0][...], ins[1][index]).astype(BF16)

    return features // tile, inputs, outputs, work


def norm_job(full, gain):
    rows, features = full.shape
    tile = rows // 4

    def work(j, s, ins, outs):
        value = ins[0][...].astype(F32)
        inverse = lax.rsqrt(jnp.mean(value * value, -1, keepdims=True) + EPS)
        outs[0][...] = (value * inverse * ins[1][...]).astype(BF16)
        outs[1][...] = inverse

    inputs = [
        (full, (tile, features), lambda j, s: (j, 0)),
        (gain, (1, features), lambda j, s: (0, 0)),
    ]
    outputs = [
        ((rows, features), BF16, (tile, features), lambda j, s: (j, 0)),
        ((rows, 1), F32, (tile, 1), lambda j, s: (j, 0)),
    ]
    return 4, inputs, outputs, work


def tail_job(h, weights, width):
    rows, features = h.shape
    blocks, _, chunk, _ = weights.shape

    def work(j, s, ins, outs):
        b, xin = (nn(ins[0][...], w[:, 0].reshape(features, width)) for w in ins[1:])
        outs[0][0] = (b * xin).astype(BF16)

    inputs = [(h, (8, features), lambda j, s: (rows // 8 - 1, 0))] + [
        (weights, (blocks, 1, chunk, width), lambda j, s, k=k: (0, j, 0, k)) for k in (0, 2)
    ]
    return 2, inputs, [((2, 8, width), BF16, (1, 8, width), lambda j, s: (j, 0, 0))], work


def project_job(h, weights, width):
    rows, features = h.shape
    blocks, _, chunk, _ = weights.shape
    def work(j, s, ins, outs):
        outs[0][0] = nn(ins[0][...], ins[1][:, 0].reshape(features, width))

    inputs = [
        (h, (rows, features), lambda j, s: (0, 0)),
        (weights, (blocks, 1, chunk, width), lambda j, s: (0, j // 3, 0, j % 3)),
    ]
    block = (1, rows, width)
    outputs = [((2, rows, 3 * width), F32, block, lambda j, s: (j // 3, 0, j % 3))]
    return 6, inputs, outputs, work


def mix_job(proj, edge, taps, weights):
    _, rows, width = proj.shape
    width //= 3
    half = rows // 2
    blocks, _, chunk, _ = weights.shape
    features = blocks * chunk
    tile = 256

    def core(j):
        return jnp.minimum(j, 1)

    def later(j):
        return jnp.maximum(j - 2, 0)

    inputs = [
        (proj, (1, rows, 3 * width), lambda j, s: (core(j), 0, 0)),
        (edge, (1, 2, width), lambda j, s: (core(j), 0, 0)),
        (taps, (1, 3, width), lambda j, s: (core(j), 0, 0)),
        (weights, (tile // chunk, 2, chunk, width), lambda j, s: (later(j), 0, 0, 3)),
    ]
    outputs = [
        ((2, rows, width), BF16, (2, rows, width), lambda j, s: (0, 0, 0)),
        ((half, features), BF16, (half, tile), lambda j, s: (0, later(j))),
    ]

    def work(j, s, ins, outs):
        values, before, filters, weight = ins

        @pl.when(j < 2)
        def _():
            b, gate, xin = (values[0, :, i * width : (i + 1) * width] for i in range(3))
            gated = (b * xin).astype(BF16).astype(F32)
            arriving = before[0].astype(F32)
            back = [shifted(gated, arriving, 2), shifted(gated, arriving, 1), gated]
            conv = sum(filters[0, k : k + 1, :] * back[k] for k in range(3))
            outs[0][j] = (gate * conv).astype(BF16)

        @pl.when(j >= 2)
        def _():
            start = pl.multiple_of((1 - s[1]) * half, half)
            made = 0.0
            for i in (0, 1):
                part = outs[0][i, pl.ds(start, half), :]
                made = made + nt(part, weight[:, i].reshape(tile, width))
            outs[1][...] = made.astype(BF16)

    return 2 + features // tile, inputs, outputs, work


def shifted(value, edge, distance):
    rows = value.shape[0]
    at = lax.broadcasted_iota(jnp.int32, value.shape, 0)
    moved = pltpu.roll(value, distance % rows, 0)
    if distance > 0:
        for i in range(distance):
            moved = jnp.where(at == i, edge[2 - distance + i : 3 - distance + i, :], moved)
    else:
        for i in range(-distance):
            moved = jnp.where(at == rows + distance + i, edge[i : i + 1, :], moved)
    return moved


def mixer_back_kernel(
    scalars,
    own,
    arrived,
    w_out,
    proj,
    edge,
    later,
    taps,
    h,
    mixed,
    w_in,
    tokens,
    inverse,
    gain,
    full,
    d_proj,
    dots,
    sums,
    grad_own,
    grad_other,
    gain_dots,
    sent,
):
    half = own.shape[0]
    width = w_out.shape[3]
    step = pl.program_id(0)
    core, rank = scalars[0], scalars[1]

    @pl.when(step == 0)
    def _():
        full[pl.ds(pl.multiple_of(rank * half, half), half), :] = own[...]
        full[pl.ds(pl.multiple_of((1 - rank) * half, half), half), :] = arrived[...]

    @pl.when(step < 2)
    def _():
        weight = w_out[:, 0].reshape(full.shape[1], width)
        d_y = nn(full[...], weight)
        b, gate, xin = (proj[0, :, i * width : (i + 1) * width] for i in range(3))
        gated = (b * xin).astype(BF16).astype(F32)
        before = edge[0].astype(F32)
        back = [shifted(gated, before, 2), shifted(gated, before, 1), gated]
        conv = sum(taps[0, k : k + 1, :] * back[k] for k in range(3))
        d_conv = (d_y * gate).astype(BF16).astype(F32)
        following = later[0].astype(F32)
        d_gated = (
            taps[0, 2:3, :] * d_conv
            + taps[0, 1:2, :] * shifted(d_conv, following, -1)
            + taps[0, 0:1, :] * shifted(d_conv, following, -2)
        )
        parts = [(d_gated * xin).astype(BF16), (d_y * conv).astype(BF16), (d_gated * b).astype(BF16)]
        for i, part in enumerate(parts):
            d_proj[step, :, i * width : (i + 1) * width] = part
        product = sum(part.astype(F32) * gate for part, gate in zip(parts, (b, gate, xin)))
        dots[step] = jnp.sum(product, -1, keepdims=True)
        rows = [jnp.sum(d_conv * value, 0, keepdims=True) for value in back]
        sums[0] = jnp.concatenate(rows + [jnp.zeros((5, width), F32)], 0)

    tiles = full.shape[1] // grad_own.shape[0]

    @pl.when((step >= 2) & (step < 2 + tiles))
    def _():
        tile = grad_own.shape[0]
        start = pl.multiple_of((step - 2) * tile, tile)
        dot = 0.0
        for out, index in ((grad_own, core), (grad_other, 1 - core)):
            made = tn(h[...], d_proj[index])
            out[:, : 3 * width] = made.astype(BF16)
            weight = w_in[:, index].reshape(made.shape).astype(F32)
            dot = dot + jnp.sum(made * weight, -1, keepdims=True)
            out[:, 3 * width :] = tn(full[:, pl.ds(start, tile)], mixed[index]).astype(BF16)
        gain_dots[...] = jnp.broadcast_to(dot, gain_dots.shape)

    @pl.when(step >= 2 + tiles)
    def _():
        sent[...] = back_tile(d_proj, w_in, tokens, inverse, dots, gain, full.shape[1]).astype(BF16)


def mixer_back(
    scalars, own, arrived, weights, proj, edge, later, taps, h, mixed, tokens, inverse, gain
):
    half, features = own.shape
    rows = 2 * half
    blocks, _, chunk, _ = weights.shape
    width = proj.shape[2] // 3
    tile = 256

    def per_core(shape):
        return pl.BlockSpec((1, *shape), lambda t, s: (jnp.minimum(t, 1), 0, 0))

    def whole(shape):
        return pl.BlockSpec(shape, lambda t, s: (0,) * len(shape))

    tiles = features // tile

    def tiled(block):
        return pl.BlockSpec(
            block, lambda t, s: (jnp.clip(t - 2, 0, tiles - 1),) + (0,) * (len(block) - 1)
        )

    def back(t, s):
        return (1 - s[1]) * (tiles // 2) + jnp.maximum(t - 2 - tiles, 0)

    def of_tile(t, s):
        return jnp.where(t < 2 + tiles, jnp.maximum(t - 2, 0), back(t, s))

    return pl.pallas_call(
        mixer_back_kernel,
        out_shape=[
            jax.ShapeDtypeStruct((rows, features), BF16),
            jax.ShapeDtypeStruct((2, rows, 3 * width), BF16),
            jax.ShapeDtypeStruct((2, rows, 1), F32),
            jax.ShapeDtypeStruct((2, 8, width), F32),
            jax.ShapeDtypeStruct((features, 4 * width), BF16),
            jax.ShapeDtypeStruct((features, 4 * width), BF16),
            jax.ShapeDtypeStruct((features, 128), F32),
            jax.ShapeDtypeStruct((rows, features // 2), BF16),
        ],
        grid_spec=pltpu.PrefetchScalarGridSpec(
            num_scalar_prefetch=1,
            grid=(2 + tiles + tiles // 2,),
            in_specs=[
                whole((half, features)),
                whole((half, features)),
                pl.BlockSpec((blocks, 1, chunk, width), lambda t, s: (0, jnp.minimum(t, 1), 0, 3)),
                per_core((rows, 3 * width)),
                per_core((2, width)),
                per_core((2, width)),
                per_core((3, width)),
                pl.BlockSpec((rows, tile), lambda t, s: (0, jnp.clip(t - 2, 0, tiles - 1))),
                whole((2, rows, width)),
                pl.BlockSpec(
                    (tile // chunk, 2, chunk, 3 * width), lambda t, s: (of_tile(t, s), 0, 0, 0)
                ),
                pl.BlockSpec((rows, tile), lambda t, s: (0, back(t, s))),
                whole((rows, 1)),
                pl.BlockSpec((1, tile), lambda t, s: (0, back(t, s))),
            ],
            out_specs=[
                whole((rows, features)),
                whole((2, rows, 3 * width)),
                whole((2, rows, 1)),
                per_core((8, width)),
                tiled((tile, 4 * width)),
                tiled((tile, 4 * width)),
                tiled((tile, 128)),
                pl.BlockSpec((rows, tile), lambda t, s: (0, jnp.maximum(t - 2 - tiles, 0))),
            ],
        ),
        compiler_params=pltpu.CompilerParams(vmem_limit_bytes=VMEM_LIMIT),
        name="mixer_back",
    )(
        scalars, own, arrived, weights, proj, edge, later, taps, h, mixed, weights, tokens, inverse, gain
    )


def body(
    tokens,
    in_weight,
    conv_kernel,
    out_weight,
    gate_weight,
    up_weight,
    down_weight,
    mixer_norm_gain,
    gain_ffn,
    cotangent,
):
    x, y, c = (lax.axis_index(name) for name in ("dp", "y", "c"))
    nx, nz = lax.axis_size("dp"), lax.axis_size("tok")
    width = tokens.shape[1]
    features = 4 * width
    rows = tokens.shape[0] // 2
    half = rows // 2
    chunk = in_weight.shape[0]
    pair = 2 * width
    scalars = jnp.stack([c, y, x])
    gain_row = mixer_norm_gain[None]

    def to_mp(value):
        mine, theirs = pick_rows(value, c, rows), pick_rows(value, 1 - c, rows)
        cross = [(2 * i + j, 2 * (1 - i) + 1 - j) for i in (0, 1) for j in (0, 1)]
        return mine, swap(theirs, "c"), swap(mine, "y"), lax.ppermute(theirs, ("y", "c"), cross)

    def join_mp(mine, beside, across, cross):
        near = by_rank(c, mine, beside, 1)
        return near, by_rank(y, near, by_rank(c, across, cross, 1), 1)

    every = ("dp", "tok", "c")

    def gather(shard):
        shard = with_layout_constraint(shard, Layout((0, 1)))
        whole = lax.all_gather(shard, every, axis=0, tiled=True)
        return whole.reshape(features // chunk, 2, chunk, shard.shape[1])

    first = jnp.concatenate([in_weight.reshape(chunk, 3 * width), out_weight.T], 1)
    first_tok = lax.all_to_all(
        jnp.concatenate([first] * nz, 0), "tok", split_axis=0, concat_axis=0, tiled=True
    )
    weights = jnp.concatenate([gate_weight, up_weight, down_weight.T], 1)
    pieces = to_mp(tokens)
    first_tok, weights, cotangent, *pieces = tie(first_tok, weights, cotangent, *pieces)
    weights = gather(weights)
    pieces_cot = to_mp(cotangent)
    taps = by_rank(c, conv_kernel[None], swap(conv_kernel, "c")[None]).astype(F32)

    def both_cores(part):
        mine, theirs = (v.reshape(-1, 1, chunk, v.shape[1]) for v in (part, swap(part, "c")))
        return by_rank(c, mine, theirs, 1)

    if nx == 2:
        first_dp = swap(first_tok, "dp")
        first_tok = both_cores(first_tok)
    else:
        first = lax.all_gather(both_cores(first_tok), "dp", axis=0, tiled=True)

    _, full = join_mp(*pieces)
    h_mix, inverse_mix = run_jobs("norm", scalars, [norm_job(full, gain_row)])
    if nx == 2:
        first_dp, first_tok, h_mix, *pieces_cot = tie(first_dp, first_tok, h_mix, *pieces_cot)
        first = by_rank(x, first_tok, both_cores(first_dp))
    _, cot = join_mp(*pieces_cot)
    cot = jnp.concatenate([pick_rows(cot, y, half), pick_rows(cot, 1 - y, half)], 0)

    ranks = nz * 2
    [gated] = run_jobs("tail", scalars, [tail_job(h_mix, first, width)])
    edge = lax.ppermute(gated[:, -2:], ("tok", "c"), [(i, i + 1) for i in range(ranks - 1)])
    [proj] = run_jobs("project", scalars, [project_job(h_mix, first, width)])
    gate_c = proj[:, :8, width : 2 * width]
    edge, proj = tie(edge, proj)
    mixed_in, sent = run_jobs("mix", scalars, [mix_job(proj, edge, taps, first)])

    def own_rows(s):
        return s[1]

    def other_rows(s):
        return 1 - s[1]

    arrived = swap(sent, "y")
    [kept] = run_jobs(
        "project_out", scalars, [back_job((mixed_in,), first, (3,), own_rows, F32)]
    )
    residual = pick_rows(full, y, half).astype(F32) + kept + arrived.astype(F32)

    inverse_ffn = lax.rsqrt(jnp.mean(residual * residual, -1, keepdims=True) + EPS)
    normalized = residual * inverse_ffn
    h_own = (normalized * gain_ffn).astype(BF16)
    h, hidden, d_gate, d_up = hidden_units(h_own, swap(h_own, "y"), cot, weights)

    def of_core(other):
        return swap(other, "c")

    down_own, down_other = run_jobs("down_gradient", scalars, [pair_job(cot, hidden)])
    d_gate, d_up, down_own, down_other = tie(d_gate, d_up, down_own, down_other)
    both = (d_gate, d_up)
    down_other = of_core(down_other)
    [sent] = run_jobs(
        "back_hidden", scalars, [back_job(both, weights, (0, 1), lambda s: 1, BF16)]
    )
    sent, down_own, down_other = tie(sent, down_own, down_other)

    late_gate, sent, *pieces = tie(d_gate, sent, *for_dp(down_own, down_other))
    arrived, pieces = swap(sent, "y"), to_dp(pieces)
    own, other, kept = run_jobs(
        "gate_gradient",
        scalars,
        [pair_job(h, late_gate), back_job(both, weights, (0, 1), lambda s: 0, F32)],
    )
    arrived, own, other, *pieces = tie(arrived, own, other, *pieces)
    other = of_core(other)
    d_h = kept + arrived.astype(F32)
    grad_gain_ffn = jnp.sum(d_h * normalized, 0)
    scaled = d_h * gain_ffn
    d_res = cot[:half].astype(F32) + inverse_ffn * (
        scaled - normalized * jnp.mean(scaled * normalized, -1, keepdims=True)
    )
    d_res_own = d_res.astype(BF16)
    down_mine = add_dp(down_own, down_other, pieces)
    late_up, late_hidden, d_res_own, down_mine, *pieces = tie(
        d_up, hidden, d_res_own, down_mine, *for_dp(own, other)
    )
    arrived, down_got, pieces = swap(d_res_own, "y"), to_tok(down_mine), to_dp(pieces)
    up_own, up_other, made_sent, made_kept = run_jobs(
        "up_gradient",
        scalars,
        [pair_job(h, late_up), made_job(late_hidden, weights, 2, residual)],
    )
    arrived, up_own, up_other, made_sent, made_kept, down_got, *pieces = tie(
        arrived, up_own, up_other, made_sent, made_kept, down_got, *pieces
    )
    up_other = of_core(up_other)
    gate_mine = add_dp(own, other, pieces)

    head = jnp.where(y == 0, d_res_own[:8], arrived[:8])
    w_out = first[:, :, :, 3 * width :]
    d_head = jnp.stack([nn(head, w_out[:, i].reshape(features, width)) for i in (0, 1)])
    d_head = (d_head * gate_c).astype(BF16)[:, :2]
    later = lax.ppermute(d_head, ("tok", "c"), [(i + 1, i) for i in range(ranks - 1)])
    arrived, gate_mine, later, *pieces = tie(
        arrived, gate_mine, later, *for_dp(up_own, up_other)
    )
    gate_got, pieces = to_tok(gate_mine), to_dp(pieces)
    d_res_full, d_proj, dots, grad_taps, own, other, gain_dots, sent = mixer_back(
        scalars,
        d_res_own,
        arrived,
        first,
        proj,
        edge,
        later,
        taps,
        h_mix,
        mixed_in,
        full,
        inverse_mix,
        gain_row,
    )
    near_sums = jnp.concatenate([grad_taps[0, :3], grad_taps[1, :3]], 1)
    sums = lax.dynamic_update_slice(jnp.zeros((3, features), F32), near_sums, (0, y * pair))
    gain_sum = gain_dots[:, 0] / mixer_norm_gain
    sums = jnp.concatenate([sums, gain_sum[None], grad_gain_ffn[None]], 0)
    d_proj, own, other, sent, gate_got, *pieces = tie(
        d_proj, own, other, sent, gate_got, *pieces
    )
    other, sums = of_core(other), sum_over(sums, "c")
    up_mine = add_dp(up_own, up_other, pieces)
    sent, d_proj, up_mine, sums, *pieces = tie(
        sent, d_proj, up_mine, sums, *for_dp(own, other)
    )
    arrived, up_got, pieces = swap(sent, "y"), to_tok(up_mine), to_dp(pieces)
    if nx == 2:
        cross = [(2 * i + j, 2 * (1 - i) + 1 - j) for i in (0, 1) for j in (0, 1)]
        near, far = swap(sums, "y"), lax.ppermute(sums, ("dp", "y"), cross)
        sums = [sums, near, swap(sums, "dp"), far]
    else:
        sums = [sum_over(sum_over(sums, "dp"), "y")]
    [kept] = run_jobs(
        "back_in",
        scalars,
        [back_in_job(d_proj, first, full, inverse_mix, dots, gain_row, own_rows, F32)],
    )
    arrived, kept, up_got, sums, *pieces = tie(arrived, kept, up_got, sums, *pieces)
    sums = (sums[0] + sums[1]) + (sums[2] + sums[3]) if nx == 2 else sums[0]
    mixer_mine = add_dp(own, other, pieces)

    high = sums.astype(BF16)
    low = (sums - high.astype(F32)).astype(BF16)
    extra = jnp.concatenate([high, low, jnp.zeros((16 - 2 * sums.shape[0], features), BF16)], 0)
    mixer_mine = jnp.concatenate(
        [
            mixer_mine.reshape(nz, chunk, features),
            jnp.broadcast_to(extra, (nz, 16, features)),
        ],
        1,
    )
    mixer_got = to_tok(mixer_mine.reshape(nz * (chunk + 16), features))
    made_sent, arrived = tie(made_sent, arrived)
    made_arrived = swap(made_sent, "y")

    d_res_near = jnp.where(y == 0, d_res_full[:, :pair], d_res_full[:, pair:]).astype(F32)

    def by_core(value):
        mine = jnp.where(c == 0, value[:, :width], value[:, width:])
        theirs = jnp.where(c == 0, value[:, width:], value[:, :width])
        return by_rank(c, mine, swap(theirs, "c"))

    input_gradient = by_core(
        d_res_near + inverse_mix * (kept + arrived.astype(F32))
    )
    out_near = by_rank(
        y,
        (made_kept[:half] + made_arrived[half:].astype(F32)).astype(BF16),
        (made_kept[half:] + made_arrived[:half].astype(F32)).astype(BF16),
    )
    mixed = by_core(out_near)
    grad_down, grad_gate, grad_up = (add_tok(v) for v in (down_got, gate_got, up_got))
    mixer_sum = add_tok(mixer_got)
    grad_mixer = mixer_sum[:chunk]
    sums = mixer_sum[chunk : chunk + 5] + mixer_sum[chunk + 5 : chunk + 10]
    grad_in = grad_mixer[:, : 3 * width].reshape(chunk, 3, width)
    grad_out = grad_mixer[:, 3 * width :].T

    sums = lax.dynamic_slice_in_dim(sums, (2 * y + c) * width, width, 1)

    return (
        mixed,
        input_gradient,
        grad_in,
        sums[:3],
        grad_out,
        grad_gate,
        grad_up,
        grad_down.T,
        sums[3],
        sums[4],
    )


def solution(mesh):
    split = Mesh(
        mesh.devices.reshape(mesh.shape["dp"], mesh.shape["tok"], mesh.shape["mp"] // 2, 2),
        ("dp", "tok", "y", "c"),
    )
    tok, mp = ("dp", "tok"), ("y", "c")
    return jax.shard_map(
        body,
        mesh=split,
        in_specs=(
            P(tok, mp),
            P(tok, None, mp),
            P(None, mp),
            P(mp, tok),
            P(tok, mp),
            P(tok, mp),
            P(mp, tok),
            P(),
            P(),
            P(tok, mp),
        ),
        out_specs=(
            P(tok, mp),
            P(tok, mp),
            P(tok, None, mp),
            P(None, mp),
            P(mp, tok),
            P(tok, mp),
            P(tok, mp),
            P(mp, tok),
            P(mp),
            P(mp),
        ),
        check_vma=False,
    )
```

time: 634 us -> 422 us (0.67)
  Pallas kernels: 0 us -> 142 us
  matrix products: 132 us -> 1.83 us
  waiting for transfers between devices: 222 us -> 133 us
  blocking collectives: 84 us -> 0 us
  starting transfers between devices: 111 us -> 51.5 us
  other arithmetic: 41.2 us -> 58.6 us
  local copies, waits for them, and re-layouts: 35.4 us -> 18.7 us
  between operations: 2.34 us -> 14.6 us
    pallas_call x0 -> x12, Pallas kernels: none -> 142 us  [the longest x10 99 us: run_jobs(): pl.pallas_call(kernel, out_shape=shapes, grid_spec=pltpu.PrefetchScalarGr...]
    dot_general x44 -> x2, matrix products: 132 us -> 1.83 us  [dot(): lax.dot_general(left, right, (contract, ((), ())), preferred_element_type...]
    psum x1 -> x0, blocking collectives: 84 us -> none  [body(): lax.psum(jnp.concatenate([place_near(near_sums), ffn_sum[None]], 0), ('dp...]
    ppermute x30 -> x6, waiting for transfers between devices: 76.4 us -> 1.86 us  [the longest x1 1.6 us: sum_over(): lax.ppermute(value, axis, [(s, s ^ step) for s in range(size)])]
    ppermute x16 -> x4, waiting for transfers between devices: 63 us -> 8.58 us  [deliver(): lax.ppermute(value, axis, [(s, (s + distance) % size) for s in range(size)])]
    ppermute x30 -> x6, starting transfers between devices: 61 us -> 8.19 us  [the longest x1 2.56 us: body(): near, far = (swap(sums, 'y'), lax.ppermute(sums, ('dp', 'y'), cross))]
    all_to_all x0 -> x5, waiting for transfers between devices: none -> 35.9 us  [the longest x1 21.7 us: body(): lax.all_to_all(jnp.concatenate([first] * nz, 0), 'tok', split_axis=0, con...]
    ppermute x16 -> x4, starting transfers between devices: 36.1 us -> 5.31 us  [deliver(): lax.ppermute(value, axis, [(s, (s + distance) % size) for s in range(size)])]
  transfers between devices with their start and end apart: 68 -> 38, of which waited for: 32 -> 18; matrix products, arithmetic and copies ran while one was open for 23% -> 15% of each run, Pallas kernels for 0% -> 26%
where the time goes in v2:
time: 422 us; the launch traced here: 420 us
  Pallas kernels  142 us (34%)
  waiting for transfers between devices  133 us (32%)
  other arithmetic  58.6 us (14%)
  starting transfers between devices  51.5 us (12%)
  local copies, waits for them, and re-layouts  18.7 us (4%)
  between operations  14.6 us (3%)
    pallas_call x10, Pallas kernels, run_jobs(): pl.pallas_call(kernel, out_shape=shapes, grid_spec=pltpu.PrefetchScalarGr...  99 us
    ppermute x22, waiting for transfers between devices, swap(): return lax.ppermute(value, axis, [(0, 1), (1, 0)])  86.3 us
    pallas_call x1, Pallas kernels, hidden_units(): pl.pallas_call(hidden_kernel, out_shape=[jax.ShapeDtypeStruct((rows, feat...  22 us
    all_to_all x1, waiting for transfers between devices, body(): lax.all_to_all(jnp.concatenate([first] * nz, 0), 'tok', split_axis=0, con...  21.7 us
    pallas_call x1, Pallas kernels, mixer_back(): pl.pallas_call(mixer_back_kernel, out_shape=[jax.ShapeDtypeStruct((rows,...  21.2 us
    all_to_all x4, starting transfers between devices, to_tok(): return lax.all_to_all(mine, 'tok', split_axis=0, concat_axis=0, tiled=True)  17 us
    select_n x11, other arithmetic, by_rank(): jnp.where(index == 0, jnp.concatenate([first, second], axis), jnp.concate...  15 us
    ppermute x22, starting transfers between devices, swap(): return lax.ppermute(value, axis, [(0, 1), (1, 0)])  14.5 us
  transfers between devices with their start and end apart: 38, of which 18 were waited for; matrix products, arithmetic and copies ran while one was open for 15% of the time, Pallas kernels for 26%

profile of v2, /device:TPU:0, one launch (start us, length us, event | category | flops | bytes accessed | tf_op | source)
XLA Modules:
  0.0 420.1 jit_solution(10059792346876504793)
XLA Ops:
  8.4 2.1 copy_bitcast_fusion
  10.5 6.5 %all-to-all-start = ((bf16[4,128,1024]{1,2,0:T(8,128)(2,1)}), bf16[4,128,1024]{1,2,0:T(8,128)(2,1)S(1)}, u32[]{:S(2)}, u32[]{:S(2)}) async-start(bf16[4,128,1024]{1,2,0:T(8,128)(2,1)} %copy_bitcast_fusion), calls=%async_computation | async-start | bytes 2097152 | tf_op jit(solution)/shard_map/all_to_all | solution.py:637
  20.9 21.7 %all-to-all-done = bf16[4,128,1024]{1,2,0:T(8,128)(2,1)S(1)} async-done(((bf16[4,128,1024]{1,2,0:T(8,128)(2,1)}), bf16[4,128,1024]{1,2,0:T(8,128)(2,1)S(1)}, u32[]{:S(2)}, u32[]{:S(2)}) %all-to-all-start) | async-done | bytes 1048608 | tf_op jit(solution)/shard_map/all_to_all | solution.py:637
  49.0 2.5 maximum_select_fusion.6
  51.5 2.0 maximum_select_fusion.1.refs_0_.tokens.refs_2_
  53.4 5.1 %norm.1 = (bf16[1024,1024]{1,0:T(8,128)(2,1)}, f32[1024,1]{1,0:T(8,128)}) custom-call(s32[3]{0:T(128)} %pad_add_fusion.scalars_ref.scalars, bf16[1024,1024]{1,0:T(8,128)(2,1)} %maximum_select_fusion.1.refs_0_.tokens.refs_2_, f32[1,1024]{1,0:T(1,128)} %bitcast.75), custom_call_target="tpu_custom_call" | custom-call | tf_op jit(solution)/shard_map/norm/pallas_call | solution.py:200
  59.5 1.9 maximum_select_fusion.2
  61.4 11.1 %collective-permute-done.6 = bf16[1024,256]{1,0:T(8,128)(2,1)S(1)} collective-permute-done((bf16[1024,256]{1,0:T(8,128)(2,1)S(1)}, bf16[1024,256]{1,0:T(8,128)(2,1)S(1)}, u32[]{:S(2)}, u32[]{:S(2)}) %collective-permute-start.6) | collective-permute-done | bytes 524320 | tf_op jit(solution)/shard_map/ppermute | solution.py:19
  72.5 6.0 %collective-permute-done.3 = bf16[512,1024]{1,0:T(8,128)(2,1)} collective-permute-done((bf16[512,1024]{1,0:T(8,128)(2,1)S(1)}, bf16[512,1024]{1,0:T(8,128)(2,1)}, u32[]{:S(2)}, u32[]{:S(2)}) %collective-permute-start.3) | collective-permute-done | bytes 1048608 | tf_op jit(solution)/shard_map/ppermute | solution.py:19
  79.0 2.4 collective-permute-done.8
  81.3 1.8 maximum_select_fusion.3
  83.2 2.3 maximum_select_fusion.refs_1_.refs_2_.refs_3_.w_out.w_in
  85.5 3.1 tail.1
  89.3 2.2 collective-permute-start.9
  92.2 9.6 %project.1.refs_0_.proj = f32[2,1024,768]{2,1,0:T(8,128)} custom-call(s32[3]{0:T(128)} %pad_add_fusion.scalars_ref.scalars, bf16[1024,1024]{1,0:T(8,128)(2,1)} %get-tuple-element.109.refs_0_.h, bf16[8,2,128,1024]{3,2,1,0:T(8,128)(2,1)} %maximum_select_fusion.refs_1_.refs_2_.refs_3_.w_out.w_in), custom_call_target="tpu_custom_call" | custom-call | tf_op jit(solution)/shard_map/project/pallas_call | solution.py:200
  102.3 8.0 %mix.1 = (bf16[2,1024,256]{2,1,0:T(8,128)(2,1)}, bf16[512,1024]{1,0:T(8,128)(2,1)}) custom-call(s32[3]{0:T(128)} %pad_add_fusion.scalars_ref.scalars, f32[2,1024,768]{2,1,0:T(8,128)} %project.1.refs_0_.proj, bf16[2,2,256]{2,1,0:T(2,128)(2,1)} %copy-done.33, f32[2,3,256]{2,1,0:T(4,128)} %fusion.1.refs_2_.taps, ...), custom_call_target="tpu_custom_call" | custom-call | tf_op jit(solution)/shard_map/mix/pallas_call | solution.py:200
  111.6 5.3 %project_out.1 = f32[512,1024]{1,0:T(8,128)} custom-call(s32[3]{0:T(128)} %pad_add_fusion.scalars_ref.scalars, bf16[2,1024,256]{2,1,0:T(8,128)(2,1)} %get-tuple-element.114.refs_0_.mixed, bf16[8,2,128,1024]{3,2,1,0:T(8,128)(2,1)} %maximum_select_fusion.refs_1_.refs_2_.refs_3_.w_out.w_in), custom_call_target="tpu_custom_call" | custom-call | tf_op jit(solution)/shard_map/project_out/pallas_call | solution.py:200
  116.9 18.0 %collective-permute-done.11 = bf16[512,1024]{1,0:T(8,128)(2,1)S(1)} collective-permute-done((bf16[512,1024]{1,0:T(8,128)(2,1)}, bf16[512,1024]{1,0:T(8,128)(2,1)S(1)}, u32[]{:S(2)}, u32[]{:S(2)}) %collective-permute-start.11) | collective-permute-done | bytes 1048608 | tf_op jit(solution)/shard_map/ppermute | solution.py:19
  134.9 2.4 multiply_reduce_fusion.2
  143.9 21.0 %collective-permute-done.12.h_other = bf16[512,1024]{1,0:T(8,128)(2,1)} collective-permute-done((bf16[512,1024]{1,0:T(8,128)(2,1)}, bf16[512,1024]{1,0:T(8,128)(2,1)}, u32[]{:S(2)}, u32[]{:S(2)}) %collective-permute-start.12) | collective-permute-done | bytes 1048608 | tf_op jit(solution)/shard_map/ppermute | solution.py:19
  164.9 22.0 %hidden_units.1 = (bf16[1024,1024]{1,0:T(8,128)(2,1)}, bf16[2,1024,1152]{2,1,0:T(8,128)(2,1)}, bf16[2,1024,1152]{2,1,0:T(8,128)(2,1)}, bf16[2,1024,1152]{2,1,0:T(8,128)(2,1)}) custom-call(bf16[512,1024]{1,0:T(8,128)(2,1)} %multiply_convert_fusion.h_own, bf16[512,1024]{1,0:T(8,128)(2,1)} %collective-permute-done.12.h_other, ...), custom_call_target="tpu_custom_call" | custom-call | flops 14495514624 | bytes 32505856 | tf_op jit(solution)/shard_map/hidden_units/pallas_call | solution.py:151
  186.9 10.3 %down_gradient.1 = (bf16[1024,1152]{1,0:T(8,128)(2,1)}, bf16[1024,1152]{1,0:T(8,128)(2,1)}) custom-call(s32[3]{0:T(128)} %pad_add_fusion.scalars_ref.scalars, bf16[1024,1024]{1,0:T(8,128)(2,1)} %pad_maximum_fusion.cot.refs_0_, bf16[2,1024,1152]{2,1,0:T(8,128)(2,1)} %get-tuple-element.146.refs_1_.refs_2_), custom_call_target="tpu_custom_call" | custom-call | tf_op jit(solution)/shard_map/down_gradient/pallas_call | solution.py:200
  197.3 11.0 %back_hidden.1 = bf16[512,1024]{1,0:T(8,128)(2,1)} custom-call(s32[3]{0:T(128)} %pad_add_fusion.scalars_ref.scalars, bf16[2,1024,1152]{2,1,0:T(8,128)(2,1)} %get-tuple-element.134.refs_0_.refs_1_.refs_2_, bf16[2,1024,1152]{2,1,0:T(8,128)(2,1)} %get-tuple-element.145.refs_1_.refs_3_, bf16[8,2,128,3456]{3,2,1,0:T(8,128)(2,1)} %bitcast.52, ...), custom_call_target="tpu_custom_call" | custom-call | tf_op jit(solution)/shard_map/back_hidden/pallas_call | solution.py:200
  212.3 19.7 %gate_gradient.1 = (bf16[1024,1152]{1,0:T(8,128)(2,1)}, bf16[1024,1152]{1,0:T(8,128)(2,1)}, f32[512,1024]{1,0:T(8,128)}) custom-call(s32[3]{0:T(128)} %pad_add_fusion.scalars_ref.scalars, bf16[1024,1024]{1,0:T(8,128)(2,1)} %get-tuple-element.127.refs_0_, bf16[2,1024,1152]{2,1,0:T(8,128)(2,1)} %get-tuple-element.134.refs_0_.refs_1_.refs_2_, ...), custom_call_target="tpu_custom_call" | custom-call | tf_op jit(solution)/shard_map/gate_gradient/pallas_call | solution.py:200
  232.0 3.9 collective-permute-done.14
  235.9 2.6 collective-permute-done.15
  238.5 2.7 multiply_reduce_fusion
  241.2 3.0 add_convert_fusion.8.own
  244.2 3.2 add_convert_fusion.4
  247.5 2.6 add_convert_fusion.3
  250.1 3.9 all-to-all-start.1
  255.5 1.6 collective-permute-start.17
  257.1 20.0 %up_gradient.1 = (bf16[1024,1152]{1,0:T(8,128)(2,1)}, bf16[1024,1152]{1,0:T(8,128)(2,1)}, bf16[1024,512]{1,0:T(8,128)(2,1)}, f32[1024,512]{1,0:T(8,128)}) custom-call(s32[3]{0:T(128)} %pad_add_fusion.scalars_ref.scalars, bf16[1024,1024]{1,0:T(8,128)(2,1)} %get-tuple-element.127.refs_0_, bf16[2,1024,1152]{2,1,0:T(8,128)(2,1)} %get-tuple-element.145.refs_1_.refs_3_, ...), custom_call_target="tpu_custom_call" | custom-call | tf_op jit(solution)/shard_map/up_gradient/pallas_call | solution.py:200
  277.2 6.0 %all-to-all-done.1 = bf16[4,128,1152]{2,1,0:T(8,128)(2,1)S(1)} async-done(((bf16[4,128,1152]{2,1,0:T(8,128)(2,1)}), bf16[4,128,1152]{2,1,0:T(8,128)(2,1)S(1)}, u32[]{:S(2)}, u32[]{:S(2)}) %all-to-all-start.1) | async-done | bytes 1179680 | tf_op jit(solution)/shard_map/all_to_all | solution.py:81
  289.4 3.1 add_convert_fusion.2
  294.3 4.4 %all-to-all-start.2 = ((bf16[4,128,1152]{2,1,0:T(8,128)(2,1)}), bf16[4,128,1152]{2,1,0:T(8,128)(2,1)S(1)}, u32[]{:S(2)}, u32[]{:S(2)}) async-start(bf16[4,128,1152]{2,1,0:T(8,128)(2,1)} %bitcast.21), calls=%async_computation.2 | async-start | bytes 2359296 | tf_op jit(solution)/shard_map/all_to_all | solution.py:81
  300.3 21.2 %mixer_back.1 = (bf16[1024,1024]{1,0:T(8,128)(2,1)}, bf16[2,1024,768]{2,1,0:T(8,128)(2,1)}, f32[2,1024,1]{2,1,0:T(8,128)}, f32[2,8,256]{2,1,0:T(8,128)}, bf16[10...) custom-call(s32[3]{0:T(128)} %pad_add_fusion.scalars_ref.scalars, ...), custom_call_target="tpu_custom_call" | custom-call | tf_op jit(solution)/shard_map/mixer_back/pallas_call | solution.py:547
  321.5 6.0 %collective-permute-done.21 = bf16[512,1152]{1,0:T(8,128)(2,1)} collective-permute-done((bf16[512,1152]{1,0:T(8,128)(2,1)}, bf16[512,1152]{1,0:T(8,128)(2,1)}, u32[]{:S(2)}, u32[]{:S(2)}) %collective-permute-start.21) | collective-permute-done | bytes 1179680 | tf_op jit(solution)/shard_map/ppermute | solution.py:24
  332.2 3.6 add_convert_fusion
  337.5 4.0 all-to-all-start.3
  346.9 2.6 collective-permute-start.27
  350.4 7.0 %back_in.1 = f32[1024,512]{1,0:T(8,128)} custom-call(s32[3]{0:T(128)} %pad_add_fusion.scalars_ref.scalars, bf16[2,1024,768]{2,1,0:T(8,128)(2,1)} %get-tuple-element.176.refs_0_, bf16[8,2,128,1024]{3,2,1,0:T(8,128)(2,1)} %maximum_select_fusion.refs_1_.refs_2_.refs_3_.w_out.w_in, bf16[1024,1024]{1,0:T(8,128)(2,1)} %maximum_select_fusion.1.refs_0_.tokens.refs_2_, ...), custom_call_target="tpu_custom_call" | custom-call | tf_op jit(solution)/shard_map/back_in/pallas_call | solution.py:200
  357.4 10.3 %collective-permute-done.25 = f32[5,1024]{1,0:T(8,128)S(1)} collective-permute-done((f32[5,1024]{1,0:T(8,128)S(1)}, f32[5,1024]{1,0:T(8,128)S(1)}, u32[]{:S(2)}, u32[]{:S(2)}) %collective-permute-start.25) | collective-permute-done | bytes 20512 | tf_op jit(solution)/shard_map/ppermute | solution.py:19
  372.0 2.2 add_convert_fusion.6
  375.4 4.6 %all-to-all-start.4 = ((bf16[4,144,1024]{2,1,0:T(8,128)(2,1)}), bf16[4,144,1024]{2,1,0:T(8,128)(2,1)}, u32[]{:S(2)}, u32[]{:S(2)}) async-start(bf16[4,144,1024]{2,1,0:T(8,128)(2,1)} %pad_maximum_fusion.1), calls=%async_computation.4 | async-start | bytes 2359296 | tf_op jit(solution)/shard_map/all_to_all | solution.py:81
  380.0 2.4 multiply_add_fusion
  382.6 12.3 %collective-permute-done.29 = bf16[1024,512]{1,0:T(8,128)(2,1)} collective-permute-done((bf16[1024,512]{1,0:T(8,128)(2,1)}, bf16[1024,512]{1,0:T(8,128)(2,1)}, u32[]{:S(2)}, u32[]{:S(2)}) %collective-permute-start.29) | collective-permute-done | bytes 1048608 | tf_op jit(solution)/shard_map/ppermute | solution.py:19
  401.0 6.6 %all-to-all-done.4 = bf16[4,144,1024]{2,1,0:T(8,128)(2,1)} async-done(((bf16[4,144,1024]{2,1,0:T(8,128)(2,1)}), bf16[4,144,1024]{2,1,0:T(8,128)(2,1)}, u32[]{:S(2)}, u32[]{:S(2)}) %all-to-all-start.4) | async-done | bytes 1179680 | tf_op jit(solution)/shard_map/all_to_all | solution.py:81
  (190 shorter events, 67.7 us)
Async XLA Ops:
  7.2 9.7 %copy-start.21 = (bf16[2048,256]{1,0:T(8,128)(2,1)S(1)}, bf16[2048,256]{1,0:T(8,128)(2,1)}, u32[]{:S(2)}) copy-start(bf16[2048,256]{1,0:T(8,128)(2,1)} %param.10) | copy-start | bytes 3145732
  10.5 32.2 %all-to-all-start = ((bf16[4,128,1024]{1,2,0:T(8,128)(2,1)}), bf16[4,128,1024]{1,2,0:T(8,128)(2,1)S(1)}, u32[]{:S(2)}, u32[]{:S(2)}) async-start(bf16[4,128,1024]{1,2,0:T(8,128)(2,1)} %copy_bitcast_fusion), calls=%async_computation | async-start | bytes 2097152 | tf_op jit(solution)/shard_map/all_to_all | solution.py:637
  16.9 148.0 %all-gather.2.cloned.1.call-start = ((), (), s32[]{:S(2)}) async-start(), calls=%async_computation.5 | async-start | bytes 15040512 | tf_op jit(solution)/shard_map/all_gather | solution.py:633
  17.8 25.4 %collective-permute-start = (bf16[1024,256]{1,0:T(8,128)(2,1)}, bf16[1024,256]{1,0:T(8,128)(2,1)}, u32[]{:S(2)}, u32[]{:S(2)}) collective-permute-start(bf16[1024,256]{1,0:T(8,128)(2,1)} %get-tuple-element.250), channel_id=1, source_target_pairs={{0,1},{1,0},{2,3},{3,2},{4,5},{5,4},{6,7},{7,6},{8,9},{9,8},{10,11... | collective-permute-start | bytes 1572872 | tf_op jit(solution)/shard_map/ppermute | solution.py:19
  17.8 25.4 %collective-permute-start.1 = (bf16[1024,256]{1,0:T(8,128)(2,1)S(1)}, bf16[1024,256]{1,0:T(8,128)(2,1)}, u32[]{:S(2)}, u32[]{:S(2)}) collective-permute-start(bf16[1024,256]{1,0:T(8,128)(2,1)S(1)} %get-tuple-element.102), channel_id=1, source_target_pairs={{0,2},{2,0},{1,3},{3,1},{4,6},{6,4},{5,7},{7,5},{8,10},{10,8},{9,1... | collective-permute-start | bytes 1572872 | tf_op jit(solution)/shard_map/ppermute | solution.py:19
  19.3 23.9 %collective-permute-start.2 = (bf16[1024,256]{1,0:T(8,128)(2,1)}, bf16[1024,256]{1,0:T(8,128)(2,1)}, u32[]{:S(2)}, u32[]{:S(2)}) collective-permute-start(bf16[1024,256]{1,0:T(8,128)(2,1)} %get-tuple-element.250), channel_id=1, source_target_pairs={{0,3},{1,2},{2,1},{3,0},{4,7},{5,6},{6,5},{7,4},{8,11},{9,10},{10,... | collective-permute-start | bytes 1572872 | tf_op jit(solution)/shard_map/ppermute | solution.py:623
  43.2 15.3 %collective-permute-start.4 = (bf16[512,1024]{1,0:T(8,128)(2,1)S(1)}, bf16[512,1024]{1,0:T(8,128)(2,1)S(1)}, u32[]{:S(2)}, u32[]{:S(2)}) collective-permute-start(bf16[512,1024]{1,0:T(8,128)(2,1)S(1)} %bitcast.62), channel_id=1, source_target_pairs={{0,1},{1,0},{2,3},{3,2},{4,5},{5,4},{6,7},{7,6},{8,9},{9,8},{10,11... | collective-permute-start | bytes 3145736 | tf_op jit(solution)/shard_map/ppermute | solution.py:19
  43.4 35.1 %collective-permute-start.3 = (bf16[512,1024]{1,0:T(8,128)(2,1)S(1)}, bf16[512,1024]{1,0:T(8,128)(2,1)}, u32[]{:S(2)}, u32[]{:S(2)}) collective-permute-start(bf16[512,1024]{1,0:T(8,128)(2,1)S(1)} %bitcast.63), channel_id=1, source_target_pairs={{0,16},{16,0},{1,17},{17,1},{2,18},{18,2},{3,19},{19,3},{4,20},{20... | collective-permute-start | bytes 3145736 | tf_op jit(solution)/shard_map/ppermute | solution.py:19
  46.8 14.6 %collective-permute-start.5 = (bf16[1024,256]{1,0:T(8,128)(2,1)S(1)}, bf16[1024,256]{1,0:T(8,128)(2,1)S(1)}, u32[]{:S(2)}, u32[]{:S(2)}) collective-permute-start(bf16[1024,256]{1,0:T(8,128)(2,1)S(1)} %get-tuple-element.248), channel_id=1, source_target_pairs={{0,1},{1,0},{2,3},{3,2},{4,5},{5,4},{6,7},{7,6},{8,9},{9,8},{10,11... | collective-permute-start | bytes 1572872 | tf_op jit(solution)/shard_map/ppermute | solution.py:19
  47.0 25.5 %collective-permute-start.7 = (bf16[1024,256]{1,0:T(8,128)(2,1)S(1)}, bf16[1024,256]{1,0:T(8,128)(2,1)S(1)}, u32[]{:S(2)}, u32[]{:S(2)}) collective-permute-start(bf16[1024,256]{1,0:T(8,128)(2,1)S(1)} %get-tuple-element.248), channel_id=1, source_target_pairs={{0,3},{1,2},{2,1},{3,0},{4,7},{5,6},{6,5},{7,4},{8,11},{9,10},{10,... | collective-permute-start | bytes 1572872 | tf_op jit(solution)/shard_map/ppermute | solution.py:623
  48.5 24.0 %collective-permute-start.6 = (bf16[1024,256]{1,0:T(8,128)(2,1)S(1)}, bf16[1024,256]{1,0:T(8,128)(2,1)S(1)}, u32[]{:S(2)}, u32[]{:S(2)}) collective-permute-start(bf16[1024,256]{1,0:T(8,128)(2,1)S(1)} %get-tuple-element.116), channel_id=1, source_target_pairs={{0,2},{2,0},{1,3},{3,1},{4,6},{6,4},{5,7},{7,5},{8,10},{10,8},{9,1... | collective-permute-start | bytes 1572872 | tf_op jit(solution)/shard_map/ppermute | solution.py:19
  59.5 19.0 %copy-start.35 = (bf16[3,256]{1,0:T(4,128)(2,1)S(1)}, bf16[3,256]{1,0:T(4,128)(2,1)}, u32[]{:S(2)}) copy-start(bf16[3,256]{1,0:T(4,128)(2,1)} %param.12) | copy-start | bytes 4612
  61.4 17.1 %copy-start.22 = (bf16[1024,256]{1,0:T(8,128)(2,1)}, bf16[1024,256]{1,0:T(8,128)(2,1)S(1)}, u32[]{:S(2)}) copy-start(bf16[1024,256]{1,0:T(8,128)(2,1)S(1)} %collective-permute-done.5) | copy-start | bytes 1572868
  78.5 2.9 collective-permute-start.8
  78.5 13.1 %collective-permute-start.10 = (bf16[3,256]{1,0:T(4,128)(2,1)S(1)}, bf16[3,256]{1,0:T(4,128)(2,1)S(1)}, u32[]{:S(2)}, u32[]{:S(2)}) collective-permute-start(bf16[3,256]{1,0:T(4,128)(2,1)S(1)} %copy-done.35), channel_id=1, source_target_pairs={{0,1},{1,0},{2,3},{3,2},{4,5},{5,4},{6,7},{7,6},{8,9},{9,8},{10,11... | collective-permute-start | bytes 4616 | tf_op jit(solution)/shard_map/ppermute | solution.py:19
  89.3 12.4 %collective-permute-start.9 = (bf16[2,2,256]{2,1,0:T(2,128)(2,1)S(1)}, bf16[2,2,256]{2,1,0:T(2,128)(2,1)S(1)}, u32[]{:S(2)}, u32[]{:S(2)}) collective-permute-start(bf16[2,2,256]{2,1,0:T(2,128)(2,1)S(1)} %slice.197), channel_id=1, source_target_pairs={{0,1},{1,4},{4,5},{5,8},{8,9},{9,12},{12,13},{2,3},{3,6},{6,7},{7,... | collective-permute-start | bytes 6152 | tf_op jit(solution)/shard_map/ppermute | solution.py:667
  110.3 24.6 %collective-permute-start.11 = (bf16[512,1024]{1,0:T(8,128)(2,1)}, bf16[512,1024]{1,0:T(8,128)(2,1)S(1)}, u32[]{:S(2)}, u32[]{:S(2)}) collective-permute-start(bf16[512,1024]{1,0:T(8,128)(2,1)} %get-tuple-element.115), channel_id=1, source_target_pairs={{0,2},{2,0},{1,3},{3,1},{4,6},{6,4},{5,7},{7,5},{8,10},{10,8},{9,1... | collective-permute-start | bytes 3145736 | tf_op jit(solution)/shard_map/ppermute | solution.py:19
  111.6 23.3 %copy-start.1 = (bf16[1024,1024]{1,0:T(8,128)(2,1)S(1)}, bf16[1024,1024]{1,0:T(8,128)(2,1)}, u32[]{:S(2)}) copy-start(bf16[1024,1024]{1,0:T(8,128)(2,1)} %maximum_select_fusion.1.refs_0_.tokens.refs_2_) | copy-start | bytes 6291460
  116.9 20.5 %copy-start.32 = (f32[1024]{0:T(1024)S(1)}, f32[1024]{0:T(1024)}, u32[]{:S(2)}) copy-start(f32[1024]{0:T(1024)} %param.18) | copy-start | bytes 12292
  137.4 103.8 %copy-start = (f32[512,1024]{1,0:T(8,128)}, f32[512,1024]{1,0:T(8,128)S(1)}, u32[]{:S(2)}) copy-start(f32[512,1024]{1,0:T(8,128)S(1)} %get-tuple-element.231.refs_4_) | copy-start | bytes 6291460
  138.7 26.2 %collective-permute-start.12 = (bf16[512,1024]{1,0:T(8,128)(2,1)}, bf16[512,1024]{1,0:T(8,128)(2,1)}, u32[]{:S(2)}, u32[]{:S(2)}) collective-permute-start(bf16[512,1024]{1,0:T(8,128)(2,1)} %multiply_convert_fusion.h_own), channel_id=1, source_target_pairs={{0,2},{2,0},{1,3},{3,1},{4,6},{6,4},{5,7},{7,5},{8,10},{10,8},{9,1... | collective-permute-start | bytes 3145736 | tf_op jit(solution)/shard_map/ppermute | solution.py:19
  197.2 11.2 %collective-permute-start.13 = (bf16[1024,1152]{1,0:T(8,128)(2,1)}, bf16[1024,1152]{1,0:T(8,128)(2,1)}, u32[]{:S(2)}, u32[]{:S(2)}) collective-permute-start(bf16[1024,1152]{1,0:T(8,128)(2,1)} %get-tuple-element.130), channel_id=1, source_target_pairs={{0,1},{1,0},{2,3},{3,2},{4,5},{5,4},{6,7},{7,6},{8,9},{9,8},{10,11... | collective-permute-start | bytes 7077896 | tf_op jit(solution)/shard_map/ppermute | solution.py:19
  197.3 11.1 %copy-start.11 = (bf16[1024,1152]{1,0:T(8,128)(2,1)S(1)}, bf16[1024,1152]{1,0:T(8,128)(2,1)}, u32[]{:S(2)}) copy-start(bf16[1024,1152]{1,0:T(8,128)(2,1)} %get-tuple-element.132) | copy-start | bytes 7077892
  210.0 28.5 %collective-permute-start.15 = (bf16[512,1152]{1,0:T(8,128)(2,1)S(1)}, bf16[512,1152]{1,0:T(8,128)(2,1)}, u32[]{:S(2)}, u32[]{:S(2)}) collective-permute-start(bf16[512,1152]{1,0:T(8,128)(2,1)S(1)} %add_convert_fusion.5), channel_id=1, source_target_pairs={{0,16},{16,0},{1,17},{17,1},{2,18},{18,2},{3,19},{19,3},{4,20},{20... | collective-permute-start | bytes 3538952 | tf_op jit(solution)/shard_map/ppermute | solution.py:24
  210.8 25.1 %collective-permute-start.14 = (bf16[512,1024]{1,0:T(8,128)(2,1)S(1)}, bf16[512,1024]{1,0:T(8,128)(2,1)}, u32[]{:S(2)}, u32[]{:S(2)}) collective-permute-start(bf16[512,1024]{1,0:T(8,128)(2,1)S(1)} %copy-done.20), channel_id=1, source_target_pairs={{0,2},{2,0},{1,3},{3,1},{4,6},{6,4},{5,7},{7,5},{8,10},{10,8},{9,1... | collective-permute-start | bytes 3145736 | tf_op jit(solution)/shard_map/ppermute | solution.py:19
  238.5 9.0 %collective-permute-start.16 = (bf16[1024,1152]{1,0:T(8,128)(2,1)}, bf16[1024,1152]{1,0:T(8,128)(2,1)}, u32[]{:S(2)}, u32[]{:S(2)}) collective-permute-start(bf16[1024,1152]{1,0:T(8,128)(2,1)} %get-tuple-element.143), channel_id=1, source_target_pairs={{0,1},{1,0},{2,3},{3,2},{4,5},{5,4},{6,7},{7,6},{8,9},{9,8},{10,11... | collective-permute-start | bytes 7077896 | tf_op jit(solution)/shard_map/ppermute | solution.py:19
  250.1 33.1 %all-to-all-start.1 = ((bf16[4,128,1152]{2,1,0:T(8,128)(2,1)}), bf16[4,128,1152]{2,1,0:T(8,128)(2,1)S(1)}, u32[]{:S(2)}, u32[]{:S(2)}) async-start(bf16[4,128,1152]{2,1,0:T(8,128)(2,1)} %bitcast.15), calls=%async_computation.1 | async-start | bytes 2359296 | tf_op jit(solution)/shard_map/all_to_all | solution.py:81
  254.0 29.8 %collective-permute-start.18 = (bf16[512,1152]{1,0:T(8,128)(2,1)}, bf16[512,1152]{1,0:T(8,128)(2,1)}, u32[]{:S(2)}, u32[]{:S(2)}) collective-permute-start(bf16[512,1152]{1,0:T(8,128)(2,1)} %add_convert_fusion.3), channel_id=1, source_target_pairs={{0,16},{16,0},{1,17},{17,1},{2,18},{18,2},{3,19},{19,3},{4,20},{20... | collective-permute-start | bytes 3538952 | tf_op jit(solution)/shard_map/ppermute | solution.py:24
  255.5 28.4 %collective-permute-start.17 = (bf16[512,1024]{1,0:T(8,128)(2,1)}, bf16[512,1024]{1,0:T(8,128)(2,1)}, u32[]{:S(2)}, u32[]{:S(2)}) collective-permute-start(bf16[512,1024]{1,0:T(8,128)(2,1)} %add_convert_fusion.8.own), channel_id=1, source_target_pairs={{0,2},{2,0},{1,3},{3,1},{4,6},{6,4},{5,7},{7,5},{8,10},{10,8},{9,1... | collective-permute-start | bytes 3145736 | tf_op jit(solution)/shard_map/ppermute | solution.py:19
  283.9 8.6 %collective-permute-start.20 = (bf16[1024,1152]{1,0:T(8,128)(2,1)}, bf16[1024,1152]{1,0:T(8,128)(2,1)S(1)}, u32[]{:S(2)}, u32[]{:S(2)}) collective-permute-start(bf16[1024,1152]{1,0:T(8,128)(2,1)} %get-tuple-element.158), channel_id=1, source_target_pairs={{0,1},{1,0},{2,3},{3,2},{4,5},{5,4},{6,7},{7,6},{8,9},{9,8},{10,11... | collective-permute-start | bytes 7077896 | tf_op jit(solution)/shard_map/ppermute | solution.py:19
  288.0 6.4 %collective-permute-start.19 = (bf16[2,2,256]{2,1,0:T(2,128)(2,1)S(1)}, bf16[2,2,256]{2,1,0:T(2,128)(2,1)S(1)}, u32[]{:S(2)}, u32[]{:S(2)}) collective-permute-start(bf16[2,2,256]{2,1,0:T(2,128)(2,1)S(1)} %fusion), channel_id=1, source_target_pairs={{1,0},{4,1},{5,4},{8,5},{9,8},{12,9},{13,12},{3,2},{6,3},{7,6},{10... | collective-permute-start | bytes 6152 | tf_op jit(solution)/shard_map/ppermute | solution.py:738
  294.3 33.6 %all-to-all-start.2 = ((bf16[4,128,1152]{2,1,0:T(8,128)(2,1)}), bf16[4,128,1152]{2,1,0:T(8,128)(2,1)S(1)}, u32[]{:S(2)}, u32[]{:S(2)}) async-start(bf16[4,128,1152]{2,1,0:T(8,128)(2,1)} %bitcast.21), calls=%async_computation.2 | async-start | bytes 2359296 | tf_op jit(solution)/shard_map/all_to_all | solution.py:81
  298.8 28.7 %collective-permute-start.21 = (bf16[512,1152]{1,0:T(8,128)(2,1)}, bf16[512,1152]{1,0:T(8,128)(2,1)}, u32[]{:S(2)}, u32[]{:S(2)}) collective-permute-start(bf16[512,1152]{1,0:T(8,128)(2,1)} %add_convert_fusion.1), channel_id=1, source_target_pairs={{0,16},{16,0},{1,17},{17,1},{2,18},{18,2},{3,19},{19,3},{4,20},{20... | collective-permute-start | bytes 3538952 | tf_op jit(solution)/shard_map/ppermute | solution.py:24
  300.3 29.3 %copy-start.31 = (f32[1024]{0:T(1024)S(1)}, f32[1024]{0:T(1024)}, u32[]{:S(2)}) copy-start(f32[1024]{0:T(1024)} %param.17) | copy-start | bytes 12292
  327.9 7.9 %collective-permute-start.23 = (bf16[1024,1024]{1,0:T(8,128)(2,1)}, bf16[1024,1024]{1,0:T(8,128)(2,1)S(1)}, u32[]{:S(2)}, u32[]{:S(2)}) collective-permute-start(bf16[1024,1024]{1,0:T(8,128)(2,1)} %get-tuple-element.174), channel_id=1, source_target_pairs={{0,1},{1,0},{2,3},{3,2},{4,5},{5,4},{6,7},{7,6},{8,9},{9,8},{10,11... | collective-permute-start | bytes 6291464 | tf_op jit(solution)/shard_map/ppermute | solution.py:19
  330.4 1.8 collective-permute-start.22
  337.5 32.9 %all-to-all-start.3 = ((bf16[4,128,1152]{2,1,0:T(8,128)(2,1)}), bf16[4,128,1152]{2,1,0:T(8,128)(2,1)S(1)}, u32[]{:S(2)}, u32[]{:S(2)}) async-start(bf16[4,128,1152]{2,1,0:T(8,128)(2,1)} %bitcast.27), calls=%async_computation.3 | async-start | bytes 2359296 | tf_op jit(solution)/shard_map/all_to_all | solution.py:81
  341.6 27.7 %collective-permute-start.24 = (bf16[1024,512]{1,0:T(8,128)(2,1)}, bf16[1024,512]{1,0:T(8,128)(2,1)}, u32[]{:S(2)}, u32[]{:S(2)}) collective-permute-start(bf16[1024,512]{1,0:T(8,128)(2,1)} %get-tuple-element.175), channel_id=1, source_target_pairs={{0,2},{2,0},{1,3},{3,1},{4,6},{6,4},{5,7},{7,5},{8,10},{10,8},{9,1... | collective-permute-start | bytes 3145736 | tf_op jit(solution)/shard_map/ppermute | solution.py:19
  343.1 26.2 %collective-permute-start.28 = (bf16[512,1024]{1,0:T(8,128)(2,1)}, bf16[512,1024]{1,0:T(8,128)(2,1)}, u32[]{:S(2)}, u32[]{:S(2)}) collective-permute-start(bf16[512,1024]{1,0:T(8,128)(2,1)} %add_convert_fusion.7), channel_id=1, source_target_pairs={{0,16},{16,0},{1,17},{17,1},{2,18},{18,2},{3,19},{19,3},{4,20},{20... | collective-permute-start | bytes 3145736 | tf_op jit(solution)/shard_map/ppermute | solution.py:24
  346.0 21.7 %collective-permute-start.25 = (f32[5,1024]{1,0:T(8,128)S(1)}, f32[5,1024]{1,0:T(8,128)S(1)}, u32[]{:S(2)}, u32[]{:S(2)}) collective-permute-start(f32[5,1024]{1,0:T(8,128)S(1)} %fusion.2), channel_id=1, source_target_pairs={{0,2},{2,0},{1,3},{3,1},{4,6},{6,4},{5,7},{7,5},{8,10},{10,8},{9,1... | collective-permute-start | bytes 61448 | tf_op jit(solution)/shard_map/ppermute | solution.py:19
  346.3 22.7 %collective-permute-start.26 = (f32[5,1024]{1,0:T(8,128)S(1)}, f32[5,1024]{1,0:T(8,128)S(1)}, u32[]{:S(2)}, u32[]{:S(2)}) collective-permute-start(f32[5,1024]{1,0:T(8,128)S(1)} %fusion.2), channel_id=1, source_target_pairs={{0,16},{16,0},{1,17},{17,1},{2,18},{18,2},{3,19},{19,3},{4,20},{20... | collective-permute-start | bytes 61448 | tf_op jit(solution)/shard_map/ppermute | solution.py:19
  346.9 22.4 %collective-permute-start.27 = (f32[5,1024]{1,0:T(8,128)S(1)}, f32[5,1024]{1,0:T(8,128)S(1)}, u32[]{:S(2)}, u32[]{:S(2)}) collective-permute-start(f32[5,1024]{1,0:T(8,128)S(1)} %fusion.2), channel_id=1, source_target_pairs={{0,18},{2,16},{16,2},{18,0},{1,19},{3,17},{17,3},{19,1},{4,22},{6,... | collective-permute-start | bytes 61448 | tf_op jit(solution)/shard_map/ppermute | solution.py:773
  350.4 21.6 %copy-start.14 = (bf16[1024,1024]{1,0:T(8,128)(2,1)S(1)}, bf16[1024,1024]{1,0:T(8,128)(2,1)}, u32[]{:S(2)}) copy-start(bf16[1024,1024]{1,0:T(8,128)(2,1)} %get-tuple-element.173) | copy-start | bytes 6291460
  370.4 24.5 %collective-permute-start.29 = (bf16[1024,512]{1,0:T(8,128)(2,1)}, bf16[1024,512]{1,0:T(8,128)(2,1)}, u32[]{:S(2)}, u32[]{:S(2)}) collective-permute-start(bf16[1024,512]{1,0:T(8,128)(2,1)} %get-tuple-element.182), channel_id=1, source_target_pairs={{0,2},{2,0},{1,3},{3,1},{4,6},{6,4},{5,7},{7,5},{8,10},{10,8},{9,1... | collective-permute-start | bytes 3145736 | tf_op jit(solution)/shard_map/ppermute | solution.py:19
  375.4 32.2 %all-to-all-start.4 = ((bf16[4,144,1024]{2,1,0:T(8,128)(2,1)}), bf16[4,144,1024]{2,1,0:T(8,128)(2,1)}, u32[]{:S(2)}, u32[]{:S(2)}) async-start(bf16[4,144,1024]{2,1,0:T(8,128)(2,1)} %pad_maximum_fusion.1), calls=%async_computation.4 | async-start | bytes 2359296 | tf_op jit(solution)/shard_map/all_to_all | solution.py:81
  382.4 12.5 %copy-start.16 = (f32[1024,512]{1,0:T(8,128)S(1)}, f32[1024,512]{1,0:T(8,128)}, u32[]{:S(2)}) copy-start(f32[1024,512]{1,0:T(8,128)} %get-tuple-element.153) | copy-start | bytes 6291460
  382.5 15.6 %collective-permute-start.31 = (f32[1024,256]{1,0:T(8,128)S(1)}, f32[1024,256]{1,0:T(8,128)S(1)}, u32[]{:S(2)}, u32[]{:S(2)}) collective-permute-start(f32[1024,256]{1,0:T(8,128)S(1)} %get-tuple-element.237), channel_id=1, source_target_pairs={{0,1},{1,0},{2,3},{3,2},{4,5},{5,4},{6,7},{7,6},{8,9},{9,8},{10,11... | collective-permute-start | bytes 3145736 | tf_op jit(solution)/shard_map/ppermute | solution.py:19
  397.1 2.6 collective-permute-start.30
  (26 other events, 115.2 us)
Sparse Core Ops, SparseCore 0:
  43.3 115.8 all-gather.1

commit v3 on v2

--- a/solution.py
+++ b/solution.py
@@ -87,10 +87,14 @@
     return total([got[i * size : (i + 1) * size] for i in range(steps)])
 
 
-def add_dp(own, other, arrived):
-    size = arrived[0].shape[0]
+def for_self(own, other):
+    size = own.shape[0] // lax.axis_size("dp")
     mine = [pick_rows(part, lax.axis_index("dp"), size) for part in (own, other)]
-    return total(mine + list(arrived)).astype(BF16)
+    return total(mine).astype(BF16)
+
+
+def add_dp(keep, arrived):
+    return total([keep, *arrived]).astype(BF16)
 
 
 def sum_over(value, axis):
@@ -104,7 +108,7 @@
     return value
 
 
-def hidden_kernel(h_own, h_other, cot, w_gate, w_up, w_down, h, hidden, d_gate, d_up):
+def hidden_kernel(scalars, h_own, h_other, cot, w_gate, w_up, w_down, h, *outs):
     features = h.shape[1]
     half = h_own.shape[0]
 
@@ -113,8 +117,12 @@
         h[:half, :] = h_own[...]
         h[half:, :] = h_other[...]
 
+    core = scalars[0]
+
     def both(w):
-        return jnp.concatenate([w[:, i].reshape(features, w.shape[3]) for i in (0, 1)], 1)
+        return jnp.concatenate(
+            [w[:, i].reshape(features, w.shape[3]) for i in (core, 1 - core)], 1
+        )
 
     w_gate, w_up, w_down = both(w_gate), both(w_up), both(w_down)
     width = w_gate.shape[1] // 2
@@ -126,17 +134,17 @@
         sigma = jax.nn.sigmoid(gate)
         silu = gate * sigma
         results = (
-            (hidden, silu * up),
-            (d_gate, d_hidden * up * sigma * (1.0 + gate * (1.0 - sigma))),
-            (d_up, d_hidden * silu),
+            silu * up,
+            d_hidden * up * sigma * (1.0 + gate * (1.0 - sigma)),
+            d_hidden * silu,
         )
-        for ref, value in results:
+        for i, value in enumerate(results):
             value = value.astype(BF16)
-            ref[0, part, :] = value[:, :width]
-            ref[1, part, :] = value[:, width:]
-
-
-def hidden_units(h_own, h_other, cot, weights):
+            outs[2 * i][part, :] = value[:, :width]
+            outs[2 * i + 1][part, :] = value[:, width:]
+
+
+def hidden_units(scalars, h_own, h_other, cot, weights):
     rows, features = cot.shape
     blocks, _, chunk, width = weights.shape
     width //= 3
@@ -144,28 +152,26 @@
     tiles = width // tile
 
     def of(matrix):
-        return pl.BlockSpec((blocks, 2, chunk, tile), lambda j: (0, 0, 0, matrix * tiles + j))
-
-    whole = pl.BlockSpec((rows, features), lambda j: (0, 0))
-    half = pl.BlockSpec((rows // 2, features), lambda j: (0, 0))
+        return pl.BlockSpec((blocks, 2, chunk, tile), lambda j, s: (0, 0, 0, matrix * tiles + j))
+
+    whole = pl.BlockSpec((rows, features), lambda j, s: (0, 0))
+    half = pl.BlockSpec((rows // 2, features), lambda j, s: (0, 0))
     return pl.pallas_call(
         hidden_kernel,
         out_shape=[jax.ShapeDtypeStruct((rows, features), BF16)]
-        + [jax.ShapeDtypeStruct((2, rows, width), BF16)] * 3,
-        grid=(tiles,),
-        in_specs=[half, half, whole, of(0), of(1), of(2)],
-        out_specs=[whole] + [pl.BlockSpec((2, rows, tile), lambda j: (0, 0, j))] * 3,
+        + [jax.ShapeDtypeStruct((rows, width), BF16)] * 6,
+        grid_spec=pltpu.PrefetchScalarGridSpec(
+            num_scalar_prefetch=1,
+            grid=(tiles,),
+            in_specs=[half, half, whole, of(0), of(1), of(2)],
+            out_specs=[whole] + [pl.BlockSpec((rows, tile), lambda j, s: (0, j))] * 6,
+        ),
         compiler_params=pltpu.CompilerParams(vmem_limit_bytes=VMEM_LIMIT),
-        cost_estimate=pl.CostEstimate(
-            flops=12 * rows * features * width,
-            bytes_accessed=4 * (rows * features + 3 * features * width + 3 * rows * width),
-            transcendentals=2 * rows * width,
-        ),
         name="hidden_units",
-    )(h_own, h_other, cot, weights, weights, weights)
-
-
-def run_jobs(name, scalars, jobs):
+    )(scalars, h_own, h_other, cot, weights, weights, weights)
+
+
+def run_jobs(name, scalars, jobs, limit=56):
     starts, steps = [], 0
     for job in jobs:
         starts.append(steps)
@@ -203,7 +209,7 @@
         grid_spec=pltpu.PrefetchScalarGridSpec(
             num_scalar_prefetch=1, grid=(steps,), in_specs=in_specs, out_specs=out_specs
         ),
-        compiler_params=pltpu.CompilerParams(vmem_limit_bytes=VMEM_LIMIT),
+        compiler_params=pltpu.CompilerParams(vmem_limit_bytes=limit * 2**20),
         name=name,
     )(scalars, *args)
 
@@ -214,6 +220,33 @@
         for i in (0, 1):
             result = result + nt(part[i], weight[:, i].reshape(width, weight.shape[3]))
     return result
+
+
+def sum_pairs(core, parts, weights, width):
+    result = 0.0
+    for i, weight in enumerate(weights):
+        for part, index in ((parts[2 * i], core), (parts[2 * i + 1], 1 - core)):
+            result = result + nt(part[...], weight[:, index].reshape(width, weight.shape[3]))
+    return result
+
+
+def hidden_back_job(pairs, weights, matrices, half):
+    blocks, _, chunk, _ = weights.shape
+    rows, width = pairs[0].shape
+    rows //= 2
+    features = blocks * chunk
+    tile = max(256, chunk)
+    inputs = [(part, (rows, width), lambda j, s: (half, 0)) for part in pairs] + [
+        (weights, (tile // chunk, 2, chunk, width), lambda j, s, m=m: (j, 0, 0, m))
+        for m in matrices
+    ]
+    count = len(pairs)
+
+    def work(j, s, ins, outs):
+        outs[0][...] = sum_pairs(s[0], ins[:count], ins[count:], tile).astype(BF16)
+
+    outputs = [((rows, features), BF16, (rows, tile), lambda j, s: (0, j))]
+    return features // tile, inputs, outputs, work
 
 
 def back_job(parts, weights, matrices, rows_of, dtype, divide=1, block_of=None):
@@ -277,7 +310,7 @@
 
 def made_job(hidden, weights, matrix, residual):
     blocks, _, chunk, _ = weights.shape
-    _, rows, width = hidden.shape
+    rows, width = hidden[0].shape
     features = blocks * chunk
     tile = max(256, chunk)
     steps = features // tile
@@ -287,8 +320,7 @@
     def at(j, s):
         return jnp.where(j < part, (1 - s[1]) * part + j, s[1] * part + j - part)
 
-    inputs = [
-        (hidden, (2, rows, width), lambda j, s: (0, 0, 0)),
+    inputs = [(value, (rows, width), lambda j, s: (0, 0)) for value in hidden] + [
         (weights, (tile // chunk, 2, chunk, width), lambda j, s: (at(j, s), 0, 0, matrix)),
         (residual, (height, tile), lambda j, s: (0, at(j, s))),
     ]
@@ -298,32 +330,43 @@
     ]
 
     def work(j, s, ins, outs):
-        result = sum_through(ins[:1], ins[1:2], tile)
+        result = sum_pairs(s[0], ins[:2], ins[2:3], tile)
         for out, mine in zip(outs, (j < part, j >= part)):
 
             @pl.when(mine)
             def _(out=out):
-                out[:height, :] = (result[:height] + ins[2][...]).astype(out.dtype)
+                out[:height, :] = (result[:height] + ins[3][...]).astype(out.dtype)
                 out[height:, :] = result[height:].astype(out.dtype)
 
     return steps, inputs, outputs, work
 
 
-def pair_job(left, right):
-    rows, features = left.shape
-    width = right.shape[2]
-    tile = 256
+def gradient_job(lefts, rights, devices):
+    rows, features = lefts[0].shape
+    width = rights[0].shape[1]
+    size = features // devices
+    tile = min(256, size)
+    steps, mine = features // tile, size // tile
     inputs = [
-        (left, (rows, tile), lambda j, s: (0, j)),
-        (right, (2, rows, width), lambda j, s: (0, 0, 0)),
-    ]
-    outputs = [((features, width), BF16, (tile, width), lambda j, s: (j, 0))] * 2
+        (left, (rows, tile), lambda j, s: (0, lax.rem(s[2] * mine + j, steps))) for left in lefts
+    ] + [(right, (rows, width), lambda j, s: (0, 0)) for right in rights]
+    outputs = [
+        ((size, width), BF16, (tile, width), lambda j, s: (jnp.minimum(j, mine - 1), 0)),
+        ((features - size, width), BF16, (tile, width), lambda j, s: (jnp.maximum(j - mine, 0), 0)),
+    ]
 
     def work(j, s, ins, outs):
-        for i, index in enumerate((s[0], 1 - s[0])):
-            outs[i][...] = tn(ins[0][...], ins[1][index]).astype(BF16)
-
-    return features // tile, inputs, outputs, work
+        made = (tn(ins[0][...], ins[2][...]) + tn(ins[1][...], ins[3][...])).astype(BF16)
+
+        @pl.when(j < mine)
+        def _():
+            outs[0][...] = made
+
+        @pl.when(j >= mine)
+        def _():
+            outs[1][...] = made
+
+    return steps, inputs, outputs, work
 
 
 def norm_job(full, gain):
@@ -655,20 +698,21 @@
         first = lax.all_gather(both_cores(first_tok), "dp", axis=0, tiled=True)
 
     _, full = join_mp(*pieces)
-    h_mix, inverse_mix = run_jobs("norm", scalars, [norm_job(full, gain_row)])
+    h_mix, inverse_mix = run_jobs("norm", scalars, [norm_job(full, gain_row)], 12)
     if nx == 2:
         first_dp, first_tok, h_mix, *pieces_cot = tie(first_dp, first_tok, h_mix, *pieces_cot)
         first = by_rank(x, first_tok, both_cores(first_dp))
     _, cot = join_mp(*pieces_cot)
     cot = jnp.concatenate([pick_rows(cot, y, half), pick_rows(cot, 1 - y, half)], 0)
+    cot, cot_beside = tie(cot, swap(cot, "c"))
 
     ranks = nz * 2
-    [gated] = run_jobs("tail", scalars, [tail_job(h_mix, first, width)])
+    [gated] = run_jobs("tail", scalars, [tail_job(h_mix, first, width)], 16)
     edge = lax.ppermute(gated[:, -2:], ("tok", "c"), [(i, i + 1) for i in range(ranks - 1)])
-    [proj] = run_jobs("project", scalars, [project_job(h_mix, first, width)])
+    [proj] = run_jobs("project", scalars, [project_job(h_mix, first, width)], 20)
     gate_c = proj[:, :8, width : 2 * width]
     edge, proj = tie(edge, proj)
-    mixed_in, sent = run_jobs("mix", scalars, [mix_job(proj, edge, taps, first)])
+    mixed_in, sent = run_jobs("mix", scalars, [mix_job(proj, edge, taps, first)], 28)
 
     def own_rows(s):
         return s[1]
@@ -678,68 +722,81 @@
 
     arrived = swap(sent, "y")
     [kept] = run_jobs(
-        "project_out", scalars, [back_job((mixed_in,), first, (3,), own_rows, F32)]
-    )
+        "project_out", scalars, [back_job((mixed_in,), first, (3,), own_rows, F32)], 20
+    )
+    w_out = [first[:, i, :, 3 * width :].reshape(features, width) for i in (0, 1)]
+    arrived, kept, *w_out = tie(arrived, kept, *w_out)
     residual = pick_rows(full, y, half).astype(F32) + kept + arrived.astype(F32)
 
     inverse_ffn = lax.rsqrt(jnp.mean(residual * residual, -1, keepdims=True) + EPS)
     normalized = residual * inverse_ffn
     h_own = (normalized * gain_ffn).astype(BF16)
-    h, hidden, d_gate, d_up = hidden_units(h_own, swap(h_own, "y"), cot, weights)
+    h, *units = hidden_units(scalars, h_own, swap(h_own, "y"), cot, weights)
+    hidden, d_gate, d_up = units[:2], units[2:4], units[4:]
 
     def of_core(other):
         return swap(other, "c")
 
-    down_own, down_other = run_jobs("down_gradient", scalars, [pair_job(cot, hidden)])
-    d_gate, d_up, down_own, down_other = tie(d_gate, d_up, down_own, down_other)
-    both = (d_gate, d_up)
-    down_other = of_core(down_other)
+    def pieces_of(send):
+        size = features // nx
+        return to_dp([send[i * size : (i + 1) * size] for i in range(nx - 1)])
+
+    hidden_beside, h_beside = of_core(hidden[1]), of_core(h)
     [sent] = run_jobs(
-        "back_hidden", scalars, [back_job(both, weights, (0, 1), lambda s: 1, BF16)]
-    )
-    sent, down_own, down_other = tie(sent, down_own, down_other)
-
-    late_gate, sent, *pieces = tie(d_gate, sent, *for_dp(down_own, down_other))
-    arrived, pieces = swap(sent, "y"), to_dp(pieces)
-    own, other, kept = run_jobs(
+        "back_hidden", scalars, [hidden_back_job([*d_gate, *d_up], weights, (0, 1), 1)]
+    )
+    sent, hidden_beside, h_beside, *units = tie(sent, hidden_beside, h_beside, *hidden, *d_gate, *d_up)
+    hidden, d_gate, d_up = units[:2], units[2:4], units[4:]
+    gate_beside, up_beside = of_core(d_gate[1]), of_core(d_up[1])
+    keep, send = run_jobs(
+        "down_gradient",
+        scalars,
+        [gradient_job([cot, cot_beside], [hidden[0], hidden_beside], nx)],
+    )
+    sent, keep, send, gate_beside, up_beside, *units = tie(
+        sent, keep, send, gate_beside, up_beside, *hidden, *d_gate, *d_up
+    )
+    hidden, d_gate, d_up = units[:2], units[2:4], units[4:]
+    arrived, pieces = swap(sent, "y"), pieces_of(send)
+    next_keep, send, kept = run_jobs(
         "gate_gradient",
         scalars,
-        [pair_job(h, late_gate), back_job(both, weights, (0, 1), lambda s: 0, F32)],
-    )
-    arrived, own, other, *pieces = tie(arrived, own, other, *pieces)
-    other = of_core(other)
-    d_h = kept + arrived.astype(F32)
+        [
+            gradient_job([h, h_beside], [d_gate[0], gate_beside], nx),
+            hidden_back_job([*d_gate, *d_up], weights, (0, 1), 0),
+        ],
+    )
+    arrived, send, kept, *pieces = tie(arrived, send, kept, *pieces)
+    d_h = kept.astype(F32) + arrived.astype(F32)
     grad_gain_ffn = jnp.sum(d_h * normalized, 0)
     scaled = d_h * gain_ffn
     d_res = cot[:half].astype(F32) + inverse_ffn * (
         scaled - normalized * jnp.mean(scaled * normalized, -1, keepdims=True)
     )
     d_res_own = d_res.astype(BF16)
-    down_mine = add_dp(down_own, down_other, pieces)
-    late_up, late_hidden, d_res_own, down_mine, *pieces = tie(
-        d_up, hidden, d_res_own, down_mine, *for_dp(own, other)
-    )
-    arrived, down_got, pieces = swap(d_res_own, "y"), to_tok(down_mine), to_dp(pieces)
-    up_own, up_other, made_sent, made_kept = run_jobs(
+    down_mine = add_dp(keep, pieces)
+    d_res_own, down_mine, send, *units = tie(d_res_own, down_mine, send, *hidden, *d_up)
+    hidden, d_up = units[:2], units[2:]
+    arrived, down_got, pieces = swap(d_res_own, "y"), to_tok(down_mine), pieces_of(send)
+    keep, send, made_sent, made_kept = run_jobs(
         "up_gradient",
         scalars,
-        [pair_job(h, late_up), made_job(late_hidden, weights, 2, residual)],
-    )
-    arrived, up_own, up_other, made_sent, made_kept, down_got, *pieces = tie(
-        arrived, up_own, up_other, made_sent, made_kept, down_got, *pieces
-    )
-    up_other = of_core(up_other)
-    gate_mine = add_dp(own, other, pieces)
+        [
+            gradient_job([h, h_beside], [d_up[0], up_beside], nx),
+            made_job(hidden, weights, 2, residual),
+        ],
+    )
+    arrived, send, made_sent, made_kept, down_got, *pieces = tie(
+        arrived, send, made_sent, made_kept, down_got, *pieces
+    )
+    gate_mine = add_dp(next_keep, pieces)
 
     head = jnp.where(y == 0, d_res_own[:8], arrived[:8])
-    w_out = first[:, :, :, 3 * width :]
-    d_head = jnp.stack([nn(head, w_out[:, i].reshape(features, width)) for i in (0, 1)])
+    d_head = jnp.stack([nn(head, w) for w in w_out])
     d_head = (d_head * gate_c).astype(BF16)[:, :2]
     later = lax.ppermute(d_head, ("tok", "c"), [(i + 1, i) for i in range(ranks - 1)])
-    arrived, gate_mine, later, *pieces = tie(
-        arrived, gate_mine, later, *for_dp(up_own, up_other)
-    )
-    gate_got, pieces = to_tok(gate_mine), to_dp(pieces)
+    arrived, gate_mine, later, send = tie(arrived, gate_mine, later, send)
+    gate_got, pieces = to_tok(gate_mine), pieces_of(send)
     d_res_full, d_proj, dots, grad_taps, own, other, gain_dots, sent = mixer_back(
         scalars,
         d_res_own,
@@ -755,19 +812,20 @@
         inverse_mix,
         gain_row,
     )
+    d_proj, own, other, sent, gate_got, *pieces = tie(
+        d_proj, own, other, sent, gate_got, *pieces
+    )
+    other = of_core(other)
+    up_mine = add_dp(keep, pieces)
+    sent, d_proj, up_mine, grad_taps, gain_dots, own, other, *pieces = tie(
+        sent, d_proj, up_mine, grad_taps, gain_dots, own, other, *for_dp(own, other)
+    )
+    arrived, up_got, pieces = swap(sent, "y"), to_tok(up_mine), to_dp(pieces)
     near_sums = jnp.concatenate([grad_taps[0, :3], grad_taps[1, :3]], 1)
     sums = lax.dynamic_update_slice(jnp.zeros((3, features), F32), near_sums, (0, y * pair))
     gain_sum = gain_dots[:, 0] / mixer_norm_gain
     sums = jnp.concatenate([sums, gain_sum[None], grad_gain_ffn[None]], 0)
-    d_proj, own, other, sent, gate_got, *pieces = tie(
-        d_proj, own, other, sent, gate_got, *pieces
-    )
-    other, sums = of_core(other), sum_over(sums, "c")
-    up_mine = add_dp(up_own, up_other, pieces)
-    sent, d_proj, up_mine, sums, *pieces = tie(
-        sent, d_proj, up_mine, sums, *for_dp(own, other)
-    )
-    arrived, up_got, pieces = swap(sent, "y"), to_tok(up_mine), to_dp(pieces)
+    sums = sum_over(sums, "c")
     if nx == 2:
         cross = [(2 * i + j, 2 * (1 - i) + 1 - j) for i in (0, 1) for j in (0, 1)]
         near, far = swap(sums, "y"), lax.ppermute(sums, ("dp", "y"), cross)
@@ -779,9 +837,11 @@
         scalars,
         [back_in_job(d_proj, first, full, inverse_mix, dots, gain_row, own_rows, F32)],
     )
-    arrived, kept, up_got, sums, *pieces = tie(arrived, kept, up_got, sums, *pieces)
+    arrived, kept, up_got, sums, keep, *pieces = tie(
+        arrived, kept, up_got, sums, for_self(own, other), *pieces
+    )
     sums = (sums[0] + sums[1]) + (sums[2] + sums[3]) if nx == 2 else sums[0]
-    mixer_mine = add_dp(own, other, pieces)
+    mixer_mine = add_dp(keep, pieces)
 
     high = sums.astype(BF16)
     low = (sums - high.astype(F32)).astype(BF16)

time: 422 us -> 406 us (0.962)
  other arithmetic: 58.6 us -> 44.9 us
  Pallas kernels: 142 us -> 129 us
  waiting for transfers between devices: 133 us -> 142 us
    pallas_call x10, Pallas kernels: 99 us -> 84.8 us  [run_jobs(): pl.pallas_call(kernel, out_shape=shapes, grid_spec=pltpu.PrefetchScalarGr...]
    ppermute x22 -> x24, waiting for transfers between devices: 86.3 us -> 93.3 us  [swap(): return lax.ppermute(value, axis, [(0, 1), (1, 0)])]
    all_gather x1, waiting for transfers between devices: 0.01 us -> 6.59 us  [gather(): whole = lax.all_gather(shard, every, axis=0, tiled=True)]
    convert_element_type x4 -> x1, other arithmetic: 7.25 us -> 2.57 us  [for_dp(): total([pick_rows(part, index, size) for part in (own, other)]).astype(BF16)]
    unnamed x79 -> x111, local copies, waits for them, and re-layouts: 6.26 us -> 10.8 us
    ppermute x22 -> x24, starting transfers between devices: 14.5 us -> 17.8 us  [swap(): return lax.ppermute(value, axis, [(0, 1), (1, 0)])]
    convert_element_type x4 -> x5, other arithmetic: 12.1 us -> 10.3 us  [the longest x4 8.66 us: add_dp(): return total([keep, *arrived]).astype(BF16)]
  transfers between devices with their start and end apart: 38 -> 40, of which waited for: 18 -> 19; matrix products, arithmetic and copies ran while one was open for 15% -> 11% of each run, Pallas kernels for 26% -> 26%
where the time goes in v3:
time: 406 us; the launch traced here: 404 us
  waiting for transfers between devices  142 us (35%)
  Pallas kernels  129 us (32%)
  starting transfers between devices  50 us (12%)
  other arithmetic  44.9 us (11%)
  local copies, waits for them, and re-layouts  21.5 us (5%)
  between operations  14.8 us (4%)
    ppermute x24, waiting for transfers between devices, swap(): return lax.ppermute(value, axis, [(0, 1), (1, 0)])  93.3 us
    pallas_call x10, Pallas kernels, run_jobs(): pl.pallas_call(kernel, out_shape=shapes, grid_spec=pltpu.PrefetchScalarGr...  84.8 us
    pallas_call x1, Pallas kernels, hidden_units(): pl.pallas_call(hidden_kernel, out_shape=[jax.ShapeDtypeStruct((rows, feat...  22.7 us
    pallas_call x1, Pallas kernels, mixer_back(): pl.pallas_call(mixer_back_kernel, out_shape=[jax.ShapeDtypeStruct((rows,...  21.2 us
    all_to_all x1, waiting for transfers between devices, body(): lax.all_to_all(jnp.concatenate([first] * nz, 0), 'tok', split_axis=0, con...  20.6 us
    ppermute x24, starting transfers between devices, swap(): return lax.ppermute(value, axis, [(0, 1), (1, 0)])  17.8 us
    all_to_all x4, starting transfers between devices, to_tok(): return lax.all_to_all(mine, 'tok', split_axis=0, concat_axis=0, tiled=True)  16.3 us
    select_n x11, other arithmetic, by_rank(): jnp.where(index == 0, jnp.concatenate([first, second], axis), jnp.concate...  13.7 us
  transfers between devices with their start and end apart: 40, of which 19 were waited for; matrix products, arithmetic and copies ran while one was open for 11% of the time, Pallas kernels for 26%

profile of v3, /device:TPU:0, one launch (start us, length us, event | category | flops | bytes accessed | tf_op | source)
XLA Modules:
  0.0 404.4 jit_solution(16053202753799075511)
XLA Ops:
  8.4 2.1 copy_bitcast_fusion
  10.4 6.4 %all-to-all-start = ((bf16[4,128,1024]{1,2,0:T(8,128)(2,1)}), bf16[4,128,1024]{1,2,0:T(8,128)(2,1)S(1)}, u32[]{:S(2)}, u32[]{:S(2)}) async-start(bf16[4,128,1024]{1,2,0:T(8,128)(2,1)} %copy_bitcast_fusion), calls=%async_computation | async-start | bytes 2097152 | tf_op jit(solution)/shard_map/all_to_all | solution.py:680
  19.9 2.1 pad_maximum_fusion.2
  22.0 20.6 %all-to-all-done = bf16[4,128,1024]{1,2,0:T(8,128)(2,1)S(1)} async-done(((bf16[4,128,1024]{1,2,0:T(8,128)(2,1)}), bf16[4,128,1024]{1,2,0:T(8,128)(2,1)S(1)}, u32[]{:S(2)}, u32[]{:S(2)}) %all-to-all-start) | async-done | bytes 1048608 | tf_op jit(solution)/shard_map/all_to_all | solution.py:680
  48.0 2.0 maximum_select_fusion.6
  54.3 3.9 maximum_select_fusion.1
  58.2 13.2 %collective-permute-done.6 = bf16[1024,256]{1,0:T(8,128)(2,1)S(1)} collective-permute-done((bf16[1024,256]{1,0:T(8,128)(2,1)S(1)}, bf16[1024,256]{1,0:T(8,128)(2,1)S(1)}, u32[]{:S(2)}, u32[]{:S(2)}) %collective-permute-start.6) | collective-permute-done | bytes 524320 | tf_op jit(solution)/shard_map/ppermute | solution.py:19
  71.5 7.9 %collective-permute-done.3 = bf16[512,1024]{1,0:T(8,128)(2,1)} collective-permute-done((bf16[512,1024]{1,0:T(8,128)(2,1)}, bf16[512,1024]{1,0:T(8,128)(2,1)}, u32[]{:S(2)}, u32[]{:S(2)}) %collective-permute-start.3) | collective-permute-done | bytes 1048608 | tf_op jit(solution)/shard_map/ppermute | solution.py:19
  79.9 2.4 collective-permute-done.9
  82.3 2.0 maximum_select_fusion.4
  87.5 2.2 collective-permute-start.10
  89.7 6.0 %project.1.refs_0_.proj = f32[2,1024,768]{2,1,0:T(8,128)S(1)} custom-call(s32[3]{0:T(128)S(1)} %pad_add_fusion.scalars_ref.scalars, bf16[1024,1024]{1,0:T(8,128)(2,1)S(1)} %copy-done.4, bf16[8,2,128,1024]{3,2,1,0:T(8,128)(2,1)S(1)} %maximum_select_fusion.refs_1_.refs_2_.refs_3_.w_out.w_in), custom_call_target="tpu_custom_call" | custom-call | tf_op jit(solution)/shard_map/project/pallas_call | solution.py:206
  95.8 3.2 mix.1
  99.0 1.6 collective-permute-start.12
  104.3 2.3 project_out.1
  106.6 18.4 %collective-permute-done.12 = bf16[512,1024]{1,0:T(8,128)(2,1)S(1)} collective-permute-done((bf16[512,1024]{1,0:T(8,128)(2,1)S(1)}, bf16[512,1024]{1,0:T(8,128)(2,1)S(1)}, u32[]{:S(2)}, u32[]{:S(2)}) %collective-permute-start.12) | collective-permute-done | bytes 1048608 | tf_op jit(solution)/shard_map/ppermute | solution.py:19
  127.1 1.6 collective-permute-start.13
  130.1 22.5 %collective-permute-done.13.h_other = bf16[512,1024]{1,0:T(8,128)(2,1)S(1)} collective-permute-done((bf16[512,1024]{1,0:T(8,128)(2,1)S(1)}, bf16[512,1024]{1,0:T(8,128)(2,1)S(1)}, u32[]{:S(2)}, u32[]{:S(2)}) %collective-permute-start.13) | collective-permute-done | bytes 1048608 | tf_op jit(solution)/shard_map/ppermute | solution.py:19
  152.6 6.6 %all-gather.2.cloned.1.call-done = bf16[2048,3456]{1,0:T(8,128)(2,1)} async-done(((bf16[128,3456]{1,0:T(8,128)(2,1)}), bf16[2048,3456]{1,0:T(8,128)(2,1)}) %all-gather.2.cloned.1.call-update) | async-done | bytes 14155792 | tf_op jit(solution)/shard_map/all_gather | solution.py:676
  159.2 22.7 %hidden_units.1 = (bf16[1024,1024]{1,0:T(8,128)(2,1)}, bf16[1024,1152]{1,0:T(8,128)(2,1)}, bf16[1024,1152]{1,0:T(8,128)(2,1)}, bf16[1024,1152]{1,0:T(8,128)(2,1)...) custom-call(s32[3]{0:T(128)} %copy-done.8, bf16[512,1024]{1,0:T(8,128)(2,1)} %copy-done.23, ...), custom_call_target="tpu_custom_call" | custom-call | tf_op jit(solution)/shard_map/hidden_units/pallas_call | solution.py:159
  182.5 11.4 %back_hidden.1 = bf16[512,1024]{1,0:T(8,128)(2,1)} custom-call(s32[3]{0:T(128)} %copy-done.8, bf16[1024,1152]{1,0:T(8,128)(2,1)} %get-tuple-element.167.refs_0_.refs_2_.refs_4_, bf16[1024,1152]{1,0:T(8,128)(2,1)} %get-tuple-element.169.refs_1_.refs_5_, bf16[1024,1152]{1,0:T(8,128)(2,1)} %get-tuple-element.183.refs_2_.refs_6_, ...), custom_call_target="tpu_custom_call" | custom-call | tf_op jit(solution)/shard_map/back_hidden/pallas_call | solution.py:206
  194.5 11.2 %down_gradient.1 = (bf16[512,1152]{1,0:T(8,128)(2,1)}, bf16[512,1152]{1,0:T(8,128)(2,1)}) custom-call(s32[3]{0:T(128)} %copy-done.8, bf16[1024,1024]{1,0:T(8,128)(2,1)} %copy-done.15, bf16[1024,1024]{1,0:T(8,128)(2,1)} %copy-done.25, bf16[1024,1152]{1,0:T(8,128)(2,1)} %get-tuple-element.185.refs_2_.refs_4_, bf16[1024,1152]{1,0:T(8,128)(2,1)} %collective-permute-done.14.refs_3_), custom_call_target="tpu_custom_call" | custom-call | tf_op jit(solution)/shard_map/down_gradient/pallas_call | solution.py:206
  207.9 20.1 %gate_gradient.1 = (bf16[512,1152]{1,0:T(8,128)(2,1)}, bf16[512,1152]{1,0:T(8,128)(2,1)}, bf16[512,1024]{1,0:T(8,128)(2,1)}) custom-call(s32[3]{0:T(128)} %copy-done.8, bf16[1024,1024]{1,0:T(8,128)(2,1)} %get-tuple-element.152.refs_0_, bf16[1024,1024]{1,0:T(8,128)(2,1)} %copy-done.19, bf16[1024,1152]{1,0:T(8,128)(2,1)} %get-tuple-element.167.refs_0_.refs_2_.refs_4_, ...), custom_call_target="tpu_custom_call" | custom-call | tf_op jit(solution)/shard_map/gate_gradient/pallas_call | solution.py:206
  228.0 3.4 collective-permute-done.18
  231.4 2.7 collective-permute-done.19
  234.2 2.1 multiply_reduce_fusion
  239.0 3.5 all-to-all-start.1
  245.3 21.1 %up_gradient.1 = (bf16[512,1152]{1,0:T(8,128)(2,1)}, bf16[512,1152]{1,0:T(8,128)(2,1)}, bf16[1024,512]{1,0:T(8,128)(2,1)}, f32[1024,512]{1,0:T(8,128)}) custom-call(s32[3]{0:T(128)} %copy-done.8, bf16[1024,1024]{1,0:T(8,128)(2,1)} %get-tuple-element.152.refs_0_, bf16[1024,1024]{1,0:T(8,128)(2,1)} %copy-done.19, ...), custom_call_target="tpu_custom_call" | custom-call | tf_op jit(solution)/shard_map/up_gradient/pallas_call | solution.py:206
  266.5 4.5 %all-to-all-done.1 = bf16[4,128,1152]{2,1,0:T(8,128)(2,1)S(1)} async-done(((bf16[4,128,1152]{2,1,0:T(8,128)(2,1)}), bf16[4,128,1152]{2,1,0:T(8,128)(2,1)S(1)}, u32[]{:S(2)}, u32[]{:S(2)}) %all-to-all-start.1) | async-done | bytes 1179680 | tf_op jit(solution)/shard_map/all_to_all | solution.py:81
  275.8 2.9 add_convert_fusion.1
  278.8 3.5 all-to-all-start.2
  282.9 21.2 %mixer_back.1 = (bf16[1024,1024]{1,0:T(8,128)(2,1)}, bf16[2,1024,768]{2,1,0:T(8,128)(2,1)}, f32[2,1024,1]{2,1,0:T(8,128)}, f32[2,8,256]{2,1,0:T(8,128)}, bf16[10...) custom-call(s32[3]{0:T(128)} %copy-done.8, ...), custom_call_target="tpu_custom_call" | custom-call | tf_op jit(solution)/shard_map/mixer_back/pallas_call | solution.py:590
  304.1 7.2 %collective-permute-done.23 = bf16[512,1152]{1,0:T(8,128)(2,1)} collective-permute-done((bf16[512,1152]{1,0:T(8,128)(2,1)}, bf16[512,1152]{1,0:T(8,128)(2,1)}, u32[]{:S(2)}, u32[]{:S(2)}) %collective-permute-start.23) | collective-permute-done | bytes 1179680 | tf_op jit(solution)/shard_map/ppermute | solution.py:24
  312.5 2.7 add_convert_fusion
  316.6 2.6 add_convert_fusion.5
  319.1 4.5 %all-to-all-start.3 = ((bf16[4,128,1152]{2,1,0:T(8,128)(2,1)}), bf16[4,128,1152]{2,1,0:T(8,128)(2,1)S(1)}, u32[]{:S(2)}, u32[]{:S(2)}) async-start(bf16[4,128,1152]{2,1,0:T(8,128)(2,1)} %bitcast.23), calls=%async_computation.3 | async-start | bytes 2359296 | tf_op jit(solution)/shard_map/all_to_all | solution.py:81
  323.6 2.4 add_bitcast_fusion
  334.2 1.6 add_convert_fusion.4
  335.9 6.7 %back_in.1 = f32[1024,512]{1,0:T(8,128)} custom-call(s32[3]{0:T(128)} %copy-done.8, bf16[2,1024,768]{2,1,0:T(8,128)(2,1)} %get-tuple-element.218.refs_0_, bf16[8,2,128,1024]{3,2,1,0:T(8,128)(2,1)} %copy-done, bf16[1024,1024]{1,0:T(8,128)(2,1)} %copy-done.2, f32[1024,1]{1,0:T(8,128)} %copy-done.5, f32[2,1024,1]{2,1,0:T(8,128)} %get-tuple-element.219.refs_4_, ...), custom_call_target="tpu_custom_call" | custom-call | tf_op jit(solution)/shard_map/back_in/pallas_call | solution.py:206
  342.6 9.2 %collective-permute-done.27 = f32[5,1024]{1,0:T(8,128)S(1)} collective-permute-done((f32[5,1024]{1,0:T(8,128)S(1)}, f32[5,1024]{1,0:T(8,128)S(1)}, u32[]{:S(2)}, u32[]{:S(2)}) %collective-permute-start.27) | collective-permute-done | bytes 20512 | tf_op jit(solution)/shard_map/ppermute | solution.py:19
  351.8 2.9 collective-permute-done.28
  357.5 1.6 add_convert_fusion.3
  360.4 4.8 %all-to-all-start.4 = ((bf16[4,144,1024]{2,1,0:T(8,128)(2,1)}), bf16[4,144,1024]{2,1,0:T(8,128)(2,1)}, u32[]{:S(2)}, u32[]{:S(2)}) async-start(bf16[4,144,1024]{2,1,0:T(8,128)(2,1)} %pad_maximum_fusion.1), calls=%async_computation.4 | async-start | bytes 2359296 | tf_op jit(solution)/shard_map/all_to_all | solution.py:81
  365.2 2.3 multiply_add_fusion
  367.8 12.0 %collective-permute-done.31 = bf16[1024,512]{1,0:T(8,128)(2,1)} collective-permute-done((bf16[1024,512]{1,0:T(8,128)(2,1)}, bf16[1024,512]{1,0:T(8,128)(2,1)}, u32[]{:S(2)}, u32[]{:S(2)}) %collective-permute-start.31) | collective-permute-done | bytes 1048608 | tf_op jit(solution)/shard_map/ppermute | solution.py:19
  379.8 1.6 add_convert_fusion.8
  383.0 1.6 maximum_select_fusion.5
  385.8 6.0 %all-to-all-done.4 = bf16[4,144,1024]{2,1,0:T(8,128)(2,1)} async-done(((bf16[4,144,1024]{2,1,0:T(8,128)(2,1)}), bf16[4,144,1024]{2,1,0:T(8,128)(2,1)}, u32[]{:S(2)}, u32[]{:S(2)}) %all-to-all-start.4) | async-done | bytes 1179680 | tf_op jit(solution)/shard_map/all_to_all | solution.py:81
  (224 shorter events, 62.2 us)
Async XLA Ops:
  10.4 32.2 %all-to-all-start = ((bf16[4,128,1024]{1,2,0:T(8,128)(2,1)}), bf16[4,128,1024]{1,2,0:T(8,128)(2,1)S(1)}, u32[]{:S(2)}, u32[]{:S(2)}) async-start(bf16[4,128,1024]{1,2,0:T(8,128)(2,1)} %copy_bitcast_fusion), calls=%async_computation | async-start | bytes 2097152 | tf_op jit(solution)/shard_map/all_to_all | solution.py:680
  16.9 142.3 %all-gather.2.cloned.1.call-start = ((), (), s32[]{:S(2)}) async-start(), calls=%async_computation.5 | async-start | bytes 15040512 | tf_op jit(solution)/shard_map/all_gather | solution.py:676
  17.8 26.2 %collective-permute-start = (bf16[1024,256]{1,0:T(8,128)(2,1)}, bf16[1024,256]{1,0:T(8,128)(2,1)S(1)}, u32[]{:S(2)}, u32[]{:S(2)}) collective-permute-start(bf16[1024,256]{1,0:T(8,128)(2,1)} %get-tuple-element.296), channel_id=1, source_target_pairs={{0,1},{1,0},{2,3},{3,2},{4,5},{5,4},{6,7},{7,6},{8,9},{9,8},{10,11... | collective-permute-start | bytes 1572872 | tf_op jit(solution)/shard_map/ppermute | solution.py:19
  17.8 26.2 %collective-permute-start.1 = (bf16[1024,256]{1,0:T(8,128)(2,1)S(1)}, bf16[1024,256]{1,0:T(8,128)(2,1)}, u32[]{:S(2)}, u32[]{:S(2)}) collective-permute-start(bf16[1024,256]{1,0:T(8,128)(2,1)S(1)} %get-tuple-element.126), channel_id=1, source_target_pairs={{0,2},{2,0},{1,3},{3,1},{4,6},{6,4},{5,7},{7,5},{8,10},{10,8},{9,1... | collective-permute-start | bytes 1572872 | tf_op jit(solution)/shard_map/ppermute | solution.py:19
  19.3 24.6 %collective-permute-start.2 = (bf16[1024,256]{1,0:T(8,128)(2,1)}, bf16[1024,256]{1,0:T(8,128)(2,1)}, u32[]{:S(2)}, u32[]{:S(2)}) collective-permute-start(bf16[1024,256]{1,0:T(8,128)(2,1)} %get-tuple-element.296), channel_id=1, source_target_pairs={{0,3},{1,2},{2,1},{3,0},{4,7},{5,6},{6,5},{7,4},{8,11},{9,10},{10,... | collective-permute-start | bytes 1572872 | tf_op jit(solution)/shard_map/ppermute | solution.py:666
  19.8 25.9 %copy-start.38 = (bf16[2048,256]{1,0:T(8,128)(2,1)S(1)}, bf16[2048,256]{1,0:T(8,128)(2,1)}, u32[]{:S(2)}) copy-start(bf16[2048,256]{1,0:T(8,128)(2,1)} %param.19) | copy-start | bytes 3145732
  44.0 10.3 %collective-permute-start.4 = (bf16[512,1024]{1,0:T(8,128)(2,1)}, bf16[512,1024]{1,0:T(8,128)(2,1)}, u32[]{:S(2)}, u32[]{:S(2)}) collective-permute-start(bf16[512,1024]{1,0:T(8,128)(2,1)} %bitcast.2), channel_id=1, source_target_pairs={{0,1},{1,0},{2,3},{3,2},{4,5},{5,4},{6,7},{7,6},{8,9},{9,8},{10,11... | collective-permute-start | bytes 3145736 | tf_op jit(solution)/shard_map/ppermute | solution.py:19
  44.1 35.4 %collective-permute-start.3 = (bf16[512,1024]{1,0:T(8,128)(2,1)}, bf16[512,1024]{1,0:T(8,128)(2,1)}, u32[]{:S(2)}, u32[]{:S(2)}) collective-permute-start(bf16[512,1024]{1,0:T(8,128)(2,1)} %bitcast.2), channel_id=1, source_target_pairs={{0,16},{16,0},{1,17},{17,1},{2,18},{18,2},{3,19},{19,3},{4,20},{20... | collective-permute-start | bytes 3145736 | tf_op jit(solution)/shard_map/ppermute | solution.py:19
  45.7 58.6 %copy-start.8 = (s32[3]{0:T(128)}, s32[3]{0:T(128)S(1)}, u32[]{:S(2)}) copy-start(s32[3]{0:T(128)S(1)} %pad_add_fusion.scalars_ref.scalars) | copy-start | bytes 40
  45.8 12.5 %collective-permute-start.5 = (bf16[1024,256]{1,0:T(8,128)(2,1)S(1)}, bf16[1024,256]{1,0:T(8,128)(2,1)S(1)}, u32[]{:S(2)}, u32[]{:S(2)}) collective-permute-start(bf16[1024,256]{1,0:T(8,128)(2,1)S(1)} %get-tuple-element.294), channel_id=1, source_target_pairs={{0,1},{1,0},{2,3},{3,2},{4,5},{5,4},{6,7},{7,6},{8,9},{9,8},{10,11... | collective-permute-start | bytes 1572872 | tf_op jit(solution)/shard_map/ppermute | solution.py:19
  46.0 25.5 %collective-permute-start.7 = (bf16[1024,256]{1,0:T(8,128)(2,1)S(1)}, bf16[1024,256]{1,0:T(8,128)(2,1)S(1)}, u32[]{:S(2)}, u32[]{:S(2)}) collective-permute-start(bf16[1024,256]{1,0:T(8,128)(2,1)S(1)} %get-tuple-element.294), channel_id=1, source_target_pairs={{0,3},{1,2},{2,1},{3,0},{4,7},{5,6},{6,5},{7,4},{8,11},{9,10},{10,... | collective-permute-start | bytes 1572872 | tf_op jit(solution)/shard_map/ppermute | solution.py:666
  47.5 24.0 %collective-permute-start.6 = (bf16[1024,256]{1,0:T(8,128)(2,1)S(1)}, bf16[1024,256]{1,0:T(8,128)(2,1)S(1)}, u32[]{:S(2)}, u32[]{:S(2)}) collective-permute-start(bf16[1024,256]{1,0:T(8,128)(2,1)S(1)} %get-tuple-element.132), channel_id=1, source_target_pairs={{0,2},{2,0},{1,3},{3,1},{4,6},{6,4},{5,7},{7,5},{8,10},{10,8},{9,1... | collective-permute-start | bytes 1572872 | tf_op jit(solution)/shard_map/ppermute | solution.py:19
  50.7 74.3 %copy-start.2 = (bf16[1024,1024]{1,0:T(8,128)(2,1)}, bf16[1024,1024]{1,0:T(8,128)(2,1)S(1)}, u32[]{:S(2)}) copy-start(bf16[1024,1024]{1,0:T(8,128)(2,1)S(1)} %maximum_select_fusion.2.refs_0_.tokens.refs_2_) | copy-start | bytes 6291460
  79.4 2.9 collective-permute-start.9
  79.5 10.2 %collective-permute-start.11 = (bf16[3,256]{1,0:T(4,128)(2,1)S(1)}, bf16[3,256]{1,0:T(4,128)(2,1)S(1)}, u32[]{:S(2)}, u32[]{:S(2)}) collective-permute-start(bf16[3,256]{1,0:T(4,128)(2,1)S(1)} %copy-done.51), channel_id=1, source_target_pairs={{0,1},{1,0},{2,3},{3,2},{4,5},{5,4},{6,7},{7,6},{8,9},{9,8},{10,11... | collective-permute-start | bytes 4616 | tf_op jit(solution)/shard_map/ppermute | solution.py:19
  87.5 8.3 %collective-permute-start.10 = (bf16[2,2,256]{2,1,0:T(2,128)(2,1)S(1)}, bf16[2,2,256]{2,1,0:T(2,128)(2,1)S(1)}, u32[]{:S(2)}, u32[]{:S(2)}) collective-permute-start(bf16[2,2,256]{2,1,0:T(2,128)(2,1)S(1)} %slice.198), channel_id=1, source_target_pairs={{0,1},{1,4},{4,5},{5,8},{8,9},{9,12},{12,13},{2,3},{3,6},{6,7},{7,... | collective-permute-start | bytes 6152 | tf_op jit(solution)/shard_map/ppermute | solution.py:711
  99.0 26.0 %collective-permute-start.12 = (bf16[512,1024]{1,0:T(8,128)(2,1)S(1)}, bf16[512,1024]{1,0:T(8,128)(2,1)S(1)}, u32[]{:S(2)}, u32[]{:S(2)}) collective-permute-start(bf16[512,1024]{1,0:T(8,128)(2,1)S(1)} %get-tuple-element.142), channel_id=1, source_target_pairs={{0,2},{2,0},{1,3},{3,1},{4,6},{6,4},{5,7},{7,5},{8,10},{10,8},{9,1... | collective-permute-start | bytes 3145736 | tf_op jit(solution)/shard_map/ppermute | solution.py:19
  102.2 26.5 %collective-permute-start.8 = (bf16[1024,1024]{1,0:T(8,128)(2,1)S(1)}, bf16[1024,1024]{1,0:T(8,128)(2,1)S(1)}, u32[]{:S(2)}, u32[]{:S(2)}) collective-permute-start(bf16[1024,1024]{1,0:T(8,128)(2,1)S(1)} %pad_maximum_fusion.cot.refs_0_), channel_id=1, source_target_pairs={{0,1},{1,0},{2,3},{3,2},{4,5},{5,4},{6,7},{7,6},{8,9},{9,8},{10,11... | collective-permute-start | bytes 6291464 | tf_op jit(solution)/shard_map/ppermute | solution.py:19
  127.1 32.1 %copy-start.23 = (bf16[512,1024]{1,0:T(8,128)(2,1)}, bf16[512,1024]{1,0:T(8,128)(2,1)S(1)}, u32[]{:S(2)}) copy-start(bf16[512,1024]{1,0:T(8,128)(2,1)S(1)} %multiply_convert_fusion.h_own) | copy-start | bytes 3145732
  127.1 25.5 %collective-permute-start.13 = (bf16[512,1024]{1,0:T(8,128)(2,1)S(1)}, bf16[512,1024]{1,0:T(8,128)(2,1)S(1)}, u32[]{:S(2)}, u32[]{:S(2)}) collective-permute-start(bf16[512,1024]{1,0:T(8,128)(2,1)S(1)} %multiply_convert_fusion.h_own), channel_id=1, source_target_pairs={{0,2},{2,0},{1,3},{3,1},{4,6},{6,4},{5,7},{7,5},{8,10},{10,8},{9,1... | collective-permute-start | bytes 3145736 | tf_op jit(solution)/shard_map/ppermute | solution.py:19
  182.0 12.0 %collective-permute-start.14 = (bf16[1024,1152]{1,0:T(8,128)(2,1)}, bf16[1024,1152]{1,0:T(8,128)(2,1)}, u32[]{:S(2)}, u32[]{:S(2)}) collective-permute-start(bf16[1024,1152]{1,0:T(8,128)(2,1)} %get-tuple-element.186.refs_5_), channel_id=1, source_target_pairs={{0,1},{1,0},{2,3},{3,2},{4,5},{5,4},{6,7},{7,6},{8,9},{9,8},{10,11... | collective-permute-start | bytes 7077896 | tf_op jit(solution)/shard_map/ppermute | solution.py:19
  182.3 11.6 %collective-permute-start.15 = (bf16[1024,1024]{1,0:T(8,128)(2,1)}, bf16[1024,1024]{1,0:T(8,128)(2,1)S(1)}, u32[]{:S(2)}, u32[]{:S(2)}) collective-permute-start(bf16[1024,1024]{1,0:T(8,128)(2,1)} %get-tuple-element.152.refs_0_), channel_id=1, source_target_pairs={{0,1},{1,0},{2,3},{3,2},{4,5},{5,4},{6,7},{7,6},{8,9},{9,8},{10,11... | collective-permute-start | bytes 6291464 | tf_op jit(solution)/shard_map/ppermute | solution.py:19
  193.9 11.8 %collective-permute-start.16 = (bf16[1024,1152]{1,0:T(8,128)(2,1)S(1)}, bf16[1024,1152]{1,0:T(8,128)(2,1)}, u32[]{:S(2)}, u32[]{:S(2)}) collective-permute-start(bf16[1024,1152]{1,0:T(8,128)(2,1)S(1)} %copy-done.17), channel_id=1, source_target_pairs={{0,1},{1,0},{2,3},{3,2},{4,5},{5,4},{6,7},{7,6},{8,9},{9,8},{10,11... | collective-permute-start | bytes 7077896 | tf_op jit(solution)/shard_map/ppermute | solution.py:19
  194.3 11.5 %collective-permute-start.17 = (bf16[1024,1152]{1,0:T(8,128)(2,1)S(1)}, bf16[1024,1152]{1,0:T(8,128)(2,1)}, u32[]{:S(2)}, u32[]{:S(2)}) collective-permute-start(bf16[1024,1152]{1,0:T(8,128)(2,1)S(1)} %copy-done.18), channel_id=1, source_target_pairs={{0,1},{1,0},{2,3},{3,2},{4,5},{5,4},{6,7},{7,6},{8,9},{9,8},{10,11... | collective-permute-start | bytes 7077896 | tf_op jit(solution)/shard_map/ppermute | solution.py:19
  205.7 28.4 %copy-start.14 = (f32[512,1024]{1,0:T(8,128)S(1)}, f32[512,1024]{1,0:T(8,128)}, u32[]{:S(2)}) copy-start(f32[512,1024]{1,0:T(8,128)} %copy-done.13) | copy-start | bytes 6291460
  205.8 28.4 %collective-permute-start.19 = (bf16[512,1152]{1,0:T(8,128)(2,1)}, bf16[512,1152]{1,0:T(8,128)(2,1)S(1)}, u32[]{:S(2)}, u32[]{:S(2)}) collective-permute-start(bf16[512,1152]{1,0:T(8,128)(2,1)} %get-tuple-element.174), channel_id=1, source_target_pairs={{0,16},{16,0},{1,17},{17,1},{2,18},{18,2},{3,19},{19,3},{4,20},{20... | collective-permute-start | bytes 3538952 | tf_op jit(solution)/shard_map/ppermute | solution.py:24
  206.4 25.0 %collective-permute-start.18 = (bf16[512,1024]{1,0:T(8,128)(2,1)S(1)}, bf16[512,1024]{1,0:T(8,128)(2,1)S(1)}, u32[]{:S(2)}, u32[]{:S(2)}) collective-permute-start(bf16[512,1024]{1,0:T(8,128)(2,1)S(1)} %copy-done.35), channel_id=1, source_target_pairs={{0,2},{2,0},{1,3},{3,1},{4,6},{6,4},{5,7},{7,5},{8,10},{10,8},{9,1... | collective-permute-start | bytes 3145736 | tf_op jit(solution)/shard_map/ppermute | solution.py:19
  237.6 36.0 %copy-start.22 = (bf16[512,1024]{1,0:T(8,128)(2,1)}, bf16[512,1024]{1,0:T(8,128)(2,1)S(1)}, u32[]{:S(2)}) copy-start(bf16[512,1024]{1,0:T(8,128)(2,1)S(1)} %add_convert_fusion.6.own) | copy-start | bytes 3145732
  239.0 31.9 %all-to-all-start.1 = ((bf16[4,128,1152]{2,1,0:T(8,128)(2,1)}), bf16[4,128,1152]{2,1,0:T(8,128)(2,1)S(1)}, u32[]{:S(2)}, u32[]{:S(2)}) async-start(bf16[4,128,1152]{2,1,0:T(8,128)(2,1)} %bitcast.17), calls=%async_computation.1 | async-start | bytes 2359296 | tf_op jit(solution)/shard_map/all_to_all | solution.py:81
  242.5 29.8 %collective-permute-start.21 = (bf16[512,1152]{1,0:T(8,128)(2,1)}, bf16[512,1152]{1,0:T(8,128)(2,1)}, u32[]{:S(2)}, u32[]{:S(2)}) collective-permute-start(bf16[512,1152]{1,0:T(8,128)(2,1)} %get-tuple-element.191), channel_id=1, source_target_pairs={{0,16},{16,0},{1,17},{17,1},{2,18},{18,2},{3,19},{19,3},{4,20},{20... | collective-permute-start | bytes 3538952 | tf_op jit(solution)/shard_map/ppermute | solution.py:24
  243.2 29.2 %collective-permute-start.20 = (bf16[512,1024]{1,0:T(8,128)(2,1)S(1)}, bf16[512,1024]{1,0:T(8,128)(2,1)}, u32[]{:S(2)}, u32[]{:S(2)}) collective-permute-start(bf16[512,1024]{1,0:T(8,128)(2,1)S(1)} %add_convert_fusion.6.own), channel_id=1, source_target_pairs={{0,2},{2,0},{1,3},{3,1},{4,6},{6,4},{5,7},{7,5},{8,10},{10,8},{9,1... | collective-permute-start | bytes 3145736 | tf_op jit(solution)/shard_map/ppermute | solution.py:19
  274.5 4.2 %collective-permute-start.22 = (bf16[2,2,256]{2,1,0:T(2,128)(2,1)S(1)}, bf16[2,2,256]{2,1,0:T(2,128)(2,1)S(1)}, u32[]{:S(2)}, u32[]{:S(2)}) collective-permute-start(bf16[2,2,256]{2,1,0:T(2,128)(2,1)S(1)} %fusion.1), channel_id=1, source_target_pairs={{1,0},{4,1},{5,4},{8,5},{9,8},{12,9},{13,12},{3,2},{6,3},{7,6},{10... | collective-permute-start | bytes 6152 | tf_op jit(solution)/shard_map/ppermute | solution.py:797
  278.8 33.3 %all-to-all-start.2 = ((bf16[4,128,1152]{2,1,0:T(8,128)(2,1)}), bf16[4,128,1152]{2,1,0:T(8,128)(2,1)S(1)}, u32[]{:S(2)}, u32[]{:S(2)}) async-start(bf16[4,128,1152]{2,1,0:T(8,128)(2,1)} %bitcast.21), calls=%async_computation.2 | async-start | bytes 2359296 | tf_op jit(solution)/shard_map/all_to_all | solution.py:81
  282.3 29.1 %collective-permute-start.23 = (bf16[512,1152]{1,0:T(8,128)(2,1)}, bf16[512,1152]{1,0:T(8,128)(2,1)}, u32[]{:S(2)}, u32[]{:S(2)}) collective-permute-start(bf16[512,1152]{1,0:T(8,128)(2,1)} %get-tuple-element.208), channel_id=1, source_target_pairs={{0,16},{16,0},{1,17},{17,1},{2,18},{18,2},{3,19},{19,3},{4,20},{20... | collective-permute-start | bytes 3538952 | tf_op jit(solution)/shard_map/ppermute | solution.py:24
  282.9 29.3 %copy-start.6 = (f32[1024,1]{1,0:T(8,128)S(1)}, f32[1024,1]{1,0:T(8,128)}, u32[]{:S(2)}) copy-start(f32[1024,1]{1,0:T(8,128)} %copy-done.5) | copy-start | bytes 12292
  282.9 29.5 %copy-start.32 = (bf16[512,1152]{1,0:T(8,128)(2,1)S(1)}, bf16[512,1152]{1,0:T(8,128)(2,1)}, u32[]{:S(2)}) copy-start(bf16[512,1152]{1,0:T(8,128)(2,1)} %get-tuple-element.211) | copy-start | bytes 3538948
  312.1 4.5 %collective-permute-start.24 = (bf16[1024,1024]{1,0:T(8,128)(2,1)}, bf16[1024,1024]{1,0:T(8,128)(2,1)}, u32[]{:S(2)}, u32[]{:S(2)}) collective-permute-start(bf16[1024,1024]{1,0:T(8,128)(2,1)} %get-tuple-element.216), channel_id=1, source_target_pairs={{0,1},{1,0},{2,3},{3,2},{4,5},{5,4},{6,7},{7,6},{8,9},{9,8},{10,11... | collective-permute-start | bytes 6291464 | tf_op jit(solution)/shard_map/ppermute | solution.py:19
  319.1 36.9 %all-to-all-start.3 = ((bf16[4,128,1152]{2,1,0:T(8,128)(2,1)}), bf16[4,128,1152]{2,1,0:T(8,128)(2,1)S(1)}, u32[]{:S(2)}, u32[]{:S(2)}) async-start(bf16[4,128,1152]{2,1,0:T(8,128)(2,1)} %bitcast.23), calls=%async_computation.3 | async-start | bytes 2359296 | tf_op jit(solution)/shard_map/all_to_all | solution.py:81
  326.0 29.1 %collective-permute-start.25 = (bf16[1024,512]{1,0:T(8,128)(2,1)}, bf16[1024,512]{1,0:T(8,128)(2,1)S(1)}, u32[]{:S(2)}, u32[]{:S(2)}) collective-permute-start(bf16[1024,512]{1,0:T(8,128)(2,1)} %get-tuple-element.217), channel_id=1, source_target_pairs={{0,2},{2,0},{1,3},{3,1},{4,6},{6,4},{5,7},{7,5},{8,10},{10,8},{9,1... | collective-permute-start | bytes 3145736 | tf_op jit(solution)/shard_map/ppermute | solution.py:19
  328.7 27.3 %collective-permute-start.30 = (bf16[512,1024]{1,0:T(8,128)(2,1)}, bf16[512,1024]{1,0:T(8,128)(2,1)}, u32[]{:S(2)}, u32[]{:S(2)}) collective-permute-start(bf16[512,1024]{1,0:T(8,128)(2,1)} %add_convert_fusion.5), channel_id=1, source_target_pairs={{0,16},{16,0},{1,17},{17,1},{2,18},{18,2},{3,19},{19,3},{4,20},{20... | collective-permute-start | bytes 3145736 | tf_op jit(solution)/shard_map/ppermute | solution.py:24
  329.4 1.3 collective-permute-start.26
  330.7 21.1 %collective-permute-start.27 = (f32[5,1024]{1,0:T(8,128)S(1)}, f32[5,1024]{1,0:T(8,128)S(1)}, u32[]{:S(2)}, u32[]{:S(2)}) collective-permute-start(f32[5,1024]{1,0:T(8,128)S(1)} %fusion.3), channel_id=1, source_target_pairs={{0,2},{2,0},{1,3},{3,1},{4,6},{6,4},{5,7},{7,5},{8,10},{10,8},{9,1... | collective-permute-start | bytes 61448 | tf_op jit(solution)/shard_map/ppermute | solution.py:19
  331.3 23.4 %collective-permute-start.28 = (f32[5,1024]{1,0:T(8,128)S(1)}, f32[5,1024]{1,0:T(8,128)S(1)}, u32[]{:S(2)}, u32[]{:S(2)}) collective-permute-start(f32[5,1024]{1,0:T(8,128)S(1)} %fusion.3), channel_id=1, source_target_pairs={{0,16},{16,0},{1,17},{17,1},{2,18},{18,2},{3,19},{19,3},{4,20},{20... | collective-permute-start | bytes 61448 | tf_op jit(solution)/shard_map/ppermute | solution.py:19
  332.8 22.2 %collective-permute-start.29 = (f32[5,1024]{1,0:T(8,128)S(1)}, f32[5,1024]{1,0:T(8,128)S(1)}, u32[]{:S(2)}, u32[]{:S(2)}) collective-permute-start(f32[5,1024]{1,0:T(8,128)S(1)} %fusion.3), channel_id=1, source_target_pairs={{0,18},{2,16},{16,2},{18,0},{1,19},{3,17},{17,3},{19,1},{4,22},{6,... | collective-permute-start | bytes 61448 | tf_op jit(solution)/shard_map/ppermute | solution.py:831
  356.0 23.7 %collective-permute-start.31 = (bf16[1024,512]{1,0:T(8,128)(2,1)}, bf16[1024,512]{1,0:T(8,128)(2,1)}, u32[]{:S(2)}, u32[]{:S(2)}) collective-permute-start(bf16[1024,512]{1,0:T(8,128)(2,1)} %get-tuple-element.227), channel_id=1, source_target_pairs={{0,2},{2,0},{1,3},{3,1},{4,6},{6,4},{5,7},{7,5},{8,10},{10,8},{9,1... | collective-permute-start | bytes 3145736 | tf_op jit(solution)/shard_map/ppermute | solution.py:19
  360.4 31.4 %all-to-all-start.4 = ((bf16[4,144,1024]{2,1,0:T(8,128)(2,1)}), bf16[4,144,1024]{2,1,0:T(8,128)(2,1)}, u32[]{:S(2)}, u32[]{:S(2)}) async-start(bf16[4,144,1024]{2,1,0:T(8,128)(2,1)} %pad_maximum_fusion.1), calls=%async_computation.4 | async-start | bytes 2359296 | tf_op jit(solution)/shard_map/all_to_all | solution.py:81
  367.7 15.3 %collective-permute-start.33 = (f32[1024,256]{1,0:T(8,128)S(1)}, f32[1024,256]{1,0:T(8,128)S(1)}, u32[]{:S(2)}, u32[]{:S(2)}) collective-permute-start(f32[1024,256]{1,0:T(8,128)S(1)} %get-tuple-element.283), channel_id=1, source_target_pairs={{0,1},{1,0},{2,3},{3,2},{4,5},{5,4},{6,7},{7,6},{8,9},{9,8},{10,11... | collective-permute-start | bytes 3145736 | tf_op jit(solution)/shard_map/ppermute | solution.py:19
  381.9 2.6 collective-permute-start.32
  (44 other events, 279.0 us)
Sparse Core Ops, SparseCore 0:
  44.1 115.0 all-gather.1

commit v4 on v3

--- a/solution.py
+++ b/solution.py
@@ -19,6 +19,11 @@
     return lax.ppermute(value, axis, [(0, 1), (1, 0)])
 
 
+def fetch(value, axis, distance):
+    size = lax.axis_size(axis)
+    return lax.ppermute(value, axis, [(s, (s - distance) % size) for s in range(size)])
+
+
 def deliver(value, axis, distance):
     size = lax.axis_size(axis)
     return lax.ppermute(value, axis, [(s, (s + distance) % size) for s in range(size)])
@@ -95,6 +100,13 @@
 
 def add_dp(keep, arrived):
     return total([keep, *arrived]).astype(BF16)
+
+
+def for_tok(parts, steps):
+    count = lax.axis_size("tok")
+    size = parts[0].shape[0] // count
+    index = (lax.axis_index("tok") + steps) % count
+    return total([pick_rows(part, index, size) for part in parts])
 
 
 def sum_over(value, axis):
@@ -649,7 +661,7 @@
     gain_ffn,
     cotangent,
 ):
-    x, y, c = (lax.axis_index(name) for name in ("dp", "y", "c"))
+    x, z, y, c = (lax.axis_index(name) for name in ("dp", "tok", "y", "c"))
     nx, nz = lax.axis_size("dp"), lax.axis_size("tok")
     width = tokens.shape[1]
     features = 4 * width
@@ -677,13 +689,16 @@
         return whole.reshape(features // chunk, 2, chunk, shard.shape[1])
 
     first = jnp.concatenate([in_weight.reshape(chunk, 3 * width), out_weight.T], 1)
-    first_tok = lax.all_to_all(
-        jnp.concatenate([first] * nz, 0), "tok", split_axis=0, concat_axis=0, tiled=True
-    )
+    first = with_layout_constraint(first, Layout((0, 1)))
+    blocks = [first] + [fetch(first, "tok", i) for i in range(1, nz)]
     weights = jnp.concatenate([gate_weight, up_weight, down_weight.T], 1)
     pieces = to_mp(tokens)
-    first_tok, weights, cotangent, *pieces = tie(first_tok, weights, cotangent, *pieces)
+    weights, cotangent, *pieces = tie(weights, cotangent, *pieces, *blocks)
+    pieces, blocks = pieces[:-nz], pieces[-nz:]
     weights = gather(weights)
+    first_tok = lax.dynamic_slice_in_dim(
+        jnp.concatenate(blocks + blocks[:-1], 0), ((nz - z) % nz) * chunk, nz * chunk
+    )
     pieces_cot = to_mp(cotangent)
     taps = by_rank(c, conv_kernel[None], swap(conv_kernel, "c")[None]).astype(F32)
 
@@ -774,10 +789,12 @@
         scaled - normalized * jnp.mean(scaled * normalized, -1, keepdims=True)
     )
     d_res_own = d_res.astype(BF16)
-    down_mine = add_dp(keep, pieces)
-    d_res_own, down_mine, send, *units = tie(d_res_own, down_mine, send, *hidden, *d_up)
-    hidden, d_up = units[:2], units[2:]
-    arrived, down_got, pieces = swap(d_res_own, "y"), to_tok(down_mine), pieces_of(send)
+    down_parts = [keep, *pieces]
+    down_mine = [for_tok(down_parts, i).astype(BF16) for i in range(1, nz)]
+    d_res_own, send, *units = tie(d_res_own, send, *hidden, *d_up, *down_mine)
+    hidden, d_up, down_mine = units[:2], units[2:4], units[4:]
+    arrived, pieces = swap(d_res_own, "y"), pieces_of(send)
+    down_got = [deliver(part, "tok", i + 1) for i, part in enumerate(down_mine)]
     keep, send, made_sent, made_kept = run_jobs(
         "up_gradient",
         scalars,
@@ -786,17 +803,21 @@
             made_job(hidden, weights, 2, residual),
         ],
     )
-    arrived, send, made_sent, made_kept, down_got, *pieces = tie(
-        arrived, send, made_sent, made_kept, down_got, *pieces
-    )
-    gate_mine = add_dp(next_keep, pieces)
+    arrived, send, made_sent, made_kept, *pieces = tie(
+        arrived, send, made_sent, made_kept, *pieces, *down_got
+    )
+    pieces, down_got = pieces[: 1 - nz], pieces[1 - nz :]
+    grad_down = total([for_tok(down_parts, 0), *down_got])
+    gate_parts = [next_keep, *pieces]
+    gate_mine = [for_tok(gate_parts, i).astype(BF16) for i in range(1, nz)]
 
     head = jnp.where(y == 0, d_res_own[:8], arrived[:8])
     d_head = jnp.stack([nn(head, w) for w in w_out])
     d_head = (d_head * gate_c).astype(BF16)[:, :2]
     later = lax.ppermute(d_head, ("tok", "c"), [(i + 1, i) for i in range(ranks - 1)])
-    arrived, gate_mine, later, send = tie(arrived, gate_mine, later, send)
-    gate_got, pieces = to_tok(gate_mine), pieces_of(send)
+    arrived, later, send, *gate_mine = tie(arrived, later, send, *gate_mine)
+    pieces = pieces_of(send)
+    gate_got = [deliver(part, "tok", i + 1) for i, part in enumerate(gate_mine)]
     d_res_full, d_proj, dots, grad_taps, own, other, gain_dots, sent = mixer_back(
         scalars,
         d_res_own,
@@ -812,9 +833,9 @@
         inverse_mix,
         gain_row,
     )
-    d_proj, own, other, sent, gate_got, *pieces = tie(
-        d_proj, own, other, sent, gate_got, *pieces
-    )
+    d_proj, own, other, sent, *pieces = tie(d_proj, own, other, sent, *pieces, *gate_got)
+    pieces, gate_got = pieces[: 1 - nz], pieces[1 - nz :]
+    grad_gate = total([for_tok(gate_parts, 0), *gate_got])
     other = of_core(other)
     up_mine = add_dp(keep, pieces)
     sent, d_proj, up_mine, grad_taps, gain_dots, own, other, *pieces = tie(
@@ -873,7 +894,7 @@
         (made_kept[half:] + made_arrived[:half].astype(F32)).astype(BF16),
     )
     mixed = by_core(out_near)
-    grad_down, grad_gate, grad_up = (add_tok(v) for v in (down_got, gate_got, up_got))
+    grad_up = add_tok(up_got)
     mixer_sum = add_tok(mixer_got)
     grad_mixer = mixer_sum[:chunk]
     sums = mixer_sum[chunk : chunk + 5] + mixer_sum[chunk + 5 : chunk + 10]

time: 406 us -> 386 us (0.951)
  waiting for transfers between devices: 142 us -> 129 us
  other arithmetic: 44.9 us -> 37.4 us
    all_to_all x1 -> x0, waiting for transfers between devices: 20.6 us -> none  [body(): lax.all_to_all(jnp.concatenate([first] * nz, 0), 'tok', split_axis=0, con...]
    ppermute x0 -> x3, waiting for transfers between devices: none -> 16.9 us  [fetch(): lax.ppermute(value, axis, [(s, (s - distance) % size) for s in range(size)])]
    ppermute x4 -> x10, starting transfers between devices: 2.49 us -> 12.6 us  [deliver(): lax.ppermute(value, axis, [(s, (s + distance) % size) for s in range(size)])]
    all_to_all x4 -> x2, waiting for transfers between devices: 11.1 us -> 3.95 us  [to_tok(): return lax.all_to_all(mine, 'tok', split_axis=0, concat_axis=0, tiled=True)]
    ppermute x4 -> x10, waiting for transfers between devices: 9.98 us -> 3.01 us  [deliver(): lax.ppermute(value, axis, [(s, (s + distance) % size) for s in range(size)])]
    all_to_all x1 -> x0, starting transfers between devices: 6.45 us -> none  [body(): lax.all_to_all(jnp.concatenate([first] * nz, 0), 'tok', split_axis=0, con...]
    all_to_all x4 -> x2, starting transfers between devices: 16.3 us -> 10.7 us  [to_tok(): return lax.all_to_all(mine, 'tok', split_axis=0, concat_axis=0, tiled=True)]
    convert_element_type x4 -> x2, other arithmetic: 8.66 us -> 3.3 us  [add_dp(): return total([keep, *arrived]).astype(BF16)]
  transfers between devices with their start and end apart: 40 -> 46, of which waited for: 19 -> 19; matrix products, arithmetic and copies ran while one was open for 11% -> 10% of each run, Pallas kernels for 26% -> 28%
where the time goes in v4:
time: 386 us; the launch traced here: 385 us
  waiting for transfers between devices  129 us (33%)
  Pallas kernels  129 us (33%)
  starting transfers between devices  51.5 us (13%)
  other arithmetic  37.4 us (10%)
  local copies, waits for them, and re-layouts  23.3 us (6%)
  between operations  15.1 us (4%)
    ppermute x24, waiting for transfers between devices, swap(): return lax.ppermute(value, axis, [(0, 1), (1, 0)])  93.6 us
    pallas_call x10, Pallas kernels, run_jobs(): pl.pallas_call(kernel, out_shape=shapes, grid_spec=pltpu.PrefetchScalarGr...  84.9 us
    pallas_call x1, Pallas kernels, hidden_units(): pl.pallas_call(hidden_kernel, out_shape=[jax.ShapeDtypeStruct((rows, feat...  22.6 us
    pallas_call x1, Pallas kernels, mixer_back(): pl.pallas_call(mixer_back_kernel, out_shape=[jax.ShapeDtypeStruct((rows,...  21.2 us
    ppermute x24, starting transfers between devices, swap(): return lax.ppermute(value, axis, [(0, 1), (1, 0)])  17 us
    ppermute x3, waiting for transfers between devices, fetch(): lax.ppermute(value, axis, [(s, (s - distance) % size) for s in range(size)])  16.9 us
    unnamed x135, local copies, waits for them, and re-layouts  14.8 us
    ppermute x10, starting transfers between devices, deliver(): lax.ppermute(value, axis, [(s, (s + distance) % size) for s in range(size)])  12.6 us
  transfers between devices with their start and end apart: 46, of which 19 were waited for; matrix products, arithmetic and copies ran while one was open for 10% of the time, Pallas kernels for 28%

profile of v4, /device:TPU:0, one launch (start us, length us, event | category | flops | bytes accessed | tf_op | source)
XLA Modules:
  0.0 385.0 jit_solution(6753674747991726009)
XLA Ops:
  9.6 5.1 %collective-permute-start.3 = (bf16[128,1024]{1,0:T(8,128)(2,1)S(1)}, bf16[128,1024]{1,0:T(8,128)(2,1)S(1)}, u32[]{:S(2)}, u32[]{:S(2)}) collective-permute-start(bf16[128,1024]{1,0:T(8,128)(2,1)S(1)} %pad_maximum_fusion.3), channel_id=1, source_target_pairs={{0,12},{4,0},{8,4},{12,8},{1,13},{5,1},{9,5},{13,9},{2,14},{6,2},{... | collective-permute-start | bytes 786440 | tf_op jit(solution)/shard_map/ppermute | solution.py:24
  18.5 2.9 collective-permute-done.3
  21.4 1.9 pad_maximum_fusion.2
  23.4 14.1 %collective-permute-done.4 = bf16[128,1024]{1,0:T(8,128)(2,1)S(1)} collective-permute-done((bf16[128,1024]{1,0:T(8,128)(2,1)S(1)}, bf16[128,1024]{1,0:T(8,128)(2,1)S(1)}, u32[]{:S(2)}, u32[]{:S(2)}) %collective-permute-start.4) | collective-permute-done | bytes 262176 | tf_op jit(solution)/shard_map/ppermute | solution.py:24
  37.5 3.3 collective-permute-done.2
  45.4 1.6 collective-permute-start.10
  52.3 3.2 maximum_select_fusion.1
  55.6 15.3 %collective-permute-done.9 = bf16[1024,256]{1,0:T(8,128)(2,1)S(1)} collective-permute-done((bf16[1024,256]{1,0:T(8,128)(2,1)S(1)}, bf16[1024,256]{1,0:T(8,128)(2,1)S(1)}, u32[]{:S(2)}, u32[]{:S(2)}) %collective-permute-start.9) | collective-permute-done | bytes 524320 | tf_op jit(solution)/shard_map/ppermute | solution.py:19
  70.9 6.4 %collective-permute-done.6 = bf16[512,1024]{1,0:T(8,128)(2,1)} collective-permute-done((bf16[512,1024]{1,0:T(8,128)(2,1)S(1)}, bf16[512,1024]{1,0:T(8,128)(2,1)}, u32[]{:S(2)}, u32[]{:S(2)}) %collective-permute-start.6) | collective-permute-done | bytes 1048608 | tf_op jit(solution)/shard_map/ppermute | solution.py:19
  77.8 2.4 collective-permute-done.12
  80.2 2.0 maximum_select_fusion.4
  85.4 2.2 collective-permute-start.13
  87.6 6.0 %project.1.refs_0_.proj = f32[2,1024,768]{2,1,0:T(8,128)S(1)} custom-call(s32[3]{0:T(128)S(1)} %pad_add_fusion.scalars_ref.scalars, bf16[1024,1024]{1,0:T(8,128)(2,1)S(1)} %copy-done.4, bf16[8,2,128,1024]{3,2,1,0:T(8,128)(2,1)S(1)} %maximum_select_fusion.refs_1_.refs_2_.refs_3_.w_out.w_in), custom_call_target="tpu_custom_call" | custom-call | tf_op jit(solution)/shard_map/project/pallas_call | solution.py:218
  93.7 3.2 mix.1
  97.0 1.6 collective-permute-start.15
  100.4 2.3 project_out.1
  102.8 19.3 %collective-permute-done.15 = bf16[512,1024]{1,0:T(8,128)(2,1)S(1)} collective-permute-done((bf16[512,1024]{1,0:T(8,128)(2,1)S(1)}, bf16[512,1024]{1,0:T(8,128)(2,1)S(1)}, u32[]{:S(2)}, u32[]{:S(2)}) %collective-permute-start.15) | collective-permute-done | bytes 1048608 | tf_op jit(solution)/shard_map/ppermute | solution.py:19
  124.2 1.6 collective-permute-start.16
  127.1 21.5 %collective-permute-done.16.h_other = bf16[512,1024]{1,0:T(8,128)(2,1)S(1)} collective-permute-done((bf16[512,1024]{1,0:T(8,128)(2,1)S(1)}, bf16[512,1024]{1,0:T(8,128)(2,1)S(1)}, u32[]{:S(2)}, u32[]{:S(2)}) %collective-permute-start.16) | collective-permute-done | bytes 1048608 | tf_op jit(solution)/shard_map/ppermute | solution.py:19
  148.6 5.0 %all-gather.2.cloned.1.call-done = bf16[2048,3456]{1,0:T(8,128)(2,1)} async-done(((bf16[128,3456]{1,0:T(8,128)(2,1)}), bf16[2048,3456]{1,0:T(8,128)(2,1)}) %all-gather.2.cloned.1.call-update) | async-done | bytes 14155792 | tf_op jit(solution)/shard_map/all_gather | solution.py:688
  153.7 22.6 %hidden_units.1 = (bf16[1024,1024]{1,0:T(8,128)(2,1)}, bf16[1024,1152]{1,0:T(8,128)(2,1)}, bf16[1024,1152]{1,0:T(8,128)(2,1)}, bf16[1024,1152]{1,0:T(8,128)(2,1)...) custom-call(s32[3]{0:T(128)} %copy-done.8, bf16[512,1024]{1,0:T(8,128)(2,1)} %copy-done.23, ...), custom_call_target="tpu_custom_call" | custom-call | tf_op jit(solution)/shard_map/hidden_units/pallas_call | solution.py:171
  176.9 11.4 %back_hidden.1 = bf16[512,1024]{1,0:T(8,128)(2,1)} custom-call(s32[3]{0:T(128)} %copy-done.8, bf16[1024,1152]{1,0:T(8,128)(2,1)} %get-tuple-element.181.refs_0_.refs_2_.refs_4_, bf16[1024,1152]{1,0:T(8,128)(2,1)} %get-tuple-element.183.refs_1_.refs_5_, bf16[1024,1152]{1,0:T(8,128)(2,1)} %get-tuple-element.197.refs_2_.refs_6_, ...), custom_call_target="tpu_custom_call" | custom-call | tf_op jit(solution)/shard_map/back_hidden/pallas_call | solution.py:218
  188.9 11.1 %down_gradient.1 = (bf16[512,1152]{1,0:T(8,128)(2,1)}, bf16[512,1152]{1,0:T(8,128)(2,1)}) custom-call(s32[3]{0:T(128)} %copy-done.8, bf16[1024,1024]{1,0:T(8,128)(2,1)} %copy-done.15, bf16[1024,1024]{1,0:T(8,128)(2,1)} %copy-done.25, bf16[1024,1152]{1,0:T(8,128)(2,1)} %get-tuple-element.199.refs_2_.refs_4_, bf16[1024,1152]{1,0:T(8,128)(2,1)} %collective-permute-done.17.refs_3_), custom_call_target="tpu_custom_call" | custom-call | tf_op jit(solution)/shard_map/down_gradient/pallas_call | solution.py:218
  202.1 20.2 %gate_gradient.1 = (bf16[512,1152]{1,0:T(8,128)(2,1)}, bf16[512,1152]{1,0:T(8,128)(2,1)}, bf16[512,1024]{1,0:T(8,128)(2,1)}) custom-call(s32[3]{0:T(128)} %copy-done.8, bf16[1024,1024]{1,0:T(8,128)(2,1)} %get-tuple-element.166.refs_0_, bf16[1024,1024]{1,0:T(8,128)(2,1)} %copy-done.19, bf16[1024,1152]{1,0:T(8,128)(2,1)} %get-tuple-element.181.refs_0_.refs_2_.refs_4_, ...), custom_call_target="tpu_custom_call" | custom-call | tf_op jit(solution)/shard_map/gate_gradient/pallas_call | solution.py:218
  222.3 3.6 collective-permute-done.21
  225.8 2.7 collective-permute-done.22
  228.5 2.1 multiply_reduce_fusion
  232.0 1.7 add_convert_fusion.10
  235.8 2.0 collective-permute-start.26
  237.7 2.5 collective-permute-start.27
  240.9 21.3 %up_gradient.1 = (bf16[512,1152]{1,0:T(8,128)(2,1)}, bf16[512,1152]{1,0:T(8,128)(2,1)}, bf16[1024,512]{1,0:T(8,128)(2,1)}, f32[1024,512]{1,0:T(8,128)}) custom-call(s32[3]{0:T(128)} %copy-done.8, bf16[1024,1024]{1,0:T(8,128)(2,1)} %get-tuple-element.166.refs_0_, bf16[1024,1024]{1,0:T(8,128)(2,1)} %copy-done.19, ...), custom_call_target="tpu_custom_call" | custom-call | tf_op jit(solution)/shard_map/up_gradient/pallas_call | solution.py:218
  267.1 2.0 collective-permute-start.30
  270.6 1.6 collective-permute-start.32
  272.2 21.2 %mixer_back.1 = (bf16[1024,1024]{1,0:T(8,128)(2,1)}, bf16[2,1024,768]{2,1,0:T(8,128)(2,1)}, f32[2,1024,1]{2,1,0:T(8,128)}, f32[2,8,256]{2,1,0:T(8,128)}, bf16[10...) custom-call(s32[3]{0:T(128)} %copy-done.8, ...), custom_call_target="tpu_custom_call" | custom-call | tf_op jit(solution)/shard_map/mixer_back/pallas_call | solution.py:602
  295.0 2.9 add_convert_fusion
  298.8 2.6 add_convert_fusion.3
  301.4 5.9 %all-to-all-start = ((bf16[4,128,1152]{2,1,0:T(8,128)(2,1)}), bf16[4,128,1152]{2,1,0:T(8,128)(2,1)S(1)}, u32[]{:S(2)}, u32[]{:S(2)}) async-start(bf16[4,128,1152]{2,1,0:T(8,128)(2,1)} %bitcast.18), calls=%async_computation | async-start | bytes 2359296 | tf_op jit(solution)/shard_map/all_to_all | solution.py:86
  312.3 2.2 convert_add_fusion.4
  314.5 1.5 collective-permute-start.36
  318.1 1.6 add_convert_fusion.2
  319.7 6.7 %back_in.1 = f32[1024,512]{1,0:T(8,128)} custom-call(s32[3]{0:T(128)} %copy-done.8, bf16[2,1024,768]{2,1,0:T(8,128)(2,1)} %get-tuple-element.236.refs_0_, bf16[8,2,128,1024]{3,2,1,0:T(8,128)(2,1)} %copy-done, bf16[1024,1024]{1,0:T(8,128)(2,1)} %copy-done.2, f32[1024,1]{1,0:T(8,128)} %copy-done.5, f32[2,1024,1]{2,1,0:T(8,128)} %get-tuple-element.237.refs_4_, ...), custom_call_target="tpu_custom_call" | custom-call | tf_op jit(solution)/shard_map/back_in/pallas_call | solution.py:218
  326.5 9.4 %collective-permute-done.36 = f32[5,1024]{1,0:T(8,128)S(1)} collective-permute-done((f32[5,1024]{1,0:T(8,128)S(1)}, f32[5,1024]{1,0:T(8,128)S(1)}, u32[]{:S(2)}, u32[]{:S(2)}) %collective-permute-start.36) | collective-permute-done | bytes 20512 | tf_op jit(solution)/shard_map/ppermute | solution.py:19
  340.7 4.8 %all-to-all-start.1 = ((bf16[4,144,1024]{2,1,0:T(8,128)(2,1)}), bf16[4,144,1024]{2,1,0:T(8,128)(2,1)}, u32[]{:S(2)}, u32[]{:S(2)}) async-start(bf16[4,144,1024]{2,1,0:T(8,128)(2,1)} %pad_maximum_fusion.1), calls=%async_computation.1 | async-start | bytes 2359296 | tf_op jit(solution)/shard_map/all_to_all | solution.py:86
  345.6 2.3 multiply_add_fusion
  348.2 14.3 %collective-permute-done.40 = bf16[1024,512]{1,0:T(8,128)(2,1)} collective-permute-done((bf16[1024,512]{1,0:T(8,128)(2,1)}, bf16[1024,512]{1,0:T(8,128)(2,1)}, u32[]{:S(2)}, u32[]{:S(2)}) %collective-permute-start.40) | collective-permute-done | bytes 1048608 | tf_op jit(solution)/shard_map/ppermute | solution.py:19
  362.5 1.6 add_convert_fusion.6
  365.7 1.6 maximum_select_fusion.5
  368.5 3.9 %all-to-all-done.1 = bf16[4,144,1024]{2,1,0:T(8,128)(2,1)} async-done(((bf16[4,144,1024]{2,1,0:T(8,128)(2,1)}), bf16[4,144,1024]{2,1,0:T(8,128)(2,1)}, u32[]{:S(2)}, u32[]{:S(2)}) %all-to-all-start.1) | async-done | bytes 1179680 | tf_op jit(solution)/shard_map/all_to_all | solution.py:86
  (261 shorter events, 61.6 us)
Async XLA Ops:
  7.2 146.5 %all-gather.2.cloned.1.call-start = ((), (), s32[]{:S(2)}) async-start(), calls=%async_computation.2 | async-start | bytes 15040512 | tf_op jit(solution)/shard_map/all_gather | solution.py:688
  9.6 11.9 %collective-permute-start.3 = (bf16[128,1024]{1,0:T(8,128)(2,1)S(1)}, bf16[128,1024]{1,0:T(8,128)(2,1)S(1)}, u32[]{:S(2)}, u32[]{:S(2)}) collective-permute-start(bf16[128,1024]{1,0:T(8,128)(2,1)S(1)} %pad_maximum_fusion.3), channel_id=1, source_target_pairs={{0,12},{4,0},{8,4},{12,8},{1,13},{5,1},{9,5},{13,9},{2,14},{6,2},{... | collective-permute-start | bytes 786440 | tf_op jit(solution)/shard_map/ppermute | solution.py:24
  15.5 21.9 %collective-permute-start = (bf16[1024,256]{1,0:T(8,128)(2,1)}, bf16[1024,256]{1,0:T(8,128)(2,1)S(1)}, u32[]{:S(2)}, u32[]{:S(2)}) collective-permute-start(bf16[1024,256]{1,0:T(8,128)(2,1)} %get-tuple-element.324), channel_id=1, source_target_pairs={{0,1},{1,0},{2,3},{3,2},{4,5},{5,4},{6,7},{7,6},{8,9},{9,8},{10,11... | collective-permute-start | bytes 1572872 | tf_op jit(solution)/shard_map/ppermute | solution.py:19
  15.5 21.9 %collective-permute-start.1 = (bf16[1024,256]{1,0:T(8,128)(2,1)S(1)}, bf16[1024,256]{1,0:T(8,128)(2,1)S(1)}, u32[]{:S(2)}, u32[]{:S(2)}) collective-permute-start(bf16[1024,256]{1,0:T(8,128)(2,1)S(1)} %get-tuple-element.140), channel_id=1, source_target_pairs={{0,2},{2,0},{1,3},{3,1},{4,6},{6,4},{5,7},{7,5},{8,10},{10,8},{9,1... | collective-permute-start | bytes 1572872 | tf_op jit(solution)/shard_map/ppermute | solution.py:19
  17.0 23.7 %collective-permute-start.2 = (bf16[1024,256]{1,0:T(8,128)(2,1)}, bf16[1024,256]{1,0:T(8,128)(2,1)S(1)}, u32[]{:S(2)}, u32[]{:S(2)}) collective-permute-start(bf16[1024,256]{1,0:T(8,128)(2,1)} %get-tuple-element.324), channel_id=1, source_target_pairs={{0,3},{1,2},{2,1},{3,0},{4,7},{5,6},{6,5},{7,4},{8,11},{9,10},{10,... | collective-permute-start | bytes 1572872 | tf_op jit(solution)/shard_map/ppermute | solution.py:678
  17.4 20.0 %collective-permute-start.4 = (bf16[128,1024]{1,0:T(8,128)(2,1)S(1)}, bf16[128,1024]{1,0:T(8,128)(2,1)S(1)}, u32[]{:S(2)}, u32[]{:S(2)}) collective-permute-start(bf16[128,1024]{1,0:T(8,128)(2,1)S(1)} %pad_maximum_fusion.3), channel_id=1, source_target_pairs={{0,8},{4,12},{8,0},{12,4},{1,9},{5,13},{9,1},{13,5},{2,10},{6,14},... | collective-permute-start | bytes 786440 | tf_op jit(solution)/shard_map/ppermute | solution.py:24
  21.4 16.0 %collective-permute-start.5 = (bf16[128,1024]{1,0:T(8,128)(2,1)S(1)}, bf16[128,1024]{1,0:T(8,128)(2,1)}, u32[]{:S(2)}, u32[]{:S(2)}) collective-permute-start(bf16[128,1024]{1,0:T(8,128)(2,1)S(1)} %pad_maximum_fusion.3), channel_id=1, source_target_pairs={{0,4},{4,8},{8,12},{12,0},{1,5},{5,9},{9,13},{13,1},{2,6},{6,10},{... | collective-permute-start | bytes 786440 | tf_op jit(solution)/shard_map/ppermute | solution.py:24
  42.1 10.2 %collective-permute-start.7 = (bf16[512,1024]{1,0:T(8,128)(2,1)S(1)}, bf16[512,1024]{1,0:T(8,128)(2,1)}, u32[]{:S(2)}, u32[]{:S(2)}) collective-permute-start(bf16[512,1024]{1,0:T(8,128)(2,1)S(1)} %constant_dynamic-slice_fusion.4), channel_id=1, source_target_pairs={{0,1},{1,0},{2,3},{3,2},{4,5},{5,4},{6,7},{7,6},{8,9},{9,8},{10,11... | collective-permute-start | bytes 3145736 | tf_op jit(solution)/shard_map/ppermute | solution.py:19
  42.4 34.9 %collective-permute-start.6 = (bf16[512,1024]{1,0:T(8,128)(2,1)S(1)}, bf16[512,1024]{1,0:T(8,128)(2,1)}, u32[]{:S(2)}, u32[]{:S(2)}) collective-permute-start(bf16[512,1024]{1,0:T(8,128)(2,1)S(1)} %constant_dynamic-slice_fusion.4), channel_id=1, source_target_pairs={{0,16},{16,0},{1,17},{17,1},{2,18},{18,2},{3,19},{19,3},{4,20},{20... | collective-permute-start | bytes 3145736 | tf_op jit(solution)/shard_map/ppermute | solution.py:19
  43.9 56.5 %copy-start.8 = (s32[3]{0:T(128)}, s32[3]{0:T(128)S(1)}, u32[]{:S(2)}) copy-start(s32[3]{0:T(128)S(1)} %pad_add_fusion.scalars_ref.scalars) | copy-start | bytes 40
  45.3 10.3 %collective-permute-start.8 = (bf16[1024,256]{1,0:T(8,128)(2,1)S(1)}, bf16[1024,256]{1,0:T(8,128)(2,1)S(1)}, u32[]{:S(2)}, u32[]{:S(2)}) collective-permute-start(bf16[1024,256]{1,0:T(8,128)(2,1)S(1)} %get-tuple-element.322), channel_id=1, source_target_pairs={{0,1},{1,0},{2,3},{3,2},{4,5},{5,4},{6,7},{7,6},{8,9},{9,8},{10,11... | collective-permute-start | bytes 1572872 | tf_op jit(solution)/shard_map/ppermute | solution.py:19
  45.4 25.5 %collective-permute-start.10 = (bf16[1024,256]{1,0:T(8,128)(2,1)S(1)}, bf16[1024,256]{1,0:T(8,128)(2,1)S(1)}, u32[]{:S(2)}, u32[]{:S(2)}) collective-permute-start(bf16[1024,256]{1,0:T(8,128)(2,1)S(1)} %get-tuple-element.322), channel_id=1, source_target_pairs={{0,3},{1,2},{2,1},{3,0},{4,7},{5,6},{6,5},{7,4},{8,11},{9,10},{10,... | collective-permute-start | bytes 1572872 | tf_op jit(solution)/shard_map/ppermute | solution.py:678
  47.0 23.9 %collective-permute-start.9 = (bf16[1024,256]{1,0:T(8,128)(2,1)S(1)}, bf16[1024,256]{1,0:T(8,128)(2,1)S(1)}, u32[]{:S(2)}, u32[]{:S(2)}) collective-permute-start(bf16[1024,256]{1,0:T(8,128)(2,1)S(1)} %get-tuple-element.146), channel_id=1, source_target_pairs={{0,2},{2,0},{1,3},{3,1},{4,6},{6,4},{5,7},{7,5},{8,10},{10,8},{9,1... | collective-permute-start | bytes 1572872 | tf_op jit(solution)/shard_map/ppermute | solution.py:19
  48.7 73.4 %copy-start.2 = (bf16[1024,1024]{1,0:T(8,128)(2,1)}, bf16[1024,1024]{1,0:T(8,128)(2,1)S(1)}, u32[]{:S(2)}) copy-start(bf16[1024,1024]{1,0:T(8,128)(2,1)S(1)} %maximum_select_fusion.2.refs_0_.tokens.refs_2_) | copy-start | bytes 6291460
  77.3 2.9 collective-permute-start.12
  77.4 10.2 %collective-permute-start.14 = (bf16[3,256]{1,0:T(4,128)(2,1)S(1)}, bf16[3,256]{1,0:T(4,128)(2,1)S(1)}, u32[]{:S(2)}, u32[]{:S(2)}) collective-permute-start(bf16[3,256]{1,0:T(4,128)(2,1)S(1)} %copy-done.59), channel_id=1, source_target_pairs={{0,1},{1,0},{2,3},{3,2},{4,5},{5,4},{6,7},{7,6},{8,9},{9,8},{10,11... | collective-permute-start | bytes 4616 | tf_op jit(solution)/shard_map/ppermute | solution.py:19
  85.4 8.3 %collective-permute-start.13 = (bf16[2,2,256]{2,1,0:T(2,128)(2,1)S(1)}, bf16[2,2,256]{2,1,0:T(2,128)(2,1)S(1)}, u32[]{:S(2)}, u32[]{:S(2)}) collective-permute-start(bf16[2,2,256]{2,1,0:T(2,128)(2,1)S(1)} %slice.166), channel_id=1, source_target_pairs={{0,1},{1,4},{4,5},{5,8},{8,9},{9,12},{12,13},{2,3},{3,6},{6,7},{7,... | collective-permute-start | bytes 6152 | tf_op jit(solution)/shard_map/ppermute | solution.py:726
  97.0 25.2 %collective-permute-start.15 = (bf16[512,1024]{1,0:T(8,128)(2,1)S(1)}, bf16[512,1024]{1,0:T(8,128)(2,1)S(1)}, u32[]{:S(2)}, u32[]{:S(2)}) collective-permute-start(bf16[512,1024]{1,0:T(8,128)(2,1)S(1)} %get-tuple-element.156), channel_id=1, source_target_pairs={{0,2},{2,0},{1,3},{3,1},{4,6},{6,4},{5,7},{7,5},{8,10},{10,8},{9,1... | collective-permute-start | bytes 3145736 | tf_op jit(solution)/shard_map/ppermute | solution.py:19
  100.2 25.6 %collective-permute-start.11 = (bf16[1024,1024]{1,0:T(8,128)(2,1)S(1)}, bf16[1024,1024]{1,0:T(8,128)(2,1)S(1)}, u32[]{:S(2)}, u32[]{:S(2)}) collective-permute-start(bf16[1024,1024]{1,0:T(8,128)(2,1)S(1)} %pad_maximum_fusion.cot.refs_0_), channel_id=1, source_target_pairs={{0,1},{1,0},{2,3},{3,2},{4,5},{5,4},{6,7},{7,6},{8,9},{9,8},{10,11... | collective-permute-start | bytes 6291464 | tf_op jit(solution)/shard_map/ppermute | solution.py:19
  124.2 24.4 %collective-permute-start.16 = (bf16[512,1024]{1,0:T(8,128)(2,1)S(1)}, bf16[512,1024]{1,0:T(8,128)(2,1)S(1)}, u32[]{:S(2)}, u32[]{:S(2)}) collective-permute-start(bf16[512,1024]{1,0:T(8,128)(2,1)S(1)} %multiply_convert_fusion.h_own), channel_id=1, source_target_pairs={{0,2},{2,0},{1,3},{3,1},{4,6},{6,4},{5,7},{7,5},{8,10},{10,8},{9,1... | collective-permute-start | bytes 3145736 | tf_op jit(solution)/shard_map/ppermute | solution.py:19
  176.3 12.0 %collective-permute-start.17 = (bf16[1024,1152]{1,0:T(8,128)(2,1)}, bf16[1024,1152]{1,0:T(8,128)(2,1)}, u32[]{:S(2)}, u32[]{:S(2)}) collective-permute-start(bf16[1024,1152]{1,0:T(8,128)(2,1)} %get-tuple-element.200.refs_5_), channel_id=1, source_target_pairs={{0,1},{1,0},{2,3},{3,2},{4,5},{5,4},{6,7},{7,6},{8,9},{9,8},{10,11... | collective-permute-start | bytes 7077896 | tf_op jit(solution)/shard_map/ppermute | solution.py:19
  176.7 11.6 %collective-permute-start.18 = (bf16[1024,1024]{1,0:T(8,128)(2,1)}, bf16[1024,1024]{1,0:T(8,128)(2,1)S(1)}, u32[]{:S(2)}, u32[]{:S(2)}) collective-permute-start(bf16[1024,1024]{1,0:T(8,128)(2,1)} %get-tuple-element.166.refs_0_), channel_id=1, source_target_pairs={{0,1},{1,0},{2,3},{3,2},{4,5},{5,4},{6,7},{7,6},{8,9},{9,8},{10,11... | collective-permute-start | bytes 6291464 | tf_op jit(solution)/shard_map/ppermute | solution.py:19
  188.3 11.6 %collective-permute-start.19 = (bf16[1024,1152]{1,0:T(8,128)(2,1)S(1)}, bf16[1024,1152]{1,0:T(8,128)(2,1)}, u32[]{:S(2)}, u32[]{:S(2)}) collective-permute-start(bf16[1024,1152]{1,0:T(8,128)(2,1)S(1)} %copy-done.17), channel_id=1, source_target_pairs={{0,1},{1,0},{2,3},{3,2},{4,5},{5,4},{6,7},{7,6},{8,9},{9,8},{10,11... | collective-permute-start | bytes 7077896 | tf_op jit(solution)/shard_map/ppermute | solution.py:19
  188.6 11.3 %collective-permute-start.20 = (bf16[1024,1152]{1,0:T(8,128)(2,1)S(1)}, bf16[1024,1152]{1,0:T(8,128)(2,1)}, u32[]{:S(2)}, u32[]{:S(2)}) collective-permute-start(bf16[1024,1152]{1,0:T(8,128)(2,1)S(1)} %copy-done.18), channel_id=1, source_target_pairs={{0,1},{1,0},{2,3},{3,2},{4,5},{5,4},{6,7},{7,6},{8,9},{9,8},{10,11... | collective-permute-start | bytes 7077896 | tf_op jit(solution)/shard_map/ppermute | solution.py:19
  200.0 28.5 %collective-permute-start.22 = (bf16[512,1152]{1,0:T(8,128)(2,1)}, bf16[512,1152]{1,0:T(8,128)(2,1)}, u32[]{:S(2)}, u32[]{:S(2)}) collective-permute-start(bf16[512,1152]{1,0:T(8,128)(2,1)} %get-tuple-element.188), channel_id=1, source_target_pairs={{0,16},{16,0},{1,17},{17,1},{2,18},{18,2},{3,19},{19,3},{4,20},{20... | collective-permute-start | bytes 3538952 | tf_op jit(solution)/shard_map/ppermute | solution.py:29
  200.6 25.3 %collective-permute-start.21 = (bf16[512,1024]{1,0:T(8,128)(2,1)}, bf16[512,1024]{1,0:T(8,128)(2,1)S(1)}, u32[]{:S(2)}, u32[]{:S(2)}) collective-permute-start(bf16[512,1024]{1,0:T(8,128)(2,1)} %back_hidden.1), channel_id=1, source_target_pairs={{0,2},{2,0},{1,3},{3,1},{4,6},{6,4},{5,7},{7,5},{8,10},{10,8},{9,1... | collective-permute-start | bytes 3145736 | tf_op jit(solution)/shard_map/ppermute | solution.py:19
  233.7 28.6 %collective-permute-start.24 = (bf16[512,1152]{1,0:T(8,128)(2,1)}, bf16[512,1152]{1,0:T(8,128)(2,1)S(1)}, u32[]{:S(2)}, u32[]{:S(2)}) collective-permute-start(bf16[512,1152]{1,0:T(8,128)(2,1)} %get-tuple-element.204), channel_id=1, source_target_pairs={{0,16},{16,0},{1,17},{17,1},{2,18},{18,2},{3,19},{19,3},{4,20},{20... | collective-permute-start | bytes 3538952 | tf_op jit(solution)/shard_map/ppermute | solution.py:29
  234.3 27.9 %collective-permute-start.23 = (bf16[512,1024]{1,0:T(8,128)(2,1)S(1)}, bf16[512,1024]{1,0:T(8,128)(2,1)S(1)}, u32[]{:S(2)}, u32[]{:S(2)}) collective-permute-start(bf16[512,1024]{1,0:T(8,128)(2,1)S(1)} %add_convert_fusion.4.own), channel_id=1, source_target_pairs={{0,2},{2,0},{1,3},{3,1},{4,6},{6,4},{5,7},{7,5},{8,10},{10,8},{9,1... | collective-permute-start | bytes 3145736 | tf_op jit(solution)/shard_map/ppermute | solution.py:19
  235.8 26.4 %collective-permute-start.25 = (bf16[128,1152]{1,0:T(8,128)(2,1)S(1)}, bf16[128,1152]{1,0:T(8,128)(2,1)S(1)}, u32[]{:S(2)}, u32[]{:S(2)}) collective-permute-start(bf16[128,1152]{1,0:T(8,128)(2,1)S(1)} %get-tuple-element.205), channel_id=1, source_target_pairs={{0,4},{4,8},{8,12},{12,0},{1,5},{5,9},{9,13},{13,1},{2,6},{6,10},{... | collective-permute-start | bytes 884744 | tf_op jit(solution)/shard_map/ppermute | solution.py:29
  235.8 26.4 %collective-permute-start.26 = (bf16[128,1152]{1,0:T(8,128)(2,1)S(1)}, bf16[128,1152]{1,0:T(8,128)(2,1)S(1)}, u32[]{:S(2)}, u32[]{:S(2)}) collective-permute-start(bf16[128,1152]{1,0:T(8,128)(2,1)S(1)} %get-tuple-element.206), channel_id=1, source_target_pairs={{0,8},{4,12},{8,0},{12,4},{1,9},{5,13},{9,1},{13,5},{2,10},{6,14},... | collective-permute-start | bytes 884744 | tf_op jit(solution)/shard_map/ppermute | solution.py:29
  237.7 24.5 %collective-permute-start.27 = (bf16[128,1152]{1,0:T(8,128)(2,1)S(1)}, bf16[128,1152]{1,0:T(8,128)(2,1)S(1)}, u32[]{:S(2)}, u32[]{:S(2)}) collective-permute-start(bf16[128,1152]{1,0:T(8,128)(2,1)S(1)} %get-tuple-element.207), channel_id=1, source_target_pairs={{0,12},{4,0},{8,4},{12,8},{1,13},{5,1},{9,5},{13,9},{2,14},{6,2},{... | collective-permute-start | bytes 884744 | tf_op jit(solution)/shard_map/ppermute | solution.py:29
  262.6 3.0 collective-permute-start.28
  265.7 28.1 %collective-permute-start.29 = (bf16[512,1152]{1,0:T(8,128)(2,1)}, bf16[512,1152]{1,0:T(8,128)(2,1)}, u32[]{:S(2)}, u32[]{:S(2)}) collective-permute-start(bf16[512,1152]{1,0:T(8,128)(2,1)} %get-tuple-element.223), channel_id=1, source_target_pairs={{0,16},{16,0},{1,17},{17,1},{2,18},{18,2},{3,19},{19,3},{4,20},{20... | collective-permute-start | bytes 3538952 | tf_op jit(solution)/shard_map/ppermute | solution.py:29
  267.1 26.3 %collective-permute-start.30 = (bf16[128,1152]{1,0:T(8,128)(2,1)S(1)}, bf16[128,1152]{1,0:T(8,128)(2,1)S(1)}, u32[]{:S(2)}, u32[]{:S(2)}) collective-permute-start(bf16[128,1152]{1,0:T(8,128)(2,1)S(1)} %get-tuple-element.224), channel_id=1, source_target_pairs={{0,4},{4,8},{8,12},{12,0},{1,5},{5,9},{9,13},{13,1},{2,6},{6,10},{... | collective-permute-start | bytes 884744 | tf_op jit(solution)/shard_map/ppermute | solution.py:29
  269.1 24.3 %collective-permute-start.31 = (bf16[128,1152]{1,0:T(8,128)(2,1)S(1)}, bf16[128,1152]{1,0:T(8,128)(2,1)}, u32[]{:S(2)}, u32[]{:S(2)}) collective-permute-start(bf16[128,1152]{1,0:T(8,128)(2,1)S(1)} %get-tuple-element.225), channel_id=1, source_target_pairs={{0,8},{4,12},{8,0},{12,4},{1,9},{5,13},{9,1},{13,5},{2,10},{6,14},... | collective-permute-start | bytes 884744 | tf_op jit(solution)/shard_map/ppermute | solution.py:29
  270.6 22.9 %collective-permute-start.32 = (bf16[128,1152]{1,0:T(8,128)(2,1)S(1)}, bf16[128,1152]{1,0:T(8,128)(2,1)}, u32[]{:S(2)}, u32[]{:S(2)}) collective-permute-start(bf16[128,1152]{1,0:T(8,128)(2,1)S(1)} %get-tuple-element.226), channel_id=1, source_target_pairs={{0,12},{4,0},{8,4},{12,8},{1,13},{5,1},{9,5},{13,9},{2,14},{6,2},{... | collective-permute-start | bytes 884744 | tf_op jit(solution)/shard_map/ppermute | solution.py:29
  293.8 5.0 %collective-permute-start.33 = (bf16[1024,1024]{1,0:T(8,128)(2,1)}, bf16[1024,1024]{1,0:T(8,128)(2,1)}, u32[]{:S(2)}, u32[]{:S(2)}) collective-permute-start(bf16[1024,1024]{1,0:T(8,128)(2,1)} %get-tuple-element.234), channel_id=1, source_target_pairs={{0,1},{1,0},{2,3},{3,2},{4,5},{5,4},{6,7},{7,6},{8,9},{9,8},{10,11... | collective-permute-start | bytes 6291464 | tf_op jit(solution)/shard_map/ppermute | solution.py:19
  301.4 37.0 %all-to-all-start = ((bf16[4,128,1152]{2,1,0:T(8,128)(2,1)}), bf16[4,128,1152]{2,1,0:T(8,128)(2,1)S(1)}, u32[]{:S(2)}, u32[]{:S(2)}) async-start(bf16[4,128,1152]{2,1,0:T(8,128)(2,1)} %bitcast.18), calls=%async_computation | async-start | bytes 2359296 | tf_op jit(solution)/shard_map/all_to_all | solution.py:86
  309.8 27.7 %collective-permute-start.34 = (bf16[1024,512]{1,0:T(8,128)(2,1)}, bf16[1024,512]{1,0:T(8,128)(2,1)S(1)}, u32[]{:S(2)}, u32[]{:S(2)}) collective-permute-start(bf16[1024,512]{1,0:T(8,128)(2,1)} %get-tuple-element.235), channel_id=1, source_target_pairs={{0,2},{2,0},{1,3},{3,1},{4,6},{6,4},{5,7},{7,5},{8,10},{10,8},{9,1... | collective-permute-start | bytes 3145736 | tf_op jit(solution)/shard_map/ppermute | solution.py:19
  310.4 28.1 %collective-permute-start.39 = (bf16[512,1024]{1,0:T(8,128)(2,1)}, bf16[512,1024]{1,0:T(8,128)(2,1)S(1)}, u32[]{:S(2)}, u32[]{:S(2)}) collective-permute-start(bf16[512,1024]{1,0:T(8,128)(2,1)} %add_convert_fusion.3), channel_id=1, source_target_pairs={{0,16},{16,0},{1,17},{17,1},{2,18},{18,2},{3,19},{19,3},{4,20},{20... | collective-permute-start | bytes 3145736 | tf_op jit(solution)/shard_map/ppermute | solution.py:29
  312.2 2.3 collective-permute-start.35
  314.5 21.3 %collective-permute-start.36 = (f32[5,1024]{1,0:T(8,128)S(1)}, f32[5,1024]{1,0:T(8,128)S(1)}, u32[]{:S(2)}, u32[]{:S(2)}) collective-permute-start(f32[5,1024]{1,0:T(8,128)S(1)} %fusion.3), channel_id=1, source_target_pairs={{0,2},{2,0},{1,3},{3,1},{4,6},{6,4},{5,7},{7,5},{8,10},{10,8},{9,1... | collective-permute-start | bytes 61448 | tf_op jit(solution)/shard_map/ppermute | solution.py:19
  316.1 20.2 %collective-permute-start.37 = (f32[5,1024]{1,0:T(8,128)S(1)}, f32[5,1024]{1,0:T(8,128)S(1)}, u32[]{:S(2)}, u32[]{:S(2)}) collective-permute-start(f32[5,1024]{1,0:T(8,128)S(1)} %fusion.3), channel_id=1, source_target_pairs={{0,16},{16,0},{1,17},{17,1},{2,18},{18,2},{3,19},{19,3},{4,20},{20... | collective-permute-start | bytes 61448 | tf_op jit(solution)/shard_map/ppermute | solution.py:19
  317.6 19.9 %collective-permute-start.38 = (f32[5,1024]{1,0:T(8,128)S(1)}, f32[5,1024]{1,0:T(8,128)S(1)}, u32[]{:S(2)}, u32[]{:S(2)}) collective-permute-start(f32[5,1024]{1,0:T(8,128)S(1)} %fusion.3), channel_id=1, source_target_pairs={{0,18},{2,16},{16,2},{18,0},{1,19},{3,17},{17,3},{19,1},{4,22},{6,... | collective-permute-start | bytes 61448 | tf_op jit(solution)/shard_map/ppermute | solution.py:852
  338.5 24.0 %collective-permute-start.40 = (bf16[1024,512]{1,0:T(8,128)(2,1)}, bf16[1024,512]{1,0:T(8,128)(2,1)}, u32[]{:S(2)}, u32[]{:S(2)}) collective-permute-start(bf16[1024,512]{1,0:T(8,128)(2,1)} %get-tuple-element.245), channel_id=1, source_target_pairs={{0,2},{2,0},{1,3},{3,1},{4,6},{6,4},{5,7},{7,5},{8,10},{10,8},{9,1... | collective-permute-start | bytes 3145736 | tf_op jit(solution)/shard_map/ppermute | solution.py:19
  340.7 31.7 %all-to-all-start.1 = ((bf16[4,144,1024]{2,1,0:T(8,128)(2,1)}), bf16[4,144,1024]{2,1,0:T(8,128)(2,1)}, u32[]{:S(2)}, u32[]{:S(2)}) async-start(bf16[4,144,1024]{2,1,0:T(8,128)(2,1)} %pad_maximum_fusion.1), calls=%async_computation.1 | async-start | bytes 2359296 | tf_op jit(solution)/shard_map/all_to_all | solution.py:86
  348.1 17.6 %collective-permute-start.42 = (f32[1024,256]{1,0:T(8,128)S(1)}, f32[1024,256]{1,0:T(8,128)S(1)}, u32[]{:S(2)}, u32[]{:S(2)}) collective-permute-start(f32[1024,256]{1,0:T(8,128)S(1)} %get-tuple-element.311), channel_id=1, source_target_pairs={{0,1},{1,0},{2,3},{3,2},{4,5},{5,4},{6,7},{7,6},{8,9},{9,8},{10,11... | collective-permute-start | bytes 3145736 | tf_op jit(solution)/shard_map/ppermute | solution.py:19
  364.7 2.6 collective-permute-start.41
  (58 other events, 495.9 us)
Sparse Core Ops, SparseCore 0:
  40.9 112.7 all-gather.1

commit v5 on v4

--- a/solution.py
+++ b/solution.py
@@ -862,19 +862,17 @@
         arrived, kept, up_got, sums, for_self(own, other), *pieces
     )
     sums = (sums[0] + sums[1]) + (sums[2] + sums[3]) if nx == 2 else sums[0]
-    mixer_mine = add_dp(keep, pieces)
+    mixer_parts = [keep, *pieces]
 
     high = sums.astype(BF16)
     low = (sums - high.astype(F32)).astype(BF16)
     extra = jnp.concatenate([high, low, jnp.zeros((16 - 2 * sums.shape[0], features), BF16)], 0)
-    mixer_mine = jnp.concatenate(
-        [
-            mixer_mine.reshape(nz, chunk, features),
-            jnp.broadcast_to(extra, (nz, 16, features)),
-        ],
-        1,
-    )
-    mixer_got = to_tok(mixer_mine.reshape(nz * (chunk + 16), features))
+    extra_own = jnp.concatenate([jnp.zeros((chunk, features), BF16), extra], 0)
+    mixer_mine = [
+        jnp.concatenate([for_tok(mixer_parts, i).astype(BF16), extra], 0) for i in range(1, nz)
+    ]
+    arrived, *mixer_mine = tie(arrived, *mixer_mine)
+    mixer_got = [deliver(part, "tok", i + 1) for i, part in enumerate(mixer_mine)]
     made_sent, arrived = tie(made_sent, arrived)
     made_arrived = swap(made_sent, "y")
 
@@ -895,9 +893,18 @@
     )
     mixed = by_core(out_near)
     grad_up = add_tok(up_got)
-    mixer_sum = add_tok(mixer_got)
-    grad_mixer = mixer_sum[:chunk]
-    sums = mixer_sum[chunk : chunk + 5] + mixer_sum[chunk + 5 : chunk + 10]
+    mixed, input_gradient, *mixer_got = tie(mixed, input_gradient, *mixer_got)
+    grad_mixer = total([for_tok(mixer_parts, 0), *[part[:chunk] for part in mixer_got]])
+    sums = [part[chunk : chunk + 10].astype(F32) for part in (extra_own, *mixer_got)]
+    if nz == 4:
+        sums = (sums[0] + sums[2]) + (sums[1] + sums[3])
+    else:
+        by_tok = jnp.stack(sums)
+        sums = sum(
+            (lax.dynamic_index_in_dim(by_tok, (z - i) % nz, 0, False) for i in range(nz)),
+            jnp.zeros_like(sums[0]),
+        )
+    sums = sums[:5] + sums[5:]
     grad_in = grad_mixer[:, : 3 * width].reshape(chunk, 3, width)
     grad_out = grad_mixer[:, 3 * width :].T
 

time: 386 us -> 383 us (level)
  waiting for transfers between devices: 129 us -> 124 us
    ppermute x10 -> x13, starting transfers between devices: 12.6 us -> 17.6 us  [deliver(): lax.ppermute(value, axis, [(s, (s + distance) % size) for s in range(size)])]
    all_to_all x2 -> x1, starting transfers between devices: 10.7 us -> 6.64 us  [to_tok(): return lax.all_to_all(mine, 'tok', split_axis=0, concat_axis=0, tiled=True)]
    unnamed x135 -> x136, local copies, waits for them, and re-layouts: 14.8 us -> 16 us
  transfers between devices with their start and end apart: 46 -> 48, of which waited for: 19 -> 19; matrix products, arithmetic and copies ran while one was open for 10% -> 9% of each run, Pallas kernels for 28% -> 28%
where the time goes in v5:
time: 383 us; the launch traced here: 379 us
  Pallas kernels  129 us (34%)
  waiting for transfers between devices  124 us (32%)
  starting transfers between devices  51.9 us (14%)
  other arithmetic  36.9 us (10%)
  local copies, waits for them, and re-layouts  21.9 us (6%)
  between operations  15.1 us (4%)
    ppermute x24, waiting for transfers between devices, swap(): return lax.ppermute(value, axis, [(0, 1), (1, 0)])  95 us
    pallas_call x10, Pallas kernels, run_jobs(): pl.pallas_call(kernel, out_shape=shapes, grid_spec=pltpu.PrefetchScalarGr...  85 us
    pallas_call x1, Pallas kernels, hidden_units(): pl.pallas_call(hidden_kernel, out_shape=[jax.ShapeDtypeStruct((rows, feat...  22.7 us
    pallas_call x1, Pallas kernels, mixer_back(): pl.pallas_call(mixer_back_kernel, out_shape=[jax.ShapeDtypeStruct((rows,...  21.2 us
    ppermute x13, starting transfers between devices, deliver(): lax.ppermute(value, axis, [(s, (s + distance) % size) for s in range(size)])  17.6 us
    ppermute x3, waiting for transfers between devices, fetch(): lax.ppermute(value, axis, [(s, (s - distance) % size) for s in range(size)])  16.9 us
    ppermute x24, starting transfers between devices, swap(): return lax.ppermute(value, axis, [(0, 1), (1, 0)])  16.4 us
    unnamed x136, local copies, waits for them, and re-layouts  16 us
  transfers between devices with their start and end apart: 48, of which 19 were waited for; matrix products, arithmetic and copies ran while one was open for 9% of the time, Pallas kernels for 28%

profile of v5, /device:TPU:0, one launch (start us, length us, event | category | flops | bytes accessed | tf_op | source)
XLA Modules:
  0.0 379.1 jit_solution(6718082236076800858)
XLA Ops:
  9.6 5.1 %collective-permute-start.3 = (bf16[128,1024]{1,0:T(8,128)(2,1)S(1)}, bf16[128,1024]{1,0:T(8,128)(2,1)S(1)}, u32[]{:S(2)}, u32[]{:S(2)}) collective-permute-start(bf16[128,1024]{1,0:T(8,128)(2,1)S(1)} %pad_maximum_fusion.8), channel_id=1, source_target_pairs={{0,12},{4,0},{8,4},{12,8},{1,13},{5,1},{9,5},{13,9},{2,14},{6,2},{... | collective-permute-start | bytes 786440 | tf_op jit(solution)/shard_map/ppermute | solution.py:24
  18.5 2.9 collective-permute-done.3
  21.4 1.9 pad_maximum_fusion.1
  23.4 14.1 %collective-permute-done.4 = bf16[128,1024]{1,0:T(8,128)(2,1)S(1)} collective-permute-done((bf16[128,1024]{1,0:T(8,128)(2,1)S(1)}, bf16[128,1024]{1,0:T(8,128)(2,1)S(1)}, u32[]{:S(2)}, u32[]{:S(2)}) %collective-permute-start.4) | collective-permute-done | bytes 262176 | tf_op jit(solution)/shard_map/ppermute | solution.py:24
  37.4 3.3 collective-permute-done.2
  45.7 1.6 collective-permute-start.10
  47.8 1.8 maximum_select_fusion.6
  54.0 3.9 %maximum_select_fusion.1 = bf16[4,2,128,1024]{3,2,1,0:T(8,128)(2,1)} fusion(bf16[4,1,128,1024]{3,2,1,0:T(8,128)(2,1)} %bitcast.4, bf16[4,1,128,1024]{3,2,1,0:T(8,128)(2,1)} %bitcast.3, pred[]{:T(512)S(6)} %eq.40), kind=kLoop, calls=%fused_computation.2 | loop fusion | flops 3145728 | bytes 4194305 | tf_op jit(solution)/shard_map/jit(_where)/select_n | solution.py:64
  57.9 13.3 %collective-permute-done.9 = bf16[1024,256]{1,0:T(8,128)(2,1)S(1)} collective-permute-done((bf16[1024,256]{1,0:T(8,128)(2,1)S(1)}, bf16[1024,256]{1,0:T(8,128)(2,1)S(1)}, u32[]{:S(2)}, u32[]{:S(2)}) %collective-permute-start.9) | collective-permute-done | bytes 524320 | tf_op jit(solution)/shard_map/ppermute | solution.py:19
  72.0 7.1 %collective-permute-done.6 = bf16[512,1024]{1,0:T(8,128)(2,1)} collective-permute-done((bf16[512,1024]{1,0:T(8,128)(2,1)}, bf16[512,1024]{1,0:T(8,128)(2,1)}, u32[]{:S(2)}, u32[]{:S(2)}) %collective-permute-start.6) | collective-permute-done | bytes 1048608 | tf_op jit(solution)/shard_map/ppermute | solution.py:19
  79.6 2.5 collective-permute-done.12
  82.1 2.7 maximum_select_fusion.4
  87.9 2.2 collective-permute-start.13
  90.2 6.0 %project.1.refs_0_.proj = f32[2,1024,768]{2,1,0:T(8,128)S(1)} custom-call(s32[3]{0:T(128)S(1)} %pad_add_fusion.scalars_ref.scalars, bf16[1024,1024]{1,0:T(8,128)(2,1)S(1)} %copy-done.4, bf16[8,2,128,1024]{3,2,1,0:T(8,128)(2,1)S(1)} %maximum_select_fusion.refs_1_.refs_2_.refs_3_.w_out.w_in), custom_call_target="tpu_custom_call" | custom-call | tf_op jit(solution)/shard_map/project/pallas_call | solution.py:218
  96.2 3.2 mix.1
  99.5 1.6 collective-permute-start.15
  103.0 2.3 project_out.1
  105.3 19.3 %collective-permute-done.15 = bf16[512,1024]{1,0:T(8,128)(2,1)S(1)} collective-permute-done((bf16[512,1024]{1,0:T(8,128)(2,1)S(1)}, bf16[512,1024]{1,0:T(8,128)(2,1)S(1)}, u32[]{:S(2)}, u32[]{:S(2)}) %collective-permute-start.15) | collective-permute-done | bytes 1048608 | tf_op jit(solution)/shard_map/ppermute | solution.py:19
  126.7 1.6 collective-permute-start.16
  129.6 21.5 %collective-permute-done.16.h_other = bf16[512,1024]{1,0:T(8,128)(2,1)S(1)} collective-permute-done((bf16[512,1024]{1,0:T(8,128)(2,1)S(1)}, bf16[512,1024]{1,0:T(8,128)(2,1)S(1)}, u32[]{:S(2)}, u32[]{:S(2)}) %collective-permute-start.16) | collective-permute-done | bytes 1048608 | tf_op jit(solution)/shard_map/ppermute | solution.py:19
  151.1 2.5 all-gather.2.cloned.1.call-done
  153.7 22.7 %hidden_units.1 = (bf16[1024,1024]{1,0:T(8,128)(2,1)}, bf16[1024,1152]{1,0:T(8,128)(2,1)}, bf16[1024,1152]{1,0:T(8,128)(2,1)}, bf16[1024,1152]{1,0:T(8,128)(2,1)...) custom-call(s32[3]{0:T(128)} %copy-done.8, bf16[512,1024]{1,0:T(8,128)(2,1)} %copy-done.23, ...), custom_call_target="tpu_custom_call" | custom-call | tf_op jit(solution)/shard_map/hidden_units/pallas_call | solution.py:171
  176.9 11.4 %back_hidden.1 = bf16[512,1024]{1,0:T(8,128)(2,1)} custom-call(s32[3]{0:T(128)} %copy-done.8, bf16[1024,1152]{1,0:T(8,128)(2,1)} %get-tuple-element.190.refs_0_.refs_2_.refs_4_, bf16[1024,1152]{1,0:T(8,128)(2,1)} %get-tuple-element.192.refs_1_.refs_5_, bf16[1024,1152]{1,0:T(8,128)(2,1)} %get-tuple-element.206.refs_2_.refs_6_, ...), custom_call_target="tpu_custom_call" | custom-call | tf_op jit(solution)/shard_map/back_hidden/pallas_call | solution.py:218
  188.9 11.1 %down_gradient.1 = (bf16[512,1152]{1,0:T(8,128)(2,1)}, bf16[512,1152]{1,0:T(8,128)(2,1)}) custom-call(s32[3]{0:T(128)} %copy-done.8, bf16[1024,1024]{1,0:T(8,128)(2,1)} %copy-done.15, bf16[1024,1024]{1,0:T(8,128)(2,1)} %copy-done.26, bf16[1024,1152]{1,0:T(8,128)(2,1)} %get-tuple-element.208.refs_2_.refs_4_, bf16[1024,1152]{1,0:T(8,128)(2,1)} %collective-permute-done.17.refs_3_), custom_call_target="tpu_custom_call" | custom-call | tf_op jit(solution)/shard_map/down_gradient/pallas_call | solution.py:218
  202.1 20.3 %gate_gradient.1 = (bf16[512,1152]{1,0:T(8,128)(2,1)}, bf16[512,1152]{1,0:T(8,128)(2,1)}, bf16[512,1024]{1,0:T(8,128)(2,1)}) custom-call(s32[3]{0:T(128)} %copy-done.8, bf16[1024,1024]{1,0:T(8,128)(2,1)} %get-tuple-element.175.refs_0_, bf16[1024,1024]{1,0:T(8,128)(2,1)} %copy-done.19, bf16[1024,1152]{1,0:T(8,128)(2,1)} %get-tuple-element.190.refs_0_.refs_2_.refs_4_, ...), custom_call_target="tpu_custom_call" | custom-call | tf_op jit(solution)/shard_map/gate_gradient/pallas_call | solution.py:218
  222.4 3.5 collective-permute-done.21
  225.8 2.6 collective-permute-done.22
  228.5 2.1 multiply_reduce_fusion
  231.9 1.7 add_convert_fusion.9
  235.7 2.0 collective-permute-start.26
  237.7 2.4 collective-permute-start.27
  240.9 21.2 %up_gradient.1 = (bf16[512,1152]{1,0:T(8,128)(2,1)}, bf16[512,1152]{1,0:T(8,128)(2,1)}, bf16[1024,512]{1,0:T(8,128)(2,1)}, f32[1024,512]{1,0:T(8,128)}) custom-call(s32[3]{0:T(128)} %copy-done.8, bf16[1024,1024]{1,0:T(8,128)(2,1)} %get-tuple-element.175.refs_0_, bf16[1024,1024]{1,0:T(8,128)(2,1)} %copy-done.19, ...), custom_call_target="tpu_custom_call" | custom-call | tf_op jit(solution)/shard_map/up_gradient/pallas_call | solution.py:218
  267.1 2.0 collective-permute-start.30
  270.6 1.6 collective-permute-start.32
  272.1 21.2 %mixer_back.1 = (bf16[1024,1024]{1,0:T(8,128)(2,1)}, bf16[2,1024,768]{2,1,0:T(8,128)(2,1)}, f32[2,1024,1]{2,1,0:T(8,128)}, f32[2,8,256]{2,1,0:T(8,128)}, bf16[10...) custom-call(s32[3]{0:T(128)} %copy-done.8, ...), custom_call_target="tpu_custom_call" | custom-call | tf_op jit(solution)/shard_map/mixer_back/pallas_call | solution.py:602
  295.9 2.9 collective-permute-done.33
  298.8 2.6 add_convert_fusion.2
  301.5 6.6 %all-to-all-start = ((bf16[4,128,1152]{2,1,0:T(8,128)(2,1)}), bf16[4,128,1152]{2,1,0:T(8,128)(2,1)S(1)}, u32[]{:S(2)}, u32[]{:S(2)}) async-start(bf16[4,128,1152]{2,1,0:T(8,128)(2,1)} %bitcast.18), calls=%async_computation | async-start | bytes 2359296 | tf_op jit(solution)/shard_map/all_to_all | solution.py:86
  313.5 1.5 collective-permute-start.36
  317.1 1.9 add_convert_fusion.1
  319.0 6.7 %back_in.1 = f32[1024,512]{1,0:T(8,128)} custom-call(s32[3]{0:T(128)} %copy-done.8, bf16[2,1024,768]{2,1,0:T(8,128)(2,1)} %get-tuple-element.245.refs_0_, bf16[8,2,128,1024]{3,2,1,0:T(8,128)(2,1)} %copy-done, bf16[1024,1024]{1,0:T(8,128)(2,1)} %copy-done.2, f32[1024,1]{1,0:T(8,128)} %copy-done.5, f32[2,1024,1]{2,1,0:T(8,128)} %get-tuple-element.246.refs_4_, ...), custom_call_target="tpu_custom_call" | custom-call | tf_op jit(solution)/shard_map/back_in/pallas_call | solution.py:218
  325.8 8.8 %collective-permute-done.36 = f32[5,1024]{1,0:T(8,128)S(1)} collective-permute-done((f32[5,1024]{1,0:T(8,128)S(1)}, f32[5,1024]{1,0:T(8,128)S(1)}, u32[]{:S(2)}, u32[]{:S(2)}) %collective-permute-start.36) | collective-permute-done | bytes 20512 | tf_op jit(solution)/shard_map/ppermute | solution.py:19
  337.0 1.6 add_convert_fusion.12
  339.5 2.1 convert_add_fusion.3
  342.4 1.7 collective-permute-start.43
  344.0 1.8 collective-permute-start.44
  347.3 15.8 %collective-permute-done.40 = bf16[1024,512]{1,0:T(8,128)(2,1)S(1)} collective-permute-done((bf16[1024,512]{1,0:T(8,128)(2,1)S(1)}, bf16[1024,512]{1,0:T(8,128)(2,1)S(1)}, u32[]{:S(2)}, u32[]{:S(2)}) %collective-permute-start.40) | collective-permute-done | bytes 1048608 | tf_op jit(solution)/shard_map/ppermute | solution.py:19
  365.2 1.6 maximum_select_fusion.5
  (265 shorter events, 62.3 us)
Async XLA Ops:
  7.2 146.5 %all-gather.2.cloned.1.call-start = ((), (), s32[]{:S(2)}) async-start(), calls=%async_computation.1 | async-start | bytes 15040512 | tf_op jit(solution)/shard_map/all_gather | solution.py:688
  9.6 11.9 %collective-permute-start.3 = (bf16[128,1024]{1,0:T(8,128)(2,1)S(1)}, bf16[128,1024]{1,0:T(8,128)(2,1)S(1)}, u32[]{:S(2)}, u32[]{:S(2)}) collective-permute-start(bf16[128,1024]{1,0:T(8,128)(2,1)S(1)} %pad_maximum_fusion.8), channel_id=1, source_target_pairs={{0,12},{4,0},{8,4},{12,8},{1,13},{5,1},{9,5},{13,9},{2,14},{6,2},{... | collective-permute-start | bytes 786440 | tf_op jit(solution)/shard_map/ppermute | solution.py:24
  15.5 21.9 %collective-permute-start = (bf16[1024,256]{1,0:T(8,128)(2,1)}, bf16[1024,256]{1,0:T(8,128)(2,1)S(1)}, u32[]{:S(2)}, u32[]{:S(2)}) collective-permute-start(bf16[1024,256]{1,0:T(8,128)(2,1)} %get-tuple-element.327), channel_id=1, source_target_pairs={{0,1},{1,0},{2,3},{3,2},{4,5},{5,4},{6,7},{7,6},{8,9},{9,8},{10,11... | collective-permute-start | bytes 1572872 | tf_op jit(solution)/shard_map/ppermute | solution.py:19
  15.5 21.9 %collective-permute-start.1 = (bf16[1024,256]{1,0:T(8,128)(2,1)S(1)}, bf16[1024,256]{1,0:T(8,128)(2,1)S(1)}, u32[]{:S(2)}, u32[]{:S(2)}) collective-permute-start(bf16[1024,256]{1,0:T(8,128)(2,1)S(1)} %get-tuple-element.149), channel_id=1, source_target_pairs={{0,2},{2,0},{1,3},{3,1},{4,6},{6,4},{5,7},{7,5},{8,10},{10,8},{9,1... | collective-permute-start | bytes 1572872 | tf_op jit(solution)/shard_map/ppermute | solution.py:19
  17.0 23.7 %collective-permute-start.2 = (bf16[1024,256]{1,0:T(8,128)(2,1)}, bf16[1024,256]{1,0:T(8,128)(2,1)S(1)}, u32[]{:S(2)}, u32[]{:S(2)}) collective-permute-start(bf16[1024,256]{1,0:T(8,128)(2,1)} %get-tuple-element.327), channel_id=1, source_target_pairs={{0,3},{1,2},{2,1},{3,0},{4,7},{5,6},{6,5},{7,4},{8,11},{9,10},{10,... | collective-permute-start | bytes 1572872 | tf_op jit(solution)/shard_map/ppermute | solution.py:678
  17.4 20.0 %collective-permute-start.4 = (bf16[128,1024]{1,0:T(8,128)(2,1)S(1)}, bf16[128,1024]{1,0:T(8,128)(2,1)S(1)}, u32[]{:S(2)}, u32[]{:S(2)}) collective-permute-start(bf16[128,1024]{1,0:T(8,128)(2,1)S(1)} %pad_maximum_fusion.8), channel_id=1, source_target_pairs={{0,8},{4,12},{8,0},{12,4},{1,9},{5,13},{9,1},{13,5},{2,10},{6,14},... | collective-permute-start | bytes 786440 | tf_op jit(solution)/shard_map/ppermute | solution.py:24
  21.4 16.0 %collective-permute-start.5 = (bf16[128,1024]{1,0:T(8,128)(2,1)S(1)}, bf16[128,1024]{1,0:T(8,128)(2,1)}, u32[]{:S(2)}, u32[]{:S(2)}) collective-permute-start(bf16[128,1024]{1,0:T(8,128)(2,1)S(1)} %pad_maximum_fusion.8), channel_id=1, source_target_pairs={{0,4},{4,8},{8,12},{12,0},{1,5},{5,9},{9,13},{13,1},{2,6},{6,10},{... | collective-permute-start | bytes 786440 | tf_op jit(solution)/shard_map/ppermute | solution.py:24
  43.7 10.3 %collective-permute-start.7 = (bf16[512,1024]{1,0:T(8,128)(2,1)}, bf16[512,1024]{1,0:T(8,128)(2,1)}, u32[]{:S(2)}, u32[]{:S(2)}) collective-permute-start(bf16[512,1024]{1,0:T(8,128)(2,1)} %constant_dynamic-slice_fusion.6), channel_id=1, source_target_pairs={{0,1},{1,0},{2,3},{3,2},{4,5},{5,4},{6,7},{7,6},{8,9},{9,8},{10,11... | collective-permute-start | bytes 3145736 | tf_op jit(solution)/shard_map/ppermute | solution.py:19
  43.9 35.2 %collective-permute-start.6 = (bf16[512,1024]{1,0:T(8,128)(2,1)}, bf16[512,1024]{1,0:T(8,128)(2,1)}, u32[]{:S(2)}, u32[]{:S(2)}) collective-permute-start(bf16[512,1024]{1,0:T(8,128)(2,1)} %constant_dynamic-slice_fusion.6), channel_id=1, source_target_pairs={{0,16},{16,0},{1,17},{17,1},{2,18},{18,2},{3,19},{19,3},{4,20},{20... | collective-permute-start | bytes 3145736 | tf_op jit(solution)/shard_map/ppermute | solution.py:19
  45.6 12.3 %collective-permute-start.8 = (bf16[1024,256]{1,0:T(8,128)(2,1)S(1)}, bf16[1024,256]{1,0:T(8,128)(2,1)S(1)}, u32[]{:S(2)}, u32[]{:S(2)}) collective-permute-start(bf16[1024,256]{1,0:T(8,128)(2,1)S(1)} %get-tuple-element.325), channel_id=1, source_target_pairs={{0,1},{1,0},{2,3},{3,2},{4,5},{5,4},{6,7},{7,6},{8,9},{9,8},{10,11... | collective-permute-start | bytes 1572872 | tf_op jit(solution)/shard_map/ppermute | solution.py:19
  45.7 25.5 %collective-permute-start.10 = (bf16[1024,256]{1,0:T(8,128)(2,1)S(1)}, bf16[1024,256]{1,0:T(8,128)(2,1)S(1)}, u32[]{:S(2)}, u32[]{:S(2)}) collective-permute-start(bf16[1024,256]{1,0:T(8,128)(2,1)S(1)} %get-tuple-element.325), channel_id=1, source_target_pairs={{0,3},{1,2},{2,1},{3,0},{4,7},{5,6},{6,5},{7,4},{8,11},{9,10},{10,... | collective-permute-start | bytes 1572872 | tf_op jit(solution)/shard_map/ppermute | solution.py:678
  47.3 23.9 %collective-permute-start.9 = (bf16[1024,256]{1,0:T(8,128)(2,1)S(1)}, bf16[1024,256]{1,0:T(8,128)(2,1)S(1)}, u32[]{:S(2)}, u32[]{:S(2)}) collective-permute-start(bf16[1024,256]{1,0:T(8,128)(2,1)S(1)} %get-tuple-element.155), channel_id=1, source_target_pairs={{0,2},{2,0},{1,3},{3,1},{4,6},{6,4},{5,7},{7,5},{8,10},{10,8},{9,1... | collective-permute-start | bytes 1572872 | tf_op jit(solution)/shard_map/ppermute | solution.py:19
  79.1 3.0 collective-permute-start.12
  79.1 11.0 %collective-permute-start.14 = (bf16[3,256]{1,0:T(4,128)(2,1)S(1)}, bf16[3,256]{1,0:T(4,128)(2,1)S(1)}, u32[]{:S(2)}, u32[]{:S(2)}) collective-permute-start(bf16[3,256]{1,0:T(4,128)(2,1)S(1)} %copy-done.60), channel_id=1, source_target_pairs={{0,1},{1,0},{2,3},{3,2},{4,5},{5,4},{6,7},{7,6},{8,9},{9,8},{10,11... | collective-permute-start | bytes 4616 | tf_op jit(solution)/shard_map/ppermute | solution.py:19
  87.9 8.3 %collective-permute-start.13 = (bf16[2,2,256]{2,1,0:T(2,128)(2,1)S(1)}, bf16[2,2,256]{2,1,0:T(2,128)(2,1)S(1)}, u32[]{:S(2)}, u32[]{:S(2)}) collective-permute-start(bf16[2,2,256]{2,1,0:T(2,128)(2,1)S(1)} %slice.158), channel_id=1, source_target_pairs={{0,1},{1,4},{4,5},{5,8},{8,9},{9,12},{12,13},{2,3},{3,6},{6,7},{7,... | collective-permute-start | bytes 6152 | tf_op jit(solution)/shard_map/ppermute | solution.py:726
  99.5 25.1 %collective-permute-start.15 = (bf16[512,1024]{1,0:T(8,128)(2,1)S(1)}, bf16[512,1024]{1,0:T(8,128)(2,1)S(1)}, u32[]{:S(2)}, u32[]{:S(2)}) collective-permute-start(bf16[512,1024]{1,0:T(8,128)(2,1)S(1)} %get-tuple-element.165), channel_id=1, source_target_pairs={{0,2},{2,0},{1,3},{3,1},{4,6},{6,4},{5,7},{7,5},{8,10},{10,8},{9,1... | collective-permute-start | bytes 3145736 | tf_op jit(solution)/shard_map/ppermute | solution.py:19
  102.7 25.6 %collective-permute-start.11 = (bf16[1024,1024]{1,0:T(8,128)(2,1)S(1)}, bf16[1024,1024]{1,0:T(8,128)(2,1)S(1)}, u32[]{:S(2)}, u32[]{:S(2)}) collective-permute-start(bf16[1024,1024]{1,0:T(8,128)(2,1)S(1)} %pad_maximum_fusion.cot.refs_0_), channel_id=1, source_target_pairs={{0,1},{1,0},{2,3},{3,2},{4,5},{5,4},{6,7},{7,6},{8,9},{9,8},{10,11... | collective-permute-start | bytes 6291464 | tf_op jit(solution)/shard_map/ppermute | solution.py:19
  126.7 24.4 %collective-permute-start.16 = (bf16[512,1024]{1,0:T(8,128)(2,1)S(1)}, bf16[512,1024]{1,0:T(8,128)(2,1)S(1)}, u32[]{:S(2)}, u32[]{:S(2)}) collective-permute-start(bf16[512,1024]{1,0:T(8,128)(2,1)S(1)} %multiply_convert_fusion.h_own), channel_id=1, source_target_pairs={{0,2},{2,0},{1,3},{3,1},{4,6},{6,4},{5,7},{7,5},{8,10},{10,8},{9,1... | collective-permute-start | bytes 3145736 | tf_op jit(solution)/shard_map/ppermute | solution.py:19
  176.3 11.9 %collective-permute-start.17 = (bf16[1024,1152]{1,0:T(8,128)(2,1)}, bf16[1024,1152]{1,0:T(8,128)(2,1)}, u32[]{:S(2)}, u32[]{:S(2)}) collective-permute-start(bf16[1024,1152]{1,0:T(8,128)(2,1)} %get-tuple-element.209.refs_5_), channel_id=1, source_target_pairs={{0,1},{1,0},{2,3},{3,2},{4,5},{5,4},{6,7},{7,6},{8,9},{9,8},{10,11... | collective-permute-start | bytes 7077896 | tf_op jit(solution)/shard_map/ppermute | solution.py:19
  176.7 11.6 %collective-permute-start.18 = (bf16[1024,1024]{1,0:T(8,128)(2,1)}, bf16[1024,1024]{1,0:T(8,128)(2,1)S(1)}, u32[]{:S(2)}, u32[]{:S(2)}) collective-permute-start(bf16[1024,1024]{1,0:T(8,128)(2,1)} %get-tuple-element.175.refs_0_), channel_id=1, source_target_pairs={{0,1},{1,0},{2,3},{3,2},{4,5},{5,4},{6,7},{7,6},{8,9},{9,8},{10,11... | collective-permute-start | bytes 6291464 | tf_op jit(solution)/shard_map/ppermute | solution.py:19
  188.3 11.6 %collective-permute-start.19 = (bf16[1024,1152]{1,0:T(8,128)(2,1)S(1)}, bf16[1024,1152]{1,0:T(8,128)(2,1)}, u32[]{:S(2)}, u32[]{:S(2)}) collective-permute-start(bf16[1024,1152]{1,0:T(8,128)(2,1)S(1)} %copy-done.17), channel_id=1, source_target_pairs={{0,1},{1,0},{2,3},{3,2},{4,5},{5,4},{6,7},{7,6},{8,9},{9,8},{10,11... | collective-permute-start | bytes 7077896 | tf_op jit(solution)/shard_map/ppermute | solution.py:19
  188.6 11.3 %collective-permute-start.20 = (bf16[1024,1152]{1,0:T(8,128)(2,1)S(1)}, bf16[1024,1152]{1,0:T(8,128)(2,1)}, u32[]{:S(2)}, u32[]{:S(2)}) collective-permute-start(bf16[1024,1152]{1,0:T(8,128)(2,1)S(1)} %copy-done.18), channel_id=1, source_target_pairs={{0,1},{1,0},{2,3},{3,2},{4,5},{5,4},{6,7},{7,6},{8,9},{9,8},{10,11... | collective-permute-start | bytes 7077896 | tf_op jit(solution)/shard_map/ppermute | solution.py:19
  199.9 28.5 %collective-permute-start.22 = (bf16[512,1152]{1,0:T(8,128)(2,1)}, bf16[512,1152]{1,0:T(8,128)(2,1)}, u32[]{:S(2)}, u32[]{:S(2)}) collective-permute-start(bf16[512,1152]{1,0:T(8,128)(2,1)} %get-tuple-element.197), channel_id=1, source_target_pairs={{0,16},{16,0},{1,17},{17,1},{2,18},{18,2},{3,19},{19,3},{4,20},{20... | collective-permute-start | bytes 3538952 | tf_op jit(solution)/shard_map/ppermute | solution.py:29
  200.6 25.3 %collective-permute-start.21 = (bf16[512,1024]{1,0:T(8,128)(2,1)}, bf16[512,1024]{1,0:T(8,128)(2,1)S(1)}, u32[]{:S(2)}, u32[]{:S(2)}) collective-permute-start(bf16[512,1024]{1,0:T(8,128)(2,1)} %back_hidden.1), channel_id=1, source_target_pairs={{0,2},{2,0},{1,3},{3,1},{4,6},{6,4},{5,7},{7,5},{8,10},{10,8},{9,1... | collective-permute-start | bytes 3145736 | tf_op jit(solution)/shard_map/ppermute | solution.py:19
  233.6 28.5 %collective-permute-start.24 = (bf16[512,1152]{1,0:T(8,128)(2,1)}, bf16[512,1152]{1,0:T(8,128)(2,1)S(1)}, u32[]{:S(2)}, u32[]{:S(2)}) collective-permute-start(bf16[512,1152]{1,0:T(8,128)(2,1)} %get-tuple-element.213), channel_id=1, source_target_pairs={{0,16},{16,0},{1,17},{17,1},{2,18},{18,2},{3,19},{19,3},{4,20},{20... | collective-permute-start | bytes 3538952 | tf_op jit(solution)/shard_map/ppermute | solution.py:29
  234.3 27.9 %collective-permute-start.23 = (bf16[512,1024]{1,0:T(8,128)(2,1)S(1)}, bf16[512,1024]{1,0:T(8,128)(2,1)S(1)}, u32[]{:S(2)}, u32[]{:S(2)}) collective-permute-start(bf16[512,1024]{1,0:T(8,128)(2,1)S(1)} %add_convert_fusion.3.own), channel_id=1, source_target_pairs={{0,2},{2,0},{1,3},{3,1},{4,6},{6,4},{5,7},{7,5},{8,10},{10,8},{9,1... | collective-permute-start | bytes 3145736 | tf_op jit(solution)/shard_map/ppermute | solution.py:19
  235.7 26.3 %collective-permute-start.25 = (bf16[128,1152]{1,0:T(8,128)(2,1)S(1)}, bf16[128,1152]{1,0:T(8,128)(2,1)S(1)}, u32[]{:S(2)}, u32[]{:S(2)}) collective-permute-start(bf16[128,1152]{1,0:T(8,128)(2,1)S(1)} %get-tuple-element.214), channel_id=1, source_target_pairs={{0,4},{4,8},{8,12},{12,0},{1,5},{5,9},{9,13},{13,1},{2,6},{6,10},{... | collective-permute-start | bytes 884744 | tf_op jit(solution)/shard_map/ppermute | solution.py:29
  235.7 26.4 %collective-permute-start.26 = (bf16[128,1152]{1,0:T(8,128)(2,1)S(1)}, bf16[128,1152]{1,0:T(8,128)(2,1)S(1)}, u32[]{:S(2)}, u32[]{:S(2)}) collective-permute-start(bf16[128,1152]{1,0:T(8,128)(2,1)S(1)} %get-tuple-element.215), channel_id=1, source_target_pairs={{0,8},{4,12},{8,0},{12,4},{1,9},{5,13},{9,1},{13,5},{2,10},{6,14},... | collective-permute-start | bytes 884744 | tf_op jit(solution)/shard_map/ppermute | solution.py:29
  237.7 24.4 %collective-permute-start.27 = (bf16[128,1152]{1,0:T(8,128)(2,1)S(1)}, bf16[128,1152]{1,0:T(8,128)(2,1)S(1)}, u32[]{:S(2)}, u32[]{:S(2)}) collective-permute-start(bf16[128,1152]{1,0:T(8,128)(2,1)S(1)} %get-tuple-element.216), channel_id=1, source_target_pairs={{0,12},{4,0},{8,4},{12,8},{1,13},{5,1},{9,5},{13,9},{2,14},{6,2},{... | collective-permute-start | bytes 884744 | tf_op jit(solution)/shard_map/ppermute | solution.py:29
  262.6 3.0 collective-permute-start.28
  265.6 27.9 %collective-permute-start.29 = (bf16[512,1152]{1,0:T(8,128)(2,1)}, bf16[512,1152]{1,0:T(8,128)(2,1)S(1)}, u32[]{:S(2)}, u32[]{:S(2)}) collective-permute-start(bf16[512,1152]{1,0:T(8,128)(2,1)} %get-tuple-element.232), channel_id=1, source_target_pairs={{0,16},{16,0},{1,17},{17,1},{2,18},{18,2},{3,19},{19,3},{4,20},{20... | collective-permute-start | bytes 3538952 | tf_op jit(solution)/shard_map/ppermute | solution.py:29
  267.1 26.3 %collective-permute-start.30 = (bf16[128,1152]{1,0:T(8,128)(2,1)S(1)}, bf16[128,1152]{1,0:T(8,128)(2,1)S(1)}, u32[]{:S(2)}, u32[]{:S(2)}) collective-permute-start(bf16[128,1152]{1,0:T(8,128)(2,1)S(1)} %get-tuple-element.233), channel_id=1, source_target_pairs={{0,4},{4,8},{8,12},{12,0},{1,5},{5,9},{9,13},{13,1},{2,6},{6,10},{... | collective-permute-start | bytes 884744 | tf_op jit(solution)/shard_map/ppermute | solution.py:29
  269.1 24.3 %collective-permute-start.31 = (bf16[128,1152]{1,0:T(8,128)(2,1)S(1)}, bf16[128,1152]{1,0:T(8,128)(2,1)S(1)}, u32[]{:S(2)}, u32[]{:S(2)}) collective-permute-start(bf16[128,1152]{1,0:T(8,128)(2,1)S(1)} %get-tuple-element.234), channel_id=1, source_target_pairs={{0,8},{4,12},{8,0},{12,4},{1,9},{5,13},{9,1},{13,5},{2,10},{6,14},... | collective-permute-start | bytes 884744 | tf_op jit(solution)/shard_map/ppermute | solution.py:29
  270.6 22.9 %collective-permute-start.32 = (bf16[128,1152]{1,0:T(8,128)(2,1)S(1)}, bf16[128,1152]{1,0:T(8,128)(2,1)S(1)}, u32[]{:S(2)}, u32[]{:S(2)}) collective-permute-start(bf16[128,1152]{1,0:T(8,128)(2,1)S(1)} %get-tuple-element.235), channel_id=1, source_target_pairs={{0,12},{4,0},{8,4},{12,8},{1,13},{5,1},{9,5},{13,9},{2,14},{6,2},{... | collective-permute-start | bytes 884744 | tf_op jit(solution)/shard_map/ppermute | solution.py:29
  294.3 4.5 %collective-permute-start.33 = (bf16[1024,1024]{1,0:T(8,128)(2,1)}, bf16[1024,1024]{1,0:T(8,128)(2,1)}, u32[]{:S(2)}, u32[]{:S(2)}) collective-permute-start(bf16[1024,1024]{1,0:T(8,128)(2,1)} %get-tuple-element.243), channel_id=1, source_target_pairs={{0,1},{1,0},{2,3},{3,2},{4,5},{5,4},{6,7},{7,6},{8,9},{9,8},{10,11... | collective-permute-start | bytes 6291464 | tf_op jit(solution)/shard_map/ppermute | solution.py:19
  301.5 35.5 %all-to-all-start = ((bf16[4,128,1152]{2,1,0:T(8,128)(2,1)}), bf16[4,128,1152]{2,1,0:T(8,128)(2,1)S(1)}, u32[]{:S(2)}, u32[]{:S(2)}) async-start(bf16[4,128,1152]{2,1,0:T(8,128)(2,1)} %bitcast.18), calls=%async_computation | async-start | bytes 2359296 | tf_op jit(solution)/shard_map/all_to_all | solution.py:86
  308.4 27.8 %collective-permute-start.34 = (bf16[1024,512]{1,0:T(8,128)(2,1)}, bf16[1024,512]{1,0:T(8,128)(2,1)S(1)}, u32[]{:S(2)}, u32[]{:S(2)}) collective-permute-start(bf16[1024,512]{1,0:T(8,128)(2,1)} %get-tuple-element.244), channel_id=1, source_target_pairs={{0,2},{2,0},{1,3},{3,1},{4,6},{6,4},{5,7},{7,5},{8,10},{10,8},{9,1... | collective-permute-start | bytes 3145736 | tf_op jit(solution)/shard_map/ppermute | solution.py:19
  309.0 27.1 %collective-permute-start.39 = (bf16[512,1024]{1,0:T(8,128)(2,1)}, bf16[512,1024]{1,0:T(8,128)(2,1)}, u32[]{:S(2)}, u32[]{:S(2)}) collective-permute-start(bf16[512,1024]{1,0:T(8,128)(2,1)} %add_convert_fusion.2), channel_id=1, source_target_pairs={{0,16},{16,0},{1,17},{17,1},{2,18},{18,2},{3,19},{19,3},{4,20},{20... | collective-permute-start | bytes 3145736 | tf_op jit(solution)/shard_map/ppermute | solution.py:29
  311.0 2.6 collective-permute-start.35
  313.5 21.0 %collective-permute-start.36 = (f32[5,1024]{1,0:T(8,128)S(1)}, f32[5,1024]{1,0:T(8,128)S(1)}, u32[]{:S(2)}, u32[]{:S(2)}) collective-permute-start(f32[5,1024]{1,0:T(8,128)S(1)} %fusion.7), channel_id=1, source_target_pairs={{0,2},{2,0},{1,3},{3,1},{4,6},{6,4},{5,7},{7,5},{8,10},{10,8},{9,1... | collective-permute-start | bytes 61448 | tf_op jit(solution)/shard_map/ppermute | solution.py:19
  315.1 19.9 %collective-permute-start.37 = (f32[5,1024]{1,0:T(8,128)S(1)}, f32[5,1024]{1,0:T(8,128)S(1)}, u32[]{:S(2)}, u32[]{:S(2)}) collective-permute-start(f32[5,1024]{1,0:T(8,128)S(1)} %fusion.7), channel_id=1, source_target_pairs={{0,16},{16,0},{1,17},{17,1},{2,18},{18,2},{3,19},{19,3},{4,20},{20... | collective-permute-start | bytes 61448 | tf_op jit(solution)/shard_map/ppermute | solution.py:19
  316.5 19.7 %collective-permute-start.38 = (f32[5,1024]{1,0:T(8,128)S(1)}, f32[5,1024]{1,0:T(8,128)S(1)}, u32[]{:S(2)}, u32[]{:S(2)}) collective-permute-start(f32[5,1024]{1,0:T(8,128)S(1)} %fusion.7), channel_id=1, source_target_pairs={{0,18},{2,16},{16,2},{18,0},{1,19},{3,17},{17,3},{19,1},{4,22},{6,... | collective-permute-start | bytes 61448 | tf_op jit(solution)/shard_map/ppermute | solution.py:852
  338.9 24.2 %collective-permute-start.40 = (bf16[1024,512]{1,0:T(8,128)(2,1)S(1)}, bf16[1024,512]{1,0:T(8,128)(2,1)S(1)}, u32[]{:S(2)}, u32[]{:S(2)}) collective-permute-start(bf16[1024,512]{1,0:T(8,128)(2,1)S(1)} %copy-done.61), channel_id=1, source_target_pairs={{0,2},{2,0},{1,3},{3,1},{4,6},{6,4},{5,7},{7,5},{8,10},{10,8},{9,1... | collective-permute-start | bytes 3145736 | tf_op jit(solution)/shard_map/ppermute | solution.py:19
  342.3 22.8 %collective-permute-start.42 = (f32[1024,256]{1,0:T(8,128)S(1)}, f32[1024,256]{1,0:T(8,128)S(1)}, u32[]{:S(2)}, u32[]{:S(2)}) collective-permute-start(f32[1024,256]{1,0:T(8,128)S(1)} %get-tuple-element.317), channel_id=1, source_target_pairs={{0,1},{1,0},{2,3},{3,2},{4,5},{5,4},{6,7},{7,6},{8,9},{9,8},{10,11... | collective-permute-start | bytes 3145736 | tf_op jit(solution)/shard_map/ppermute | solution.py:19
  342.4 25.6 %collective-permute-start.43 = (bf16[144,1024]{1,0:T(8,128)(2,1)S(1)}, bf16[144,1024]{1,0:T(8,128)(2,1)S(1)}, u32[]{:S(2)}, u32[]{:S(2)}) collective-permute-start(bf16[144,1024]{1,0:T(8,128)(2,1)S(1)} %get-tuple-element.265), channel_id=1, source_target_pairs={{0,4},{4,8},{8,12},{12,0},{1,5},{5,9},{9,13},{13,1},{2,6},{6,10},{... | collective-permute-start | bytes 884744 | tf_op jit(solution)/shard_map/ppermute | solution.py:29
  344.0 23.9 %collective-permute-start.44 = (bf16[144,1024]{1,0:T(8,128)(2,1)S(1)}, bf16[144,1024]{1,0:T(8,128)(2,1)S(1)}, u32[]{:S(2)}, u32[]{:S(2)}) collective-permute-start(bf16[144,1024]{1,0:T(8,128)(2,1)S(1)} %get-tuple-element.266), channel_id=1, source_target_pairs={{0,8},{4,12},{8,0},{12,4},{1,9},{5,13},{9,1},{13,5},{2,10},{6,14},... | collective-permute-start | bytes 884744 | tf_op jit(solution)/shard_map/ppermute | solution.py:29
  345.8 22.1 %collective-permute-start.45 = (bf16[144,1024]{1,0:T(8,128)(2,1)S(1)}, bf16[144,1024]{1,0:T(8,128)(2,1)S(1)}, u32[]{:S(2)}, u32[]{:S(2)}) collective-permute-start(bf16[144,1024]{1,0:T(8,128)(2,1)S(1)} %get-tuple-element.267), channel_id=1, source_target_pairs={{0,12},{4,0},{8,4},{12,8},{1,13},{5,1},{9,5},{13,9},{2,14},{6,2},{... | collective-permute-start | bytes 884744 | tf_op jit(solution)/shard_map/ppermute | solution.py:29
  364.1 2.6 collective-permute-start.41
  (62 other events, 622.8 us)
Sparse Core Ops, SparseCore 0:
  40.9 112.7 all-gather.1
